TPU v7x, 256 devices: a whole 4x4x8 slice. The times are simulated.
256 devices in a mesh: tok: 32 (over x, y, core), tp: 8 (over z).
Axes of the slice: x: 4, y: 4, z: 8, core: 2. Of those that a mesh axis runs over, the one named last changes fastest.
Arguments:
- hidden: bfloat16 [2048, 7168], P('tok'), may hold values from -6 to 6
- ln_gain: float32 [7168], replicated, may hold values from 0.1 to 1.9
- ln_bias: float32 [7168], replicated, may hold values from -3 to 3
- w_qkv: bfloat16 [7168, 3, 7168], P('tok', None, 'tp'), may hold values from -0.0625 to 0.0625
- qkv_bias: float32 [3, 7168], P(None, 'tp'), may hold values from -3 to 3
- w_out: bfloat16 [7168, 7168], P('tp', 'tok'), may hold values from -0.0625 to 0.0625
- out_bias: float32 [7168], replicated, may hold values from -3 to 3
- dec_cache: bfloat16 [64, 1024, 2, 7168], P('tok', None, None, 'tp'), may hold values from -8 to 8
- prior_kv: bfloat16 [512, 2, 2, 7168], P('tok', None, None, 'tp'), may hold values from -8 to 8
- dec_len: int32 [64], P('tok'), may hold values from 1 to 1024, as said below
- offsets: int32 [2], replicated, may hold values from 4 to 512, as said below
Outputs:
- result: bfloat16 [2048, 7168], P('tok')
- new_kv: bfloat16 [2048, 2, 7168], P('tok', None, 'tp')
Inputs may be any that keep to these rules, and one draw needn't show every extreme that they name: `dec_len`: each decode request has 1 to 1024 cached positions; some request has exactly 1024. `offsets`: each prefill block follows 4 to 512 earlier positions; one of the two follows exactly 512.
All inputs are finite; a program needn't handle non-finite values.
Results may differ from a plain program's by a relative error of at most 0.015.
Values may be sent and summed in bfloat16 or wider, within the bound.
No kernel may reach another device: no remote copies, remote signals or barrier semaphores. Data moves between devices by JAX's collectives and lax.ppermute only.
A program may use at most 128 MiB of HBM per device.

v0:
```python
import functools

import jax
import jax.numpy as jnp
from jax import lax
from jax.experimental import pallas as pl
from jax.experimental.pallas import tpu as pltpu
from jax.sharding import Mesh, PartitionSpec as P


HEAD = 128
WINDOW = 512
SINKS = 4
NEG = -1e30
FAR_AWAY = 1 << 20
SMALL_VMEM = 16 << 20
XS, YS, CS, ZS = 4, 4, 2, 8
GROUP = YS * CS


def shift(axis_size, step):
    return [(i, (i + step) % axis_size) for i in range(axis_size)]


def in_vmem(kernel, out_shape, scalars, arrays, scratch=()):
    vmem = pl.BlockSpec(memory_space=pltpu.VMEM)
    return pl.pallas_call(
        kernel,
        out_shape=out_shape,
        in_specs=[pl.BlockSpec(memory_space=pltpu.SMEM)] * len(scalars) + [vmem] * len(arrays),
        out_specs=jax.tree.map(lambda _: vmem, out_shape),
        scratch_shapes=list(scratch),
        compiler_params=pltpu.CompilerParams(vmem_limit_bytes=SMALL_VMEM),
    )(*scalars, *[pltpu.with_memory_space_constraint(a, pltpu.VMEM) for a in arrays])


def bf16(*shape):
    return jax.ShapeDtypeStruct(shape, jnp.bfloat16)


def product(left, right):
    return jnp.dot(left, right, preferred_element_type=jnp.float32)


def product_t(left, right):
    return lax.dot_general(
        left, right, (((1,), (1,)), ((), ())), preferred_element_type=jnp.float32
    )


def norm_kernel(hid_ref, gain_ref, bias_ref, out_ref):
    inputs = hid_ref[...].astype(jnp.float32)
    average = jnp.mean(inputs, axis=1, keepdims=True)
    centered = inputs - average
    spread = jnp.mean(centered * centered, axis=1, keepdims=True)
    normed = centered / jnp.sqrt(spread + 1e-05) * gain_ref[...] + bias_ref[...]
    piece = out_ref.shape[3]
    for block in range(XS):
        for member in range(GROUP):
            first = (block * GROUP + member) * piece
            out_ref[member, block] = normed[:, first : first + piece].astype(jnp.bfloat16)


def head_lanes(head, heads):
    return pl.ds(pl.multiple_of(jnp.minimum(head, heads - 1) * HEAD, HEAD), HEAD)


def project_kernel(with_extra, where_ref, *refs):
    if with_extra:
        in_ref, own_ref, left_ref, right_ref, far_a_ref, far_b_ref, more_ref = refs[:7]
    else:
        in_ref, own_ref, left_ref, right_ref, far_a_ref, far_b_ref = refs[:6]
    send_ref, keep_ref, extra_ref = refs[-3:]
    me = where_ref[0]
    core = where_ref[1]
    members, _, tok_rows, piece = in_ref.shape
    rows = members * tok_rows
    parts = own_ref.shape[0]
    heads = own_ref.shape[2] // HEAD
    together = 2 // parts
    width = parts * HEAD
    requests = extra_ref.shape[1] // (parts * GROUP)

    def rows_of(step):
        block = lax.rem(me + step, XS)
        return in_ref[:, pl.ds(block, 1)].reshape(rows, piece)

    inputs = [rows_of(step) for step in (0, 3, 1, 2)]
    for side, out_ref in ((1 - core, send_ref), (core, keep_ref)):
        for first in range(0, YS, together):
            slots = list(range(first, first + together))
            columns = [
                (part, head_lanes(CS * slot + side, heads))
                for slot in slots
                for part in range(parts)
            ]

            def wide(ref):
                return jnp.concatenate([ref[part, :, lanes] for part, lanes in columns], axis=1)

            weights = [wide(own_ref), wide(left_ref), wide(right_ref)]
            weights.append(jnp.concatenate([wide(far_a_ref), wide(far_b_ref)], axis=0))
            total = product(inputs[0], weights[0])
            for left, right in zip(inputs[1:], weights[1:]):
                total += product(left, right)
            for index, slot in enumerate(slots):
                mine = total[:, index * width : (index + 1) * width]
                out_ref[slot, :rows] = mine.astype(jnp.bfloat16)
                by_member = mine.reshape(members, tok_rows, width)
                for request in range(requests):
                    row = by_member[:, tok_rows - requests + request]
                    for part in range(parts):
                        place = (request * parts + part) * GROUP + CS * slot + side
                        extra_ref[:, pl.ds(place, 1)] = row[:, None, part * HEAD : (part + 1) * HEAD]
    if with_extra:
        for side, out_ref in ((1 - core, send_ref), (core, keep_ref)):
            for slot in range(YS):
                member = CS * slot + side
                for request in range(requests):
                    query = extra_ref[member, request * GROUP : (request + 1) * GROUP]
                    pair = more_ref[member, request * 2 * GROUP : (request + 1) * 2 * GROUP]
                    block = jnp.concatenate([query, pair], axis=0).astype(jnp.bfloat16)
                    if request == 0:
                        blocks = [block]
                    else:
                        blocks.append(block)
                out_ref[slot, rows:] = jnp.concatenate(blocks, axis=0)


def project(me_x, me_c, requests, pieces, weights, more=None):
    rows = pieces.shape[0] * pieces.shape[2]
    parts = weights[0].shape[0]
    extra = 0 if more is None else 3 * GROUP * requests
    out = bf16(YS, rows + extra, parts * HEAD)
    kept = jax.ShapeDtypeStruct((GROUP, parts * GROUP * requests, HEAD), jnp.float32)
    return in_vmem(
        functools.partial(project_kernel, more is not None),
        (out, out, kept),
        [jnp.stack([me_x, me_c])],
        [pieces, *weights] + ([] if more is None else [more]),
    )


def add_kernel(left_ref, right_ref, out_ref):
    total = left_ref[...].astype(jnp.float32) + right_ref[...].astype(jnp.float32)
    out_ref[...] = total.astype(jnp.bfloat16)


def reduce_partial(send, keep):
    swapped = lax.ppermute(send, "c", [(0, 1), (1, 0)])
    partial = in_vmem(add_kernel, bf16(*keep.shape), [], [keep, swapped])
    return lax.all_to_all(partial, "y", 0, 0, tiled=True)


def summed_rows(partial_ref):
    total = partial_ref[0].astype(jnp.float32)
    for source in range(1, YS):
        total += partial_ref[source].astype(jnp.float32)
    return total


def finish_kv_kernel(member_ref, partial_ref, bias_ref, out_ref):
    lanes = head_lanes(member_ref[0], bias_ref.shape[1] // HEAD)
    bias = jnp.concatenate([bias_ref[1:2, lanes], bias_ref[2:3, lanes]], axis=1)
    out_ref[...] = (summed_rows(partial_ref) + bias).astype(jnp.bfloat16)


def finish_q_kernel(member_ref, partial_ref, bias_ref, out_ref, decode_ref):
    lanes = head_lanes(member_ref[0], bias_ref.shape[1] // HEAD)
    total = summed_rows(partial_ref)
    rows = out_ref.shape[0]
    queries = (total[:rows] + bias_ref[0:1, lanes]) * HEAD ** (-0.5)
    out_ref[...] = queries.astype(jnp.bfloat16)
    decode_ref[...] = total[rows:]


def attend_kernel(pre_dev, where_ref, query_ref, own_ref, last_ref, prior_ref, out_ref):
    odd = where_ref[0]
    start = where_ref[1]
    rows = query_ref.shape[0]
    count = rows // 4
    tok_rows = rows // GROUP
    half = pre_dev * GROUP

    def local(index):
        return (index // tok_rows) * pre_dev + index % tok_rows

    key_row = lax.broadcasted_iota(jnp.int32, (1, rows), 1)
    is_prefill = key_row % tok_rows < pre_dev
    own_pos = jnp.where(is_prefill, start + odd * half + local(key_row), FAR_AWAY)
    last_pos = jnp.where(is_prefill, start + local(key_row), FAR_AWAY)
    last_pos = jnp.where(odd == 1, last_pos, FAR_AWAY)
    old = prior_ref.shape[0] * prior_ref.shape[2]
    old_pos = lax.broadcasted_iota(jnp.int32, (1, old), 1)
    old_pos = jnp.where(old_pos < start, old_pos, FAR_AWAY)
    key_pos = jnp.concatenate([own_pos, last_pos, old_pos], axis=1)
    prior_keys = prior_ref[:, 0].reshape(old, HEAD)
    prior_values = prior_ref[:, 1].reshape(old, HEAD)
    for step in range(rows // count):
        queries = query_ref[step * count : (step + 1) * count]
        row = step * count + lax.broadcasted_iota(jnp.int32, (count, 1), 0)
        query_pos = start + odd * half + local(row)
        scores = jnp.concatenate(
            [
                product_t(queries, own_ref[:, :HEAD]),
                product_t(queries, last_ref[:, :HEAD]),
                product_t(queries, prior_keys),
            ],
            axis=1,
        )
        near = (key_pos < SINKS) | (key_pos > query_pos - WINDOW)
        scores = jnp.where((key_pos <= query_pos) & near, scores, NEG)
        highest = jnp.max(scores, axis=1, keepdims=True)
        expd = jnp.exp(scores - highest)
        totals = jnp.sum(expd, axis=1, keepdims=True)
        weights = expd.astype(jnp.bfloat16)
        weighted = (
            product(weights[:, :rows], own_ref[:, HEAD:])
            + product(weights[:, rows : 2 * rows], last_ref[:, HEAD:])
            + product(weights[:, 2 * rows :], prior_values)
        )
        out_ref[step * count : (step + 1) * count] = (weighted / totals).astype(jnp.bfloat16)


def decode_kernel(len_ref, sums_ref, bias_ref, cache_ref, out_ref):
    request = pl.program_id(0)
    length = len_ref[request]
    slots, _, width = cache_ref.shape[1:]
    heads = width // HEAD

    def rounded(part, factor):
        total = (sums_ref[part * GROUP : (part + 1) * GROUP] + bias_ref[part]) * factor
        return total.astype(jnp.bfloat16).astype(jnp.float32)

    query = rounded(0, HEAD ** (-0.5))
    own_key, own_value = rounded(1, 1.0), rounded(2, 1.0)
    member = lax.broadcasted_iota(jnp.int32, (GROUP, width), 0)
    lane_head = lax.broadcasted_iota(jnp.int32, (GROUP, width), 1) // HEAD
    spread = jnp.concatenate([query] * heads, axis=1)
    spread = jnp.where(member == lane_head, spread, 0.0).astype(jnp.bfloat16)
    pairs = cache_ref[0].reshape(slots * 2, width)
    scores = product_t(spread, pairs)
    lane = lax.broadcasted_iota(jnp.int32, (1, slots * 2), 1)
    slot = lane >> 1
    near = (slot < SINKS) | (slot > length - WINDOW)
    allowed = (slot < length) & near & ((lane & 1) == 0)
    scores = jnp.where(allowed, scores, NEG)
    own_score = jnp.sum(query * own_key, axis=1, keepdims=True)
    highest = jnp.maximum(jnp.max(scores, axis=1, keepdims=True), own_score)
    expd = jnp.exp(scores - highest)
    own_expd = jnp.exp(own_score - highest)
    totals = jnp.sum(expd, axis=1, keepdims=True) + own_expd
    weights = pltpu.roll(expd, 1, 1).astype(jnp.bfloat16)
    every = product(weights, pairs)
    index = lax.broadcasted_iota(jnp.int32, (GROUP, HEAD), 0)
    weighted = own_expd.astype(jnp.bfloat16).astype(jnp.float32) * own_value
    for head in range(heads):
        lanes = every[:, head * HEAD : (head + 1) * HEAD]
        weighted += jnp.where(index == head, lanes, 0.0)
    out_ref[0] = weighted / totals


def decode(lengths, sums, bias, cache):
    requests, slots, _, width = cache.shape
    return pl.pallas_call(
        decode_kernel,
        out_shape=jax.ShapeDtypeStruct((requests, GROUP, HEAD), jnp.float32),
        grid=(requests,),
        in_specs=[
            pl.BlockSpec(memory_space=pltpu.SMEM),
            pl.BlockSpec((3 * GROUP, HEAD), lambda r: (r, 0)),
            pl.BlockSpec(bias.shape, lambda r: (0, 0, 0)),
            pl.BlockSpec((1, slots, 2, width), lambda r: (r, 0, 0, 0)),
        ],
        out_specs=pl.BlockSpec((1, GROUP, HEAD), lambda r: (r, 0, 0)),
        compiler_params=pltpu.CompilerParams(vmem_limit_bytes=2 * SMALL_VMEM),
        name="decode",
    )(lengths, sums, bias, cache)


def pack_kernel(prefill_ref, decode_ref, out_ref):
    rows = prefill_ref.shape[0]
    extra = decode_ref[...].reshape(decode_ref.shape[0] * GROUP, HEAD).astype(jnp.bfloat16)
    for target in range(GROUP):
        out_ref[target, :rows] = prefill_ref[...]
        out_ref[target, rows:] = extra


def out_kernel(where_ref, in_ref, own_ref, left_ref, right_ref, far_ref, out_ref, attn_ref, w_ref):
    me = where_ref[0]
    heads = attn_ref.shape[1] // HEAD
    rows = attn_ref.shape[0]
    tok_rows = rows // GROUP
    extra = in_ref[:, rows:].astype(jnp.float32)
    requests = extra.shape[1] // GROUP
    place = lax.broadcasted_iota(jnp.int32, (1, tok_rows, 1), 1)
    for head in range(heads):
        values = in_ref[head, :rows].reshape(GROUP, tok_rows, HEAD).astype(jnp.float32)
        for request in range(requests):
            first = request * GROUP + head
            row = extra[:, first : first + 1]
            values = jnp.where(place == tok_rows - requests + request, row, values)
        values = values.astype(jnp.bfloat16).reshape(rows, HEAD)
        attn_ref[:, head * HEAD : (head + 1) * HEAD] = values
    for step, ref in ((0, own_ref), (3, left_ref), (1, right_ref), (2, far_ref)):
        w_ref[lax.rem(me + step, XS)] = ref[...]
    weights = w_ref[...].reshape(XS * w_ref.shape[1], w_ref.shape[2])
    out_ref[...] = product_t(attn_ref[...], weights).astype(jnp.bfloat16)


def final_kernel(in_ref, hid_ref, bias_ref, out_ref, row_ref):
    piece = in_ref.shape[2] // XS
    for member in range(GROUP):
        total = in_ref[member * ZS].astype(jnp.float32)
        for source in range(1, ZS):
            total += in_ref[member * ZS + source].astype(jnp.float32)
        for block in range(XS):
            first = (block * GROUP + member) * piece
            row_ref[:, first : first + piece] = total[:, block * piece : (block + 1) * piece]
    result = hid_ref[...].astype(jnp.float32) + row_ref[...] + bias_ref[...]
    result = result.astype(jnp.bfloat16)
    for target in range(ZS):
        out_ref[target] = result


def on_device(
    hidden,
    ln_gain,
    ln_bias,
    w_qkv,
    qkv_bias,
    w_out,
    out_bias,
    dec_cache,
    prior_kv,
    dec_len,
    offsets,
):
    me_x = lax.axis_index("x")
    me_c = lax.axis_index("c")
    me_z = lax.axis_index("z")
    member = lax.axis_index("y") * CS + me_c
    tok_rows, width = hidden.shape
    dec_dev = dec_cache.shape[0]
    pre_dev = tok_rows - dec_dev
    head_width = w_qkv.shape[2]
    heads = head_width // HEAD
    pcb = prior_kv.shape[0]
    rows = GROUP * tok_rows
    start = jnp.where(me_x // 2 == 0, offsets[0], offsets[1])
    half = w_qkv.shape[0] // 2

    turned = w_qkv.transpose(1, 0, 2)
    kv_own, q_own = turned[1:], turned[:1]
    kv_left = lax.ppermute(kv_own, "x", shift(XS, 1))
    kv_right = lax.ppermute(kv_own, "x", shift(XS, -1))
    kv_left, kv_right, q_own = lax.optimization_barrier((kv_left, kv_right, q_own))
    kv_far_a = lax.ppermute(kv_left[:, :half], "x", shift(XS, 1))
    kv_far_b = lax.ppermute(kv_right[:, half:], "x", shift(XS, -1))
    q_left = lax.ppermute(q_own, "x", shift(XS, 1))
    q_right = lax.ppermute(q_own, "x", shift(XS, -1))
    q_far_a = lax.ppermute(q_left[:, :half], "x", shift(XS, 1))
    q_far_b = lax.ppermute(q_right[:, half:], "x", shift(XS, -1))

    pieces = in_vmem(
        norm_kernel,
        bf16(GROUP, XS, tok_rows, width // (XS * GROUP)),
        [],
        [hidden, ln_gain[None], ln_bias[None]],
    )
    pieces = lax.all_to_all(pieces, ("y", "c"), 0, 0, tiled=True)

    prior = prior_kv.reshape(pcb, 2, 2, heads, HEAD)
    prior = jnp.pad(prior, ((0, 0), (0, 0), (0, 0), (0, GROUP - heads), (0, 0)))
    prior = prior.transpose(1, 3, 2, 0, 4)
    prior = jnp.repeat(prior, 2, axis=0).reshape(XS * GROUP, 2, pcb, HEAD)
    pieces, prior = lax.optimization_barrier((pieces, prior))
    prior = lax.all_to_all(prior, ("x", "y", "c"), 0, 0, tiled=True)

    where = member[None]
    kv_send, kv_keep, kv_extra = project(
        me_x, me_c, dec_dev, pieces, (kv_own, kv_left, kv_right, kv_far_a, kv_far_b)
    )
    kv_keep, prior = lax.optimization_barrier((kv_keep, prior))
    kv_parts = reduce_partial(kv_send, kv_keep)
    own_kv = in_vmem(finish_kv_kernel, bf16(rows, 2 * HEAD), [where], [kv_parts, qkv_bias])
    last_kv = lax.ppermute(own_kv, "x", [(0, 1), (2, 3)])

    q_far_a, q_far_b, w_out = lax.optimization_barrier((q_far_a, q_far_b, w_out))
    q_send, q_keep, _ = project(
        me_x, me_c, dec_dev, pieces, (q_own, q_left, q_right, q_far_a, q_far_b), kv_extra
    )
    q_parts = reduce_partial(q_send, q_keep)
    w_own = w_out.T
    w_left = lax.ppermute(w_own, "x", shift(XS, 1))
    w_right = lax.ppermute(w_own, "x", shift(XS, -1))
    w_far = lax.ppermute(w_own, "x", shift(XS, 2))

    queries, sums = in_vmem(
        finish_q_kernel,
        (
            bf16(rows, HEAD),
            jax.ShapeDtypeStruct((3 * GROUP * dec_dev, HEAD), jnp.float32),
        ),
        [where],
        [q_parts, qkv_bias],
    )
    tied_kv, queries = lax.optimization_barrier((own_kv, queries))
    mine = lax.all_to_all(tied_kv.reshape(GROUP, tok_rows, 2 * HEAD), ("y", "c"), 0, 0, tiled=True)
    new_kv = mine[:heads].reshape(heads, tok_rows, 2, HEAD)
    new_kv = new_kv.transpose(1, 2, 0, 3).reshape(tok_rows, 2, head_width)
    prefilled = in_vmem(
        functools.partial(attend_kernel, pre_dev),
        bf16(rows, HEAD),
        [jnp.stack([me_x % 2, start])],
        [queries, own_kv, last_kv, prior],
    )
    head_bias = jnp.pad(qkv_bias.reshape(3, heads, HEAD), ((0, 0), (0, GROUP - heads), (0, 0)))
    decoded = decode(dec_len, sums, head_bias, dec_cache)
    payload = in_vmem(
        pack_kernel, bf16(GROUP, rows + dec_dev * GROUP, HEAD), [], [prefilled, decoded]
    )
    payload, new_kv, w_left, w_right, w_far = lax.optimization_barrier(
        (payload, new_kv, w_left, w_right, w_far)
    )
    gathered = lax.all_to_all(payload, ("y", "c"), 0, 0, tiled=True)
    piece = w_own.shape[0]
    shares = in_vmem(
        out_kernel,
        bf16(rows, XS * piece),
        [me_x[None]],
        [gathered, w_own, w_left, w_right, w_far],
        [
            pltpu.VMEM((rows, head_width), jnp.bfloat16),
            pltpu.VMEM((XS, piece, head_width), jnp.bfloat16),
        ],
    )
    slab = tok_rows // ZS
    shares = shares.reshape(GROUP * ZS, slab, XS * piece)
    shares = lax.all_to_all(shares, ("y", "c", "z"), 0, 0, tiled=True)
    residual = lax.dynamic_slice(hidden, (me_z * slab, 0), (slab, width))
    result = in_vmem(
        final_kernel,
        bf16(ZS, slab, width),
        [],
        [shares, residual, out_bias[None]],
        [pltpu.VMEM((slab, width), jnp.float32)],
    )
    result = lax.all_to_all(result, "z", 0, 0, tiled=True).reshape(tok_rows, width)
    return (result, new_kv)


def solution(mesh):
    fine = Mesh(mesh.devices.reshape(XS, YS, CS, ZS), ("x", "y", "c", "z"))
    tok = ("x", "y", "c")
    in_specs = (
        P(tok, None),
        P(),
        P(),
        P(tok, None, "z"),
        P(None, "z"),
        P("z", tok),
        P(),
        P(tok, None, None, "z"),
        P(tok, None, None, "z"),
        P(tok),
        P(),
    )
    out_specs = (P(tok, None), P(tok, None, "z"))

    return jax.shard_map(
        on_device, mesh=fine, in_specs=in_specs, out_specs=out_specs, check_vma=False
    )
```

profile of v0, /device:TPU:2, one launch (start us, length us, event | category | flops | bytes accessed | tf_op | source)
XLA Modules:
  0.0 203.8 jit_solution(7733123080792810064)
XLA Ops:
  0.6 0.0 copy-start.1
  0.7 1.3 slice.36.refs_1_
  2.0 1.6 collective-permute-start
  3.5 0.8 collective-permute-start.1
  4.4 1.9 shard_map.122
  6.3 4.2 %all-to-all-start = ((bf16[8,4,64,224]{3,2,1,0:T(8,128)(2,1)}), bf16[8,4,64,224]{3,2,1,0:T(8,128)(2,1)S(1)}, u32[]{:S(2)}, u32[]{:S(2)}) async-start(bf16[8,4,64,224]{3,2,1,0:T(8,128)(2,1)} %shard_map.122), calls=%async_computation | async-start | bytes 2097152 | tf_op jit(solution)/shard_map/all_to_all | solution.py:371
  10.5 1.8 slice.37.refs_1_
  12.2 9.4 %collective-permute-done.refs_2_ = bf16[2,224,896]{2,1,0:T(8,128)(2,1)S(1)} collective-permute-done((bf16[2,224,896]{2,1,0:T(8,128)(2,1)S(1)}, bf16[2,224,896]{2,1,0:T(8,128)(2,1)S(1)}, u32[]{:S(2)}, u32[]{:S(2)}) %collective-permute-start) | collective-permute-done | bytes 802848 | tf_op jit(solution)/shard_map/ppermute | solution.py:355
  21.7 1.2 collective-permute-done.1.refs_3_
  22.9 0.8 slice.31
  23.7 1.2 collective-permute-start.2
  24.9 0.8 slice.32
  25.6 0.8 collective-permute-start.3
  26.5 1.6 reshape.32
  28.1 0.9 pad_bitcast_fusion
  29.0 0.7 copy.19
  29.7 0.1 pad_add_fusion.1.where_ref
  29.8 0.9 broadcast_in_dim.22
  30.7 3.1 %collective-permute-done.2.refs_4_ = bf16[2,112,896]{2,1,0:T(8,128)(2,1)} collective-permute-done((bf16[2,112,896]{2,1,0:T(8,128)(2,1)}, bf16[2,112,896]{2,1,0:T(8,128)(2,1)}, u32[]{:S(2)}, u32[]{:S(2)}) %collective-permute-start.2) | collective-permute-done | bytes 401440 | tf_op jit(solution)/shard_map/ppermute | solution.py:358
  33.9 1.5 collective-permute-done.3.refs_5_
  35.4 3.5 %shard_map.123 = (bf16[4,512,256]{2,1,0:T(8,128)(2,1)S(1)}, bf16[4,512,256]{2,1,0:T(8,128)(2,1)S(1)}, f32[8,32,128]{2,1,0:T(8,128)S(1)}) custom-call(s32[2]{0:T(128)S(1)} %pad_add_fusion.1.where_ref, bf16[8,4,64,224]{3,2,1,0:T(8,128)(2,1)S(1)} %all-to-all-done.refs_0_, bf16[2,224,896]{2,1,0:T(8,128)(2,1)S(1)} %slice.36.refs_1_, ...), custom_call_target="tpu_custom_call" | custom-call | tf_op jit(solution)/shard_map/pallas_call | solution.py:27
  39.0 0.6 copy-done.3
  39.6 0.7 collective-permute-start.5
  40.3 1.3 collective-permute-start.6
  41.6 17.5 %all_to_all.40.prior_ref = bf16[32,2,16,128]{3,2,1,0:T(8,128)(2,1)S(1)} all-to-all(bf16[32,2,16,128]{3,2,1,0:T(8,128)(2,1)S(1)} %bitcast.31), channel_id=1, replica_groups=mesh['x'=4,'y'=4,'c'=2,'z'=8] {'x','y','c'}, dimensions={0} | all-to-all | bytes 524288 | tf_op jit(solution)/shard_map/all_to_all | solution.py:378
  59.1 1.2 shard_map.124
  60.4 3.6 %all-to-all-start.2 = ((bf16[4,512,256]{2,1,0:T(8,128)(2,1)}), bf16[4,512,256]{2,1,0:T(8,128)(2,1)S(1)}, u32[]{:S(2)}, u32[]{:S(2)}) async-start(bf16[4,512,256]{2,1,0:T(8,128)(2,1)} %shard_map.124), calls=%async_computation.2 | async-start | bytes 2097152 | tf_op jit(solution)/shard_map/all_to_all | solution.py:152
  64.0 0.8 collective-permute-start.7
  64.9 1.4 collective-permute-start.8
  66.3 4.9 %collective-permute-done.7.refs_4_ = bf16[1,112,896]{2,1,0:T(8,128)(2,1)S(1)} collective-permute-done((bf16[1,112,896]{2,1,0:T(8,128)(2,1)S(1)}, bf16[1,112,896]{2,1,0:T(8,128)(2,1)S(1)}, u32[]{:S(2)}, u32[]{:S(2)}) %collective-permute-start.7) | collective-permute-done | bytes 200736 | tf_op jit(solution)/shard_map/ppermute | solution.py:362
  71.2 0.6 collective-permute-done.8.refs_5_
  71.8 2.9 %shard_map.126 = (bf16[4,560,128]{2,1,0:T(8,128)(2,1)S(1)}, bf16[4,560,128]{2,1,0:T(8,128)(2,1)S(1)}, f32[8,16,128]{2,1,0:T(8,128)}) custom-call(s32[2]{0:T(128)S(1)} %pad_add_fusion.1.where_ref, bf16[8,4,64,224]{3,2,1,0:T(8,128)(2,1)S(1)} %all-to-all-done.refs_0_, bf16[1,224,896]{2,1,0:T(8,128)(2,1)} %slice.37.refs_1_, ...), custom_call_target="tpu_custom_call" | custom-call | tf_op jit(solution)/shard_map/pallas_call | solution.py:27
  74.7 2.0 collective-permute-done.9.right_ref
  76.7 0.9 shard_map.127
  77.6 2.1 %all-to-all-done.2.partial_ref = bf16[4,512,256]{2,1,0:T(8,128)(2,1)S(1)} async-done(((bf16[4,512,256]{2,1,0:T(8,128)(2,1)}), bf16[4,512,256]{2,1,0:T(8,128)(2,1)S(1)}, u32[]{:S(2)}, u32[]{:S(2)}) %all-to-all-start.2) | async-done | bytes 1048608 | tf_op jit(solution)/shard_map/all_to_all | solution.py:152
  79.7 3.5 %all-to-all-start.3 = ((bf16[4,560,128]{2,1,0:T(8,128)(2,1)}), bf16[4,560,128]{2,1,0:T(8,128)(2,1)S(1)}, u32[]{:S(2)}, u32[]{:S(2)}) async-start(bf16[4,560,128]{2,1,0:T(8,128)(2,1)} %shard_map.127), calls=%async_computation.3 | async-start | bytes 1146880 | tf_op jit(solution)/shard_map/all_to_all | solution.py:152
  83.2 0.8 collective-permute-start.11
  84.0 1.3 collective-permute-start.12
  85.3 2.3 %collective-permute-start.13 = (bf16[224,896]{1,0:T(8,128)(2,1)S(1)}, bf16[224,896]{1,0:T(8,128)(2,1)}, u32[]{:S(2)}, u32[]{:S(2)}) collective-permute-start(bf16[224,896]{1,0:T(8,128)(2,1)S(1)} %bitcast.23), channel_id=1, source_target_pairs={{0,128},{64,192},{128,0},{192,64},{1,129},{65,193},{129,1},{193,65... | collective-permute-start | bytes 1204232 | tf_op jit(solution)/shard_map/ppermute | solution.py:397
  87.6 0.9 shard_map.125.own_ref
  88.5 1.3 collective-permute-start.10
  89.8 3.1 %all-to-all-done.3.partial_ref = bf16[4,560,128]{2,1,0:T(8,128)(2,1)S(1)} async-done(((bf16[4,560,128]{2,1,0:T(8,128)(2,1)}), bf16[4,560,128]{2,1,0:T(8,128)(2,1)S(1)}, u32[]{:S(2)}, u32[]{:S(2)}) %all-to-all-start.3) | async-done | bytes 573472 | tf_op jit(solution)/shard_map/all_to_all | solution.py:152
  92.9 0.1 shard_map.128
  93.0 3.4 %all-to-all-start.4 = ((bf16[8,64,256]{2,1,0:T(8,128)(2,1)}), bf16[8,64,256]{2,1,0:T(8,128)(2,1)S(1)}, u32[]{:S(2)}, u32[]{:S(2)}) async-start(bf16[8,64,256]{2,1,0:T(8,128)(2,1)} %bitcast.12), calls=%async_computation.4 | async-start | bytes 524288 | tf_op jit(solution)/shard_map/all_to_all | solution.py:409
  96.5 0.6 fusion
  98.4 0.1 pad_add_fusion.where_ref
  98.5 3.1 %copy-done = bf16[2,1024,2,896]{3,2,1,0:T(2,128)(2,1)S(1)} copy-done((bf16[2,1024,2,896]{3,2,1,0:T(2,128)(2,1)S(1)}, bf16[2,1024,2,896]{3,2,1,0:T(2,128)(2,1)}, u32[]{:S(2)}) %copy-start) | copy-done | bytes 7340056
  101.5 4.4 %decode.1.decode_ref = f32[2,8,128]{2,1,0:T(8,128)S(1)} custom-call(s32[2]{0:T(128)S(1)} %copy-done.9, f32[48,128]{1,0:T(8,128)S(1)} %get-tuple-element.42.sums_ref, f32[3,8,128]{2,1,0:T(8,128)S(1)} %pad.9.bias_ref, bf16[2,1024,2,896]{3,2,1,0:T(2,128)(2,1)S(1)} %copy-done), custom_call_target="tpu_custom_call" | custom-call | tf_op jit(solution)/shard_map/decode/pallas_call | solution.py:265
  106.0 0.1 reshape.28
  106.1 0.2 copy.20
  106.2 0.3 reshape.29
  106.5 1.5 collective-permute-done.10.last_ref
  108.0 3.2 %shard_map.129.prefill_ref = bf16[512,128]{1,0:T(8,128)(2,1)S(1)} custom-call(s32[2]{0:T(128)S(1)} %pad_add_fusion.where_ref, bf16[512,128]{1,0:T(8,128)(2,1)S(1)} %get-tuple-element.40.query_ref, bf16[512,256]{1,0:T(8,128)(2,1)} %shard_map.125.own_ref, bf16[512,256]{1,0:T(8,128)(2,1)S(1)} %collective-permute-done.10.last_ref, ...), custom_call_target="tpu_custom_call" | custom-call | tf_op jit(solution)/shard_map/pallas_call | solution.py:27
  111.2 0.1 shard_map.130
  111.4 20.5 %all_to_all.41.in_ref = bf16[8,528,128]{2,1,0:T(8,128)(2,1)S(1)} all-to-all(bf16[8,528,128]{2,1,0:T(8,128)(2,1)S(1)} %shard_map.130), channel_id=1, replica_groups=mesh['x'=4,'y'=4,'c'=2,'z'=8] {'y','c'}, dimensions={0} | all-to-all | bytes 2162688 | tf_op jit(solution)/shard_map/all_to_all | solution.py:426
  131.9 3.4 %shard_map.131 = bf16[512,896]{1,0:T(8,128)(2,1)} custom-call(s32[1]{0:T(128)} %bitcast.where_ref, bf16[8,528,128]{2,1,0:T(8,128)(2,1)S(1)} %all_to_all.41.in_ref, bf16[224,896]{1,0:T(8,128)(2,1)S(1)} %bitcast.24, bf16[224,896]{1,0:T(8,128)(2,1)S(1)} %collective-permute-done.11.left_ref, bf16[224,896]{1,0:T(8,128)(2,1)S(1)} %collective-permute-done.12.right_ref, ...), custom_call_target="tpu_custom_call" | custom-call | tf_op jit(solution)/shard_map/pallas_call | solution.py:27
  135.3 10.2 %all-to-all-start.6 = ((bf16[64,8,896]{2,1,0:T(8,128)(2,1)}), bf16[64,8,896]{2,1,0:T(8,128)(2,1)S(1)}, u32[]{:S(2)}, u32[]{:S(2)}) async-start(bf16[64,8,896]{2,1,0:T(8,128)(2,1)} %bitcast.15), calls=%async_computation.6 | async-start | bytes 1835008 | tf_op jit(solution)/shard_map/all_to_all | solution.py:440
  145.5 0.9 constant_dynamic-slice_fusion.hid_ref
  146.4 24.9 %all-to-all-done.6.in_ref = bf16[64,8,896]{2,1,0:T(8,128)(2,1)S(1)} async-done(((bf16[64,8,896]{2,1,0:T(8,128)(2,1)}), bf16[64,8,896]{2,1,0:T(8,128)(2,1)S(1)}, u32[]{:S(2)}, u32[]{:S(2)}) %all-to-all-start.6) | async-done | bytes 917536 | tf_op jit(solution)/shard_map/all_to_all | solution.py:440
  171.3 1.2 shard_map.132
  172.5 4.2 %all-to-all-start.7 = ((bf16[8,8,7168]{2,1,0:T(8,128)(2,1)}), bf16[8,8,7168]{2,1,0:T(8,128)(2,1)S(1)}, u32[]{:S(2)}, u32[]{:S(2)}) async-start(bf16[8,8,7168]{2,1,0:T(8,128)(2,1)} %shard_map.132), calls=%async_computation.7 | async-start | bytes 1835008 | tf_op jit(solution)/shard_map/all_to_all | solution.py:449
  176.7 0.9 copy.21
  177.6 25.2 %all-to-all-done.7 = bf16[8,8,7168]{2,1,0:T(8,128)(2,1)S(1)} async-done(((bf16[8,8,7168]{2,1,0:T(8,128)(2,1)}), bf16[8,8,7168]{2,1,0:T(8,128)(2,1)S(1)}, u32[]{:S(2)}, u32[]{:S(2)}) %all-to-all-start.7) | async-done | bytes 917536 | tf_op jit(solution)/shard_map/all_to_all | solution.py:449
  202.9 0.9 copy.26
  (34 shorter events, 0.1 us)
Async XLA Ops:
  0.6 3.7 %copy-start.6 = (f32[7168]{0:T(1024)S(1)}, f32[7168]{0:T(1024)}, u32[]{:S(2)}) copy-start(f32[7168]{0:T(1024)} %param.12) | copy-start | bytes 86020
  0.6 3.7 %copy-start.7 = (f32[7168]{0:T(1024)S(1)}, f32[7168]{0:T(1024)}, u32[]{:S(2)}) copy-start(f32[7168]{0:T(1024)} %param.13) | copy-start | bytes 86020
  0.6 3.7 %copy-start.1 = (bf16[64,7168]{1,0:T(8,128)(2,1)S(1)}, bf16[64,7168]{1,0:T(8,128)(2,1)}, u32[]{:S(2)}) copy-start(bf16[64,7168]{1,0:T(8,128)(2,1)} %hid_ref.1) | copy-start | bytes 2752516
  2.0 19.7 %collective-permute-start = (bf16[2,224,896]{2,1,0:T(8,128)(2,1)S(1)}, bf16[2,224,896]{2,1,0:T(8,128)(2,1)S(1)}, u32[]{:S(2)}, u32[]{:S(2)}) collective-permute-start(bf16[2,224,896]{2,1,0:T(8,128)(2,1)S(1)} %slice.36.refs_1_), channel_id=1, source_target_pairs={{0,64},{64,128},{128,192},{192,0},{1,65},{65,129},{129,193},{193,1... | collective-permute-start | bytes 2408456 | tf_op jit(solution)/shard_map/ppermute | solution.py:355
  3.5 19.4 %collective-permute-start.1 = (bf16[2,224,896]{2,1,0:T(8,128)(2,1)S(1)}, bf16[2,224,896]{2,1,0:T(8,128)(2,1)S(1)}, u32[]{:S(2)}, u32[]{:S(2)}) collective-permute-start(bf16[2,224,896]{2,1,0:T(8,128)(2,1)S(1)} %slice.36.refs_1_), channel_id=1, source_target_pairs={{0,192},{64,0},{128,64},{192,128},{1,193},{65,1},{129,65},{193,129... | collective-permute-start | bytes 2408456 | tf_op jit(solution)/shard_map/ppermute | solution.py:356
  6.3 23.5 %all-to-all-start = ((bf16[8,4,64,224]{3,2,1,0:T(8,128)(2,1)}), bf16[8,4,64,224]{3,2,1,0:T(8,128)(2,1)S(1)}, u32[]{:S(2)}, u32[]{:S(2)}) async-start(bf16[8,4,64,224]{3,2,1,0:T(8,128)(2,1)} %shard_map.122), calls=%async_computation | async-start | bytes 2097152 | tf_op jit(solution)/shard_map/all_to_all | solution.py:371
  23.7 10.2 %collective-permute-start.2 = (bf16[2,112,896]{2,1,0:T(8,128)(2,1)}, bf16[2,112,896]{2,1,0:T(8,128)(2,1)}, u32[]{:S(2)}, u32[]{:S(2)}) collective-permute-start(bf16[2,112,896]{2,1,0:T(8,128)(2,1)} %slice.31), channel_id=1, source_target_pairs={{0,64},{64,128},{128,192},{192,0},{1,65},{65,129},{129,193},{193,1... | collective-permute-start | bytes 1204232 | tf_op jit(solution)/shard_map/ppermute | solution.py:358
  25.6 9.8 %collective-permute-start.3 = (bf16[2,112,896]{2,1,0:T(8,128)(2,1)}, bf16[2,112,896]{2,1,0:T(8,128)(2,1)}, u32[]{:S(2)}, u32[]{:S(2)}) collective-permute-start(bf16[2,112,896]{2,1,0:T(8,128)(2,1)} %slice.32), channel_id=1, source_target_pairs={{0,192},{64,0},{128,64},{192,128},{1,193},{65,1},{129,65},{193,129... | collective-permute-start | bytes 1204232 | tf_op jit(solution)/shard_map/ppermute | solution.py:359
  39.0 0.7 copy-start.3
  39.6 19.5 %collective-permute-start.4 = (bf16[4,512,256]{2,1,0:T(8,128)(2,1)S(1)}, bf16[4,512,256]{2,1,0:T(8,128)(2,1)S(1)}, u32[]{:S(2)}, u32[]{:S(2)}) collective-permute-start(bf16[4,512,256]{2,1,0:T(8,128)(2,1)S(1)} %get-tuple-element.32), channel_id=1, source_target_pairs={{0,8},{8,0},{1,9},{9,1},{2,10},{10,2},{3,11},{11,3},{4,12},{12,4},... | collective-permute-start | bytes 3145736 | tf_op jit(solution)/shard_map/ppermute | solution.py:150
  39.6 24.4 %collective-permute-start.5 = (bf16[1,224,896]{2,1,0:T(8,128)(2,1)}, bf16[1,224,896]{2,1,0:T(8,128)(2,1)S(1)}, u32[]{:S(2)}, u32[]{:S(2)}) collective-permute-start(bf16[1,224,896]{2,1,0:T(8,128)(2,1)} %slice.37.refs_1_), channel_id=1, source_target_pairs={{0,64},{64,128},{128,192},{192,0},{1,65},{65,129},{129,193},{193,1... | collective-permute-start | bytes 1204232 | tf_op jit(solution)/shard_map/ppermute | solution.py:360
  40.3 24.5 %collective-permute-start.6 = (bf16[1,224,896]{2,1,0:T(8,128)(2,1)}, bf16[1,224,896]{2,1,0:T(8,128)(2,1)S(1)}, u32[]{:S(2)}, u32[]{:S(2)}) collective-permute-start(bf16[1,224,896]{2,1,0:T(8,128)(2,1)} %slice.37.refs_1_), channel_id=1, source_target_pairs={{0,192},{64,0},{128,64},{192,128},{1,193},{65,1},{129,65},{193,129... | collective-permute-start | bytes 1204232 | tf_op jit(solution)/shard_map/ppermute | solution.py:361
  60.4 11.4 %copy-start.4 = (f32[8,32,128]{2,1,0:T(8,128)S(1)}, f32[8,32,128]{2,1,0:T(8,128)}, u32[]{:S(2)}) copy-start(f32[8,32,128]{2,1,0:T(8,128)} %copy-done.3) | copy-start | bytes 393220
  60.4 19.3 %all-to-all-start.2 = ((bf16[4,512,256]{2,1,0:T(8,128)(2,1)}), bf16[4,512,256]{2,1,0:T(8,128)(2,1)S(1)}, u32[]{:S(2)}, u32[]{:S(2)}) async-start(bf16[4,512,256]{2,1,0:T(8,128)(2,1)} %shard_map.124), calls=%async_computation.2 | async-start | bytes 2097152 | tf_op jit(solution)/shard_map/all_to_all | solution.py:152
  64.0 7.1 %collective-permute-start.7 = (bf16[1,112,896]{2,1,0:T(8,128)(2,1)S(1)}, bf16[1,112,896]{2,1,0:T(8,128)(2,1)S(1)}, u32[]{:S(2)}, u32[]{:S(2)}) collective-permute-start(bf16[1,112,896]{2,1,0:T(8,128)(2,1)S(1)} %slice.38), channel_id=1, source_target_pairs={{0,64},{64,128},{128,192},{192,0},{1,65},{65,129},{129,193},{193,1... | collective-permute-start | bytes 602120 | tf_op jit(solution)/shard_map/ppermute | solution.py:362
  64.9 6.9 %collective-permute-start.8 = (bf16[1,112,896]{2,1,0:T(8,128)(2,1)S(1)}, bf16[1,112,896]{2,1,0:T(8,128)(2,1)S(1)}, u32[]{:S(2)}, u32[]{:S(2)}) collective-permute-start(bf16[1,112,896]{2,1,0:T(8,128)(2,1)S(1)} %slice.39), channel_id=1, source_target_pairs={{0,192},{64,0},{128,64},{192,128},{1,193},{65,1},{129,65},{193,129... | collective-permute-start | bytes 602120 | tf_op jit(solution)/shard_map/ppermute | solution.py:363
  74.7 2.0 collective-permute-start.9
  76.7 6.5 %copy-start.2 = (bf16[896,224]{0,1:T(8,128)(2,1)S(1)}, bf16[896,224]{0,1:T(8,128)(2,1)}, u32[]{:S(2)}) copy-start(bf16[896,224]{0,1:T(8,128)(2,1)} %param.16) | copy-start | bytes 1204228
  76.7 11.0 %copy-start.5 = (f32[3,896]{1,0:T(4,128)S(1)}, f32[3,896]{1,0:T(4,128)}, u32[]{:S(2)}) copy-start(f32[3,896]{1,0:T(4,128)} %bias_ref.3) | copy-start | bytes 32260
  79.7 13.2 %all-to-all-start.3 = ((bf16[4,560,128]{2,1,0:T(8,128)(2,1)}), bf16[4,560,128]{2,1,0:T(8,128)(2,1)S(1)}, u32[]{:S(2)}, u32[]{:S(2)}) async-start(bf16[4,560,128]{2,1,0:T(8,128)(2,1)} %shard_map.127), calls=%async_computation.3 | async-start | bytes 1146880 | tf_op jit(solution)/shard_map/all_to_all | solution.py:152
  83.2 28.2 %collective-permute-start.11 = (bf16[224,896]{1,0:T(8,128)(2,1)S(1)}, bf16[224,896]{1,0:T(8,128)(2,1)S(1)}, u32[]{:S(2)}, u32[]{:S(2)}) collective-permute-start(bf16[224,896]{1,0:T(8,128)(2,1)S(1)} %bitcast.21), channel_id=1, source_target_pairs={{0,64},{64,128},{128,192},{192,0},{1,65},{65,129},{129,193},{193,1... | collective-permute-start | bytes 1204232 | tf_op jit(solution)/shard_map/ppermute | solution.py:395
  84.0 27.3 %collective-permute-start.12 = (bf16[224,896]{1,0:T(8,128)(2,1)S(1)}, bf16[224,896]{1,0:T(8,128)(2,1)S(1)}, u32[]{:S(2)}, u32[]{:S(2)}) collective-permute-start(bf16[224,896]{1,0:T(8,128)(2,1)S(1)} %bitcast.22), channel_id=1, source_target_pairs={{0,192},{64,0},{128,64},{192,128},{1,193},{65,1},{129,65},{193,129... | collective-permute-start | bytes 1204232 | tf_op jit(solution)/shard_map/ppermute | solution.py:396
  85.3 26.1 %collective-permute-start.13 = (bf16[224,896]{1,0:T(8,128)(2,1)S(1)}, bf16[224,896]{1,0:T(8,128)(2,1)}, u32[]{:S(2)}, u32[]{:S(2)}) collective-permute-start(bf16[224,896]{1,0:T(8,128)(2,1)S(1)} %bitcast.23), channel_id=1, source_target_pairs={{0,128},{64,192},{128,0},{192,64},{1,129},{65,193},{129,1},{193,65... | collective-permute-start | bytes 1204232 | tf_op jit(solution)/shard_map/ppermute | solution.py:397
  87.6 8.9 %copy-start.10 = (s32[2]{0:T(128)S(1)}, s32[2]{0:T(128)}, u32[]{:S(2)}) copy-start(s32[2]{0:T(128)} %param.21) | copy-start | bytes 28
  87.6 10.8 %copy-start.9 = (s32[2]{0:T(128)S(1)}, s32[2]{0:T(128)}, u32[]{:S(2)}) copy-start(s32[2]{0:T(128)} %len_ref.1) | copy-start | bytes 28
  88.5 19.5 %collective-permute-start.10 = (bf16[512,256]{1,0:T(8,128)(2,1)}, bf16[512,256]{1,0:T(8,128)(2,1)S(1)}, u32[]{:S(2)}, u32[]{:S(2)}) collective-permute-start(bf16[512,256]{1,0:T(8,128)(2,1)} %shard_map.125.own_ref), channel_id=1, source_target_pairs={{0,64},{128,192},{1,65},{129,193},{2,66},{130,194},{3,67},{131,195... | collective-permute-start | bytes 786440 | tf_op jit(solution)/shard_map/ppermute | solution.py:387
  93.0 13.0 %all-to-all-start.4 = ((bf16[8,64,256]{2,1,0:T(8,128)(2,1)}), bf16[8,64,256]{2,1,0:T(8,128)(2,1)S(1)}, u32[]{:S(2)}, u32[]{:S(2)}) async-start(bf16[8,64,256]{2,1,0:T(8,128)(2,1)} %bitcast.12), calls=%async_computation.4 | async-start | bytes 524288 | tf_op jit(solution)/shard_map/all_to_all | solution.py:409
  98.5 3.1 %copy-start = (bf16[2,1024,2,896]{3,2,1,0:T(2,128)(2,1)S(1)}, bf16[2,1024,2,896]{3,2,1,0:T(2,128)(2,1)}, u32[]{:S(2)}) copy-start(bf16[2,1024,2,896]{3,2,1,0:T(2,128)(2,1)} %cache_ref.1) | copy-start | bytes 22020100
  135.3 36.1 %copy-start.8 = (f32[7168]{0:T(1024)S(1)}, f32[7168]{0:T(1024)}, u32[]{:S(2)}) copy-start(f32[7168]{0:T(1024)} %param.17) | copy-start | bytes 86020
  135.3 36.1 %all-to-all-start.6 = ((bf16[64,8,896]{2,1,0:T(8,128)(2,1)}), bf16[64,8,896]{2,1,0:T(8,128)(2,1)S(1)}, u32[]{:S(2)}, u32[]{:S(2)}) async-start(bf16[64,8,896]{2,1,0:T(8,128)(2,1)} %bitcast.15), calls=%async_computation.6 | async-start | bytes 1835008 | tf_op jit(solution)/shard_map/all_to_all | solution.py:440
  172.5 30.4 %all-to-all-start.7 = ((bf16[8,8,7168]{2,1,0:T(8,128)(2,1)}), bf16[8,8,7168]{2,1,0:T(8,128)(2,1)S(1)}, u32[]{:S(2)}, u32[]{:S(2)}) async-start(bf16[8,8,7168]{2,1,0:T(8,128)(2,1)} %shard_map.132), calls=%async_computation.7 | async-start | bytes 1835008 | tf_op jit(solution)/shard_map/all_to_all | solution.py:449
where the time goes:
time: 206 us; the launch traced here: 204 us
  waiting for transfers between devices  79.6 us (39%)
  starting transfers between devices  43.5 us (21%)
  blocking collectives  38 us (18%)
  Pallas kernels  23.8 us (12%)
  local copies, waits for them, and re-layouts  16.5 us (8%)
  between operations  2.21 us (1%)
    all_to_all x1, waiting for transfers between devices, on_device(): lax.all_to_all(result, 'z', 0, 0, tiled=True).reshape(tok_rows, width)  25.2 us
    all_to_all x1, waiting for transfers between devices, on_device(): shares = lax.all_to_all(shares, ('y', 'c', 'z'), 0, 0, tiled=True)  24.9 us
    all_to_all x1, blocking collectives, on_device(): gathered = lax.all_to_all(payload, ('y', 'c'), 0, 0, tiled=True)  20.5 us
    pallas_call x11, Pallas kernels, in_vmem(): pl.pallas_call(kernel, out_shape=out_shape, in_specs=[pl.BlockSpec(memory...  19.4 us
    all_to_all x1, blocking collectives, on_device(): prior = lax.all_to_all(prior, ('x', 'y', 'c'), 0, 0, tiled=True)  17.5 us
    all_to_all x1, starting transfers between devices, on_device(): shares = lax.all_to_all(shares, ('y', 'c', 'z'), 0, 0, tiled=True)  10.2 us
    ppermute x1, waiting for transfers between devices, on_device(): kv_left = lax.ppermute(kv_own, 'x', shift(XS, 1))  9.43 us
    all_to_all x2, starting transfers between devices, reduce_partial(): return lax.all_to_all(partial, 'y', 0, 0, tiled=True)  7.12 us
  transfers between devices with their start and end apart: 20, of which 12 were waited for; matrix products, arithmetic and copies ran while one was open for 5% of the time, Pallas kernels for 8%

commit v1 on v0

--- a/solution.py
+++ b/solution.py
@@ -48,32 +48,51 @@
     )
 
 
-def norm_kernel(hid_ref, gain_ref, bias_ref, out_ref):
+def norm_kernel(hid_ref, gain_ref, bias_ref, prior_ref, out_ref):
     inputs = hid_ref[...].astype(jnp.float32)
+    rows = inputs.shape[0]
     average = jnp.mean(inputs, axis=1, keepdims=True)
     centered = inputs - average
     spread = jnp.mean(centered * centered, axis=1, keepdims=True)
     normed = centered / jnp.sqrt(spread + 1e-05) * gain_ref[...] + bias_ref[...]
     piece = out_ref.shape[3]
+    heads = prior_ref.shape[3] // HEAD
     for block in range(XS):
+        earlier = prior_ref[:, block // 2, block % 2]
         for member in range(GROUP):
             first = (block * GROUP + member) * piece
-            out_ref[member, block] = normed[:, first : first + piece].astype(jnp.bfloat16)
+            out_ref[member, block, :rows] = normed[:, first : first + piece].astype(jnp.bfloat16)
+            head = min(member, heads - 1)
+            out_ref[member, block, rows:, :HEAD] = earlier[:, head * HEAD : (head + 1) * HEAD]
+
+
+def my_member():
+    return lax.axis_index("y") * CS + lax.axis_index("c")
+
+
+def turned_x(step):
+    return lax.rem(lax.axis_index("x") + step, XS)
+
+
+def split_kernel(in_ref, *out_refs):
+    rows = in_ref.shape[2] - out_refs[0].shape[2]
+    for step, out_ref in zip((0, 1, 3, 2), out_refs):
+        request = turned_x(step) // 2
+        out_ref[...] = in_ref[:, pl.ds(request * 2, 2), rows:, :HEAD]
 
 
 def head_lanes(head, heads):
     return pl.ds(pl.multiple_of(jnp.minimum(head, heads - 1) * HEAD, HEAD), HEAD)
 
 
-def project_kernel(with_extra, where_ref, *refs):
+def project_kernel(with_extra, tok_rows, *refs):
     if with_extra:
         in_ref, own_ref, left_ref, right_ref, far_a_ref, far_b_ref, more_ref = refs[:7]
     else:
         in_ref, own_ref, left_ref, right_ref, far_a_ref, far_b_ref = refs[:6]
     send_ref, keep_ref, extra_ref = refs[-3:]
-    me = where_ref[0]
-    core = where_ref[1]
-    members, _, tok_rows, piece = in_ref.shape
+    core = lax.axis_index("c")
+    members, piece = in_ref.shape[0], in_ref.shape[3]
     rows = members * tok_rows
     parts = own_ref.shape[0]
     heads = own_ref.shape[2] // HEAD
@@ -82,8 +101,7 @@
     requests = extra_ref.shape[1] // (parts * GROUP)
 
     def rows_of(step):
-        block = lax.rem(me + step, XS)
-        return in_ref[:, pl.ds(block, 1)].reshape(rows, piece)
+        return in_ref[:, pl.ds(turned_x(step), 1), :tok_rows].reshape(rows, piece)
 
     inputs = [rows_of(step) for step in (0, 3, 1, 2)]
     for side, out_ref in ((1 - core, send_ref), (core, keep_ref)):
@@ -127,16 +145,16 @@
                 out_ref[slot, rows:] = jnp.concatenate(blocks, axis=0)
 
 
-def project(me_x, me_c, requests, pieces, weights, more=None):
-    rows = pieces.shape[0] * pieces.shape[2]
+def project(tok_rows, requests, pieces, weights, more=None):
+    rows = pieces.shape[0] * tok_rows
     parts = weights[0].shape[0]
     extra = 0 if more is None else 3 * GROUP * requests
     out = bf16(YS, rows + extra, parts * HEAD)
     kept = jax.ShapeDtypeStruct((GROUP, parts * GROUP * requests, HEAD), jnp.float32)
     return in_vmem(
-        functools.partial(project_kernel, more is not None),
+        functools.partial(project_kernel, more is not None, tok_rows),
         (out, out, kept),
-        [jnp.stack([me_x, me_c])],
+        [],
         [pieces, *weights] + ([] if more is None else [more]),
     )
 
@@ -159,14 +177,14 @@
     return total
 
 
-def finish_kv_kernel(member_ref, partial_ref, bias_ref, out_ref):
-    lanes = head_lanes(member_ref[0], bias_ref.shape[1] // HEAD)
+def finish_kv_kernel(partial_ref, bias_ref, out_ref):
+    lanes = head_lanes(my_member(), bias_ref.shape[1] // HEAD)
     bias = jnp.concatenate([bias_ref[1:2, lanes], bias_ref[2:3, lanes]], axis=1)
     out_ref[...] = (summed_rows(partial_ref) + bias).astype(jnp.bfloat16)
 
 
-def finish_q_kernel(member_ref, partial_ref, bias_ref, out_ref, decode_ref):
-    lanes = head_lanes(member_ref[0], bias_ref.shape[1] // HEAD)
+def finish_q_kernel(partial_ref, bias_ref, out_ref, decode_ref):
+    lanes = head_lanes(my_member(), bias_ref.shape[1] // HEAD)
     total = summed_rows(partial_ref)
     rows = out_ref.shape[0]
     queries = (total[:rows] + bias_ref[0:1, lanes]) * HEAD ** (-0.5)
@@ -174,9 +192,10 @@
     decode_ref[...] = total[rows:]
 
 
-def attend_kernel(pre_dev, where_ref, query_ref, own_ref, last_ref, prior_ref, out_ref):
-    odd = where_ref[0]
-    start = where_ref[1]
+def attend_kernel(pre_dev, offset_ref, query_ref, own_ref, last_ref, *refs):
+    prior_refs, out_ref = refs[:-1], refs[-1]
+    odd = lax.axis_index("x") % 2
+    start = offset_ref[lax.axis_index("x") // 2]
     rows = query_ref.shape[0]
     count = rows // 4
     tok_rows = rows // GROUP
@@ -190,12 +209,13 @@
     own_pos = jnp.where(is_prefill, start + odd * half + local(key_row), FAR_AWAY)
     last_pos = jnp.where(is_prefill, start + local(key_row), FAR_AWAY)
     last_pos = jnp.where(odd == 1, last_pos, FAR_AWAY)
-    old = prior_ref.shape[0] * prior_ref.shape[2]
-    old_pos = lax.broadcasted_iota(jnp.int32, (1, old), 1)
+    old = prior_refs[0].shape[0] * prior_refs[0].shape[2]
+    near_old = lax.broadcasted_iota(jnp.int32, (1, old), 1)
+    old_pos = jnp.concatenate([turned_x(step) * old + near_old for step in (0, 3, 1, 2)], axis=1)
     old_pos = jnp.where(old_pos < start, old_pos, FAR_AWAY)
     key_pos = jnp.concatenate([own_pos, last_pos, old_pos], axis=1)
-    prior_keys = prior_ref[:, 0].reshape(old, HEAD)
-    prior_values = prior_ref[:, 1].reshape(old, HEAD)
+    prior_keys = jnp.concatenate([ref[:, 0].reshape(old, HEAD) for ref in prior_refs], axis=0)
+    prior_values = jnp.concatenate([ref[:, 1].reshape(old, HEAD) for ref in prior_refs], axis=0)
     for step in range(rows // count):
         queries = query_ref[step * count : (step + 1) * count]
         row = step * count + lax.broadcasted_iota(jnp.int32, (count, 1), 0)
@@ -281,16 +301,21 @@
 def pack_kernel(prefill_ref, decode_ref, out_ref):
     rows = prefill_ref.shape[0]
     extra = decode_ref[...].reshape(decode_ref.shape[0] * GROUP, HEAD).astype(jnp.bfloat16)
-    for target in range(GROUP):
-        out_ref[target, :rows] = prefill_ref[...]
-        out_ref[target, rows:] = extra
-
-
-def out_kernel(where_ref, in_ref, own_ref, left_ref, right_ref, far_ref, out_ref, attn_ref, w_ref):
-    me = where_ref[0]
+    out_ref[:rows] = prefill_ref[...]
+    out_ref[rows:] = extra
+
+
+def out_kernel(*refs):
+    part_refs, w_refs = refs[: 2 * YS], refs[2 * YS : 2 * YS + XS]
+    out_ref, in_ref, attn_ref, w_ref = refs[2 * YS + XS :]
     heads = attn_ref.shape[1] // HEAD
     rows = attn_ref.shape[0]
     tok_rows = rows // GROUP
+    core = lax.axis_index("c")
+    for index, ref in enumerate(part_refs):
+        source_y = lax.rem(lax.axis_index("y") + (0, 3, 1, 2)[index % YS], YS)
+        source_c = core if index < YS else 1 - core
+        in_ref[source_y * CS + source_c] = ref[...]
     extra = in_ref[:, rows:].astype(jnp.float32)
     requests = extra.shape[1] // GROUP
     place = lax.broadcasted_iota(jnp.int32, (1, tok_rows, 1), 1)
@@ -302,8 +327,8 @@
             values = jnp.where(place == tok_rows - requests + request, row, values)
         values = values.astype(jnp.bfloat16).reshape(rows, HEAD)
         attn_ref[:, head * HEAD : (head + 1) * HEAD] = values
-    for step, ref in ((0, own_ref), (3, left_ref), (1, right_ref), (2, far_ref)):
-        w_ref[lax.rem(me + step, XS)] = ref[...]
+    for step, ref in zip((0, 3, 1, 2), w_refs):
+        w_ref[turned_x(step)] = ref[...]
     weights = w_ref[...].reshape(XS * w_ref.shape[1], w_ref.shape[2])
     out_ref[...] = product_t(attn_ref[...], weights).astype(jnp.bfloat16)
 
@@ -336,10 +361,7 @@
     dec_len,
     offsets,
 ):
-    me_x = lax.axis_index("x")
-    me_c = lax.axis_index("c")
     me_z = lax.axis_index("z")
-    member = lax.axis_index("y") * CS + me_c
     tok_rows, width = hidden.shape
     dec_dev = dec_cache.shape[0]
     pre_dev = tok_rows - dec_dev
@@ -347,7 +369,6 @@
     heads = head_width // HEAD
     pcb = prior_kv.shape[0]
     rows = GROUP * tok_rows
-    start = jnp.where(me_x // 2 == 0, offsets[0], offsets[1])
     half = w_qkv.shape[0] // 2
 
     turned = w_qkv.transpose(1, 0, 2)
@@ -364,31 +385,29 @@
 
     pieces = in_vmem(
         norm_kernel,
-        bf16(GROUP, XS, tok_rows, width // (XS * GROUP)),
+        bf16(GROUP, XS, tok_rows + pcb, width // (XS * GROUP)),
         [],
-        [hidden, ln_gain[None], ln_bias[None]],
+        [hidden, ln_gain[None], ln_bias[None], prior_kv],
     )
     pieces = lax.all_to_all(pieces, ("y", "c"), 0, 0, tiled=True)
-
-    prior = prior_kv.reshape(pcb, 2, 2, heads, HEAD)
-    prior = jnp.pad(prior, ((0, 0), (0, 0), (0, 0), (0, GROUP - heads), (0, 0)))
-    prior = prior.transpose(1, 3, 2, 0, 4)
-    prior = jnp.repeat(prior, 2, axis=0).reshape(XS * GROUP, 2, pcb, HEAD)
-    pieces, prior = lax.optimization_barrier((pieces, prior))
-    prior = lax.all_to_all(prior, ("x", "y", "c"), 0, 0, tiled=True)
-
-    where = member[None]
+    prior = in_vmem(split_kernel, (bf16(GROUP, 2, pcb, HEAD),) * XS, [], [pieces])
+    prior = (
+        prior[0],
+        lax.ppermute(prior[1], "x", shift(XS, 1)),
+        lax.ppermute(prior[2], "x", shift(XS, -1)),
+        lax.ppermute(prior[3], "x", shift(XS, 2)),
+    )
+
     kv_send, kv_keep, kv_extra = project(
-        me_x, me_c, dec_dev, pieces, (kv_own, kv_left, kv_right, kv_far_a, kv_far_b)
-    )
-    kv_keep, prior = lax.optimization_barrier((kv_keep, prior))
+        tok_rows, dec_dev, pieces, (kv_own, kv_left, kv_right, kv_far_a, kv_far_b)
+    )
     kv_parts = reduce_partial(kv_send, kv_keep)
-    own_kv = in_vmem(finish_kv_kernel, bf16(rows, 2 * HEAD), [where], [kv_parts, qkv_bias])
+    own_kv = in_vmem(finish_kv_kernel, bf16(rows, 2 * HEAD), [], [kv_parts, qkv_bias])
     last_kv = lax.ppermute(own_kv, "x", [(0, 1), (2, 3)])
 
     q_far_a, q_far_b, w_out = lax.optimization_barrier((q_far_a, q_far_b, w_out))
     q_send, q_keep, _ = project(
-        me_x, me_c, dec_dev, pieces, (q_own, q_left, q_right, q_far_a, q_far_b), kv_extra
+        tok_rows, dec_dev, pieces, (q_own, q_left, q_right, q_far_a, q_far_b), kv_extra
     )
     q_parts = reduce_partial(q_send, q_keep)
     w_own = w_out.T
@@ -402,7 +421,7 @@
             bf16(rows, HEAD),
             jax.ShapeDtypeStruct((3 * GROUP * dec_dev, HEAD), jnp.float32),
         ),
-        [where],
+        [],
         [q_parts, qkv_bias],
     )
     tied_kv, queries = lax.optimization_barrier((own_kv, queries))
@@ -412,25 +431,26 @@
     prefilled = in_vmem(
         functools.partial(attend_kernel, pre_dev),
         bf16(rows, HEAD),
-        [jnp.stack([me_x % 2, start])],
-        [queries, own_kv, last_kv, prior],
+        [offsets],
+        [queries, own_kv, last_kv, *prior],
     )
     head_bias = jnp.pad(qkv_bias.reshape(3, heads, HEAD), ((0, 0), (0, GROUP - heads), (0, 0)))
+    prefilled, sums = lax.optimization_barrier((prefilled, sums))
     decoded = decode(dec_len, sums, head_bias, dec_cache)
-    payload = in_vmem(
-        pack_kernel, bf16(GROUP, rows + dec_dev * GROUP, HEAD), [], [prefilled, decoded]
-    )
+    payload = in_vmem(pack_kernel, bf16(rows + dec_dev * GROUP, HEAD), [], [prefilled, decoded])
     payload, new_kv, w_left, w_right, w_far = lax.optimization_barrier(
         (payload, new_kv, w_left, w_right, w_far)
     )
-    gathered = lax.all_to_all(payload, ("y", "c"), 0, 0, tiled=True)
+    gathered = [payload] + [lax.ppermute(payload, "y", shift(YS, s)) for s in (1, -1, 2)]
+    gathered += [lax.ppermute(part, "c", [(0, 1), (1, 0)]) for part in gathered]
     piece = w_own.shape[0]
     shares = in_vmem(
         out_kernel,
         bf16(rows, XS * piece),
-        [me_x[None]],
-        [gathered, w_own, w_left, w_right, w_far],
+        [],
+        [*gathered, w_own, w_left, w_right, w_far],
         [
+            pltpu.VMEM((GROUP, *payload.shape), jnp.bfloat16),
             pltpu.VMEM((rows, head_width), jnp.bfloat16),
             pltpu.VMEM((XS, piece, head_width), jnp.bfloat16),
         ],

time: 206 us -> 207 us (level)
  blocking collectives: 38 us -> 0 us
  waiting for transfers between devices: 79.6 us -> 106 us
  starting transfers between devices: 43.5 us -> 61 us
  local copies, waits for them, and re-layouts: 16.5 us -> 12.3 us
    all_to_all x2 -> x0, blocking collectives: 38 us -> none  [the longest x1 20.5 us: on_device(): gathered = lax.all_to_all(payload, ('y', 'c'), 0, 0, tiled=True)]
    ppermute x0 -> x10, waiting for transfers between devices: none -> 22.4 us  [the longest x1 11 us: on_device(): lax.ppermute(prior[1], 'x', shift(XS, 1))]
    ppermute x0 -> x10, starting transfers between devices: none -> 12.6 us  [the longest x3 5.35 us: on_device(): lax.ppermute(payload, 'y', shift(YS, s))]
    ppermute x1, waiting for transfers between devices: 0.01 us -> 3.18 us  [on_device(): q_left = lax.ppermute(q_own, 'x', shift(XS, 1))]
    all_to_all x2, waiting for transfers between devices: 5.19 us -> 2.22 us  [reduce_partial(): return lax.all_to_all(partial, 'y', 0, 0, tiled=True)]
    all_to_all x2, starting transfers between devices: 7.12 us -> 9.65 us  [reduce_partial(): return lax.all_to_all(partial, 'y', 0, 0, tiled=True)]
    all_to_all x1, waiting for transfers between devices: 0.01 us -> 2.13 us  [on_device(): pieces = lax.all_to_all(pieces, ('y', 'c'), 0, 0, tiled=True)]
    pallas_call x11 -> x12, Pallas kernels: 19.4 us -> 20.3 us  [in_vmem(): pl.pallas_call(kernel, out_shape=out_shape, in_specs=[pl.BlockSpec(memory...]
  transfers between devices with their start and end apart: 20 -> 30, of which waited for: 12 -> 21; matrix products, arithmetic and copies ran while one was open for 5% -> 3% of each run, Pallas kernels for 8% -> 8%
where the time goes in v1:
time: 207 us; the launch traced here: 205 us
  waiting for transfers between devices  106 us (51%)
  starting transfers between devices  61 us (29%)
  Pallas kernels  24.7 us (12%)
  local copies, waits for them, and re-layouts  12.3 us (6%)
    all_to_all x1, waiting for transfers between devices, on_device(): lax.all_to_all(result, 'z', 0, 0, tiled=True).reshape(tok_rows, width)  25.2 us
    all_to_all x1, waiting for transfers between devices, on_device(): shares = lax.all_to_all(shares, ('y', 'c', 'z'), 0, 0, tiled=True)  24.9 us
    pallas_call x12, Pallas kernels, in_vmem(): pl.pallas_call(kernel, out_shape=out_shape, in_specs=[pl.BlockSpec(memory...  20.3 us
    all_to_all x1, starting transfers between devices, on_device(): shares = lax.all_to_all(shares, ('y', 'c', 'z'), 0, 0, tiled=True)  11.1 us
    ppermute x1, waiting for transfers between devices, on_device(): lax.ppermute(prior[1], 'x', shift(XS, 1))  11 us
    ppermute x1, waiting for transfers between devices, on_device(): kv_left = lax.ppermute(kv_own, 'x', shift(XS, 1))  9.66 us
    all_to_all x2, starting transfers between devices, reduce_partial(): return lax.all_to_all(partial, 'y', 0, 0, tiled=True)  9.65 us
    ppermute x3, starting transfers between devices, on_device(): lax.ppermute(payload, 'y', shift(YS, s))  5.35 us
  transfers between devices with their start and end apart: 30, of which 21 were waited for; matrix products, arithmetic and copies ran while one was open for 3% of the time, Pallas kernels for 8%

profile of v1, /device:TPU:2, one launch (start us, length us, event | category | flops | bytes accessed | tf_op | source)
XLA Modules:
  0.0 204.9 jit_solution(17015231832762838498)
XLA Ops:
  0.7 1.3 slice.28.refs_1_
  2.0 1.6 collective-permute-start
  3.5 0.8 collective-permute-start.1
  4.4 2.4 %shard_map.122 = bf16[8,4,80,224]{3,2,1,0:T(8,128)(2,1)} custom-call(bf16[64,7168]{1,0:T(8,128)(2,1)S(1)} %copy-done.1, f32[1,7168]{1,0:T(1,128)S(1)} %bitcast.15, f32[1,7168]{1,0:T(1,128)S(1)} %bitcast.16, bf16[16,2,2,896]{3,2,1,0:T(2,128)(2,1)S(1)} %copy-done.4), custom_call_target="tpu_custom_call" | custom-call | tf_op jit(solution)/shard_map/pallas_call | solution.py:27
  6.8 4.2 %all-to-all-start = ((bf16[8,4,80,224]{3,2,1,0:T(8,128)(2,1)}), bf16[8,4,80,224]{3,2,1,0:T(8,128)(2,1)S(1)}, u32[]{:S(2)}, u32[]{:S(2)}) async-start(bf16[8,4,80,224]{3,2,1,0:T(8,128)(2,1)} %shard_map.122), calls=%async_computation | async-start | bytes 2621440 | tf_op jit(solution)/shard_map/all_to_all | solution.py:392
  11.0 1.0 slice.29.refs_1_
  12.0 9.7 %collective-permute-done.refs_2_ = bf16[2,224,896]{2,1,0:T(8,128)(2,1)S(1)} collective-permute-done((bf16[2,224,896]{2,1,0:T(8,128)(2,1)S(1)}, bf16[2,224,896]{2,1,0:T(8,128)(2,1)S(1)}, u32[]{:S(2)}, u32[]{:S(2)}) %collective-permute-start) | collective-permute-done | bytes 802848 | tf_op jit(solution)/shard_map/ppermute | solution.py:376
  21.7 1.3 collective-permute-done.1.refs_3_
  23.0 0.8 slice.23
  23.8 1.2 collective-permute-start.2
  25.0 1.8 slice.24
  26.8 0.8 collective-permute-start.3
  27.6 2.1 %all-to-all-done.refs_0_.in_ref = bf16[8,4,80,224]{3,2,1,0:T(8,128)(2,1)S(1)} async-done(((bf16[8,4,80,224]{3,2,1,0:T(8,128)(2,1)}), bf16[8,4,80,224]{3,2,1,0:T(8,128)(2,1)S(1)}, u32[]{:S(2)}, u32[]{:S(2)}) %all-to-all-start) | async-done | bytes 1146912 | tf_op jit(solution)/shard_map/all_to_all | solution.py:392
  29.7 4.3 %collective-permute-done.2.refs_4_ = bf16[2,112,896]{2,1,0:T(8,128)(2,1)} collective-permute-done((bf16[2,112,896]{2,1,0:T(8,128)(2,1)}, bf16[2,112,896]{2,1,0:T(8,128)(2,1)}, u32[]{:S(2)}, u32[]{:S(2)}) %collective-permute-start.2) | collective-permute-done | bytes 401440 | tf_op jit(solution)/shard_map/ppermute | solution.py:379
  34.0 2.5 %collective-permute-done.3.refs_5_ = bf16[2,112,896]{2,1,0:T(8,128)(2,1)} collective-permute-done((bf16[2,112,896]{2,1,0:T(8,128)(2,1)}, bf16[2,112,896]{2,1,0:T(8,128)(2,1)}, u32[]{:S(2)}, u32[]{:S(2)}) %collective-permute-start.3) | collective-permute-done | bytes 401440 | tf_op jit(solution)/shard_map/ppermute | solution.py:380
  36.5 3.7 %shard_map.123 = (bf16[4,512,256]{2,1,0:T(8,128)(2,1)S(1)}, bf16[4,512,256]{2,1,0:T(8,128)(2,1)S(1)}, f32[8,32,128]{2,1,0:T(8,128)S(1)}) custom-call(bf16[8,4,80,224]{3,2,1,0:T(8,128)(2,1)S(1)} %all-to-all-done.refs_0_.in_ref, bf16[2,224,896]{2,1,0:T(8,128)(2,1)S(1)} %slice.28.refs_1_, bf16[2,224,896]{2,1,0:T(8,128)(2,1)S(1)} %collective-permute-done.refs_2_, ...), custom_call_target="tpu_custom_call" | custom-call | tf_op jit(solution)/shard_map/pallas_call | solution.py:27
  40.4 0.8 collective-permute-start.5
  41.2 1.3 collective-permute-start.6
  42.5 0.5 collective-permute-done.4.right_ref
  43.0 1.2 shard_map.124
  44.3 4.6 %all-to-all-start.1 = ((bf16[4,512,256]{2,1,0:T(8,128)(2,1)}), bf16[4,512,256]{2,1,0:T(8,128)(2,1)S(1)}, u32[]{:S(2)}, u32[]{:S(2)}) async-start(bf16[4,512,256]{2,1,0:T(8,128)(2,1)} %shard_map.124), calls=%async_computation.1 | async-start | bytes 2097152 | tf_op jit(solution)/shard_map/all_to_all | solution.py:170
  48.9 3.2 %collective-permute-done.5.refs_2_ = bf16[1,224,896]{2,1,0:T(8,128)(2,1)S(1)} collective-permute-done((bf16[1,224,896]{2,1,0:T(8,128)(2,1)S(1)}, bf16[1,224,896]{2,1,0:T(8,128)(2,1)S(1)}, u32[]{:S(2)}, u32[]{:S(2)}) %collective-permute-start.5) | collective-permute-done | bytes 401440 | tf_op jit(solution)/shard_map/ppermute | solution.py:381
  52.1 0.8 collective-permute-start.7
  52.9 0.3 collective-permute-done.6.refs_3_
  53.2 0.9 slice.31
  54.1 1.3 collective-permute-start.8
  55.4 3.7 %collective-permute-done.7.refs_4_ = bf16[1,112,896]{2,1,0:T(8,128)(2,1)S(1)} collective-permute-done((bf16[1,112,896]{2,1,0:T(8,128)(2,1)S(1)}, bf16[1,112,896]{2,1,0:T(8,128)(2,1)S(1)}, u32[]{:S(2)}, u32[]{:S(2)}) %collective-permute-start.7) | collective-permute-done | bytes 200736 | tf_op jit(solution)/shard_map/ppermute | solution.py:383
  59.1 1.7 collective-permute-done.8.refs_5_
  60.8 2.9 %shard_map.126 = (bf16[4,560,128]{2,1,0:T(8,128)(2,1)S(1)}, bf16[4,560,128]{2,1,0:T(8,128)(2,1)S(1)}, f32[8,16,128]{2,1,0:T(8,128)}) custom-call(bf16[8,4,80,224]{3,2,1,0:T(8,128)(2,1)S(1)} %all-to-all-done.refs_0_.in_ref, bf16[1,224,896]{2,1,0:T(8,128)(2,1)S(1)} %slice.29.refs_1_, bf16[1,224,896]{2,1,0:T(8,128)(2,1)S(1)} %collective-permute-done.5.refs_2_, ...), custom_call_target="tpu_custom_call" | custom-call | tf_op jit(solution)/shard_map/pallas_call | solution.py:27
  63.7 2.0 collective-permute-done.9.right_ref
  65.7 0.9 shard_map.127
  66.6 5.0 %all-to-all-start.2 = ((bf16[4,560,128]{2,1,0:T(8,128)(2,1)}), bf16[4,560,128]{2,1,0:T(8,128)(2,1)S(1)}, u32[]{:S(2)}, u32[]{:S(2)}) async-start(bf16[4,560,128]{2,1,0:T(8,128)(2,1)} %shard_map.127), calls=%async_computation.2 | async-start | bytes 1146880 | tf_op jit(solution)/shard_map/all_to_all | solution.py:170
  71.6 1.7 collective-permute-start.14
  73.3 0.4 collective-permute-start.15
  73.6 3.9 %collective-permute-start.16 = (bf16[224,896]{1,0:T(8,128)(2,1)S(1)}, bf16[224,896]{1,0:T(8,128)(2,1)}, u32[]{:S(2)}, u32[]{:S(2)}) collective-permute-start(bf16[224,896]{1,0:T(8,128)(2,1)S(1)} %bitcast.13), channel_id=1, source_target_pairs={{0,128},{64,192},{128,0},{192,64},{1,129},{65,193},{129,1},{193,65... | collective-permute-start | bytes 1204232 | tf_op jit(solution)/shard_map/ppermute | solution.py:416
  77.5 0.9 shard_map.125.own_ref
  78.4 1.3 collective-permute-start.10
  79.7 2.2 %all-to-all-done.2.partial_ref = bf16[4,560,128]{2,1,0:T(8,128)(2,1)S(1)} async-done(((bf16[4,560,128]{2,1,0:T(8,128)(2,1)}), bf16[4,560,128]{2,1,0:T(8,128)(2,1)S(1)}, u32[]{:S(2)}, u32[]{:S(2)}) %all-to-all-start.2) | async-done | bytes 573472 | tf_op jit(solution)/shard_map/all_to_all | solution.py:170
  82.0 3.4 %all-to-all-start.3 = ((bf16[8,64,256]{2,1,0:T(8,128)(2,1)}), bf16[8,64,256]{2,1,0:T(8,128)(2,1)S(1)}, u32[]{:S(2)}, u32[]{:S(2)}) async-start(bf16[8,64,256]{2,1,0:T(8,128)(2,1)} %bitcast.3), calls=%async_computation.3 | async-start | bytes 524288 | tf_op jit(solution)/shard_map/all_to_all | solution.py:428
  85.5 1.8 collective-permute-start.11
  87.3 11.0 %collective-permute-done.11.refs_1_ = bf16[8,2,16,128]{3,2,1,0:T(8,128)(2,1)S(1)} collective-permute-done((bf16[8,2,16,128]{3,2,1,0:T(8,128)(2,1)S(1)}, bf16[8,2,16,128]{3,2,1,0:T(8,128)(2,1)S(1)}, u32[]{:S(2)}, u32[]{:S(2)}) %collective-permute-start.11) | collective-permute-done | bytes 65568 | tf_op jit(solution)/shard_map/ppermute | solution.py:396
  98.3 4.3 %collective-permute-done.12.refs_2_ = bf16[8,2,16,128]{3,2,1,0:T(8,128)(2,1)S(1)} collective-permute-done((bf16[8,2,16,128]{3,2,1,0:T(8,128)(2,1)S(1)}, bf16[8,2,16,128]{3,2,1,0:T(8,128)(2,1)S(1)}, u32[]{:S(2)}, u32[]{:S(2)}) %collective-permute-start.12) | collective-permute-done | bytes 65568 | tf_op jit(solution)/shard_map/ppermute | solution.py:397
  102.6 5.1 %collective-permute-start.13 = (bf16[8,2,16,128]{3,2,1,0:T(8,128)(2,1)S(1)}, bf16[8,2,16,128]{3,2,1,0:T(8,128)(2,1)S(1)}, u32[]{:S(2)}, u32[]{:S(2)}) collective-permute-start(bf16[8,2,16,128]{3,2,1,0:T(8,128)(2,1)S(1)} %get-tuple-element.43), channel_id=1, source_target_pairs={{0,128},{64,192},{128,0},{192,64},{1,129},{65,193},{129,1},{193,65... | collective-permute-start | bytes 196616 | tf_op jit(solution)/shard_map/ppermute | solution.py:398
  108.0 0.3 reshape.25
  108.3 1.7 collective-permute-done.13.refs_3_
  110.0 3.1 %shard_map.130.prefill_ref = bf16[512,128]{1,0:T(8,128)(2,1)S(1)} custom-call(s32[2]{0:T(128)S(1)} %copy-done.8, bf16[512,128]{1,0:T(8,128)(2,1)S(1)} %get-tuple-element.39.query_ref, bf16[512,256]{1,0:T(8,128)(2,1)} %shard_map.125.own_ref, bf16[512,256]{1,0:T(8,128)(2,1)S(1)} %collective-permute-done.10.last_ref, ...), custom_call_target="tpu_custom_call" | custom-call | tf_op jit(solution)/shard_map/pallas_call | solution.py:27
  113.1 3.1 %copy-done = bf16[2,1024,2,896]{3,2,1,0:T(2,128)(2,1)S(1)} copy-done((bf16[2,1024,2,896]{3,2,1,0:T(2,128)(2,1)S(1)}, bf16[2,1024,2,896]{3,2,1,0:T(2,128)(2,1)}, u32[]{:S(2)}) %copy-start) | copy-done | bytes 7340056
  116.2 4.4 %decode.1.decode_ref = f32[2,8,128]{2,1,0:T(8,128)S(1)} custom-call(s32[2]{0:T(128)S(1)} %copy-done.9, f32[48,128]{1,0:T(8,128)S(1)} %get-tuple-element.46.sums_ref, f32[3,8,128]{2,1,0:T(8,128)S(1)} %pad.4.bias_ref, bf16[2,1024,2,896]{3,2,1,0:T(2,128)(2,1)S(1)} %copy-done), custom_call_target="tpu_custom_call" | custom-call | tf_op jit(solution)/shard_map/decode/pallas_call | solution.py:285
  120.7 1.8 collective-permute-start.17
  122.5 1.5 collective-permute-start.18
  124.0 2.0 collective-permute-start.19
  126.0 1.4 collective-permute-done.17.refs_1_
  127.5 0.4 collective-permute-start.22
  127.9 2.6 %collective-permute-done.19.refs_3_ = bf16[528,128]{1,0:T(8,128)(2,1)S(1)} collective-permute-done((bf16[528,128]{1,0:T(8,128)(2,1)S(1)}, bf16[528,128]{1,0:T(8,128)(2,1)S(1)}, u32[]{:S(2)}, u32[]{:S(2)}) %collective-permute-start.19) | collective-permute-done | bytes 135200 | tf_op jit(solution)/shard_map/ppermute | solution.py:444
  130.5 1.3 collective-permute-done.23.refs_7_
  131.9 3.7 %shard_map.132 = bf16[512,896]{1,0:T(8,128)(2,1)} custom-call(bf16[528,128]{1,0:T(8,128)(2,1)S(1)} %shard_map.131.refs_0_, bf16[528,128]{1,0:T(8,128)(2,1)S(1)} %collective-permute-done.17.refs_1_, bf16[528,128]{1,0:T(8,128)(2,1)S(1)} %collective-permute-done.18.refs_2_, bf16[528,128]{1,0:T(8,128)(2,1)S(1)} %collective-permute-done.19.refs_3_, ...), custom_call_target="tpu_custom_call" | custom-call | tf_op jit(solution)/shard_map/pallas_call | solution.py:27
  135.5 11.1 %all-to-all-start.4 = ((bf16[64,8,896]{2,1,0:T(8,128)(2,1)}), bf16[64,8,896]{2,1,0:T(8,128)(2,1)S(1)}, u32[]{:S(2)}, u32[]{:S(2)}) async-start(bf16[64,8,896]{2,1,0:T(8,128)(2,1)} %bitcast.6), calls=%async_computation.4 | async-start | bytes 1835008 | tf_op jit(solution)/shard_map/all_to_all | solution.py:460
  146.6 0.9 constant_dynamic-slice_fusion.hid_ref
  147.5 24.9 %all-to-all-done.4.in_ref = bf16[64,8,896]{2,1,0:T(8,128)(2,1)S(1)} async-done(((bf16[64,8,896]{2,1,0:T(8,128)(2,1)}), bf16[64,8,896]{2,1,0:T(8,128)(2,1)S(1)}, u32[]{:S(2)}, u32[]{:S(2)}) %all-to-all-start.4) | async-done | bytes 917536 | tf_op jit(solution)/shard_map/all_to_all | solution.py:460
  172.5 1.2 shard_map.133
  173.6 4.2 %all-to-all-start.5 = ((bf16[8,8,7168]{2,1,0:T(8,128)(2,1)}), bf16[8,8,7168]{2,1,0:T(8,128)(2,1)S(1)}, u32[]{:S(2)}, u32[]{:S(2)}) async-start(bf16[8,8,7168]{2,1,0:T(8,128)(2,1)} %shard_map.133), calls=%async_computation.5 | async-start | bytes 1835008 | tf_op jit(solution)/shard_map/all_to_all | solution.py:469
  177.8 0.9 copy.16
  178.7 25.2 %all-to-all-done.5 = bf16[8,8,7168]{2,1,0:T(8,128)(2,1)S(1)} async-done(((bf16[8,8,7168]{2,1,0:T(8,128)(2,1)}), bf16[8,8,7168]{2,1,0:T(8,128)(2,1)S(1)}, u32[]{:S(2)}, u32[]{:S(2)}) %all-to-all-start.5) | async-done | bytes 917536 | tf_op jit(solution)/shard_map/all_to_all | solution.py:469
  204.0 0.9 copy.18
  (44 shorter events, 0.7 us)
Async XLA Ops:
  0.6 3.8 %copy-start.5 = (f32[7168]{0:T(1024)S(1)}, f32[7168]{0:T(1024)}, u32[]{:S(2)}) copy-start(f32[7168]{0:T(1024)} %param.12) | copy-start | bytes 86020
  0.6 3.7 %copy-start.6 = (f32[7168]{0:T(1024)S(1)}, f32[7168]{0:T(1024)}, u32[]{:S(2)}) copy-start(f32[7168]{0:T(1024)} %param.13) | copy-start | bytes 86020
  0.7 3.7 %copy-start.1 = (bf16[64,7168]{1,0:T(8,128)(2,1)S(1)}, bf16[64,7168]{1,0:T(8,128)(2,1)}, u32[]{:S(2)}) copy-start(bf16[64,7168]{1,0:T(8,128)(2,1)} %hid_ref.1) | copy-start | bytes 2752516
  0.7 3.7 %copy-start.4 = (bf16[16,2,2,896]{3,2,1,0:T(2,128)(2,1)S(1)}, bf16[16,2,2,896]{3,2,1,0:T(2,128)(2,1)}, u32[]{:S(2)}) copy-start(bf16[16,2,2,896]{3,2,1,0:T(2,128)(2,1)} %prior_ref.1) | copy-start | bytes 344068
  2.0 19.7 %collective-permute-start = (bf16[2,224,896]{2,1,0:T(8,128)(2,1)S(1)}, bf16[2,224,896]{2,1,0:T(8,128)(2,1)S(1)}, u32[]{:S(2)}, u32[]{:S(2)}) collective-permute-start(bf16[2,224,896]{2,1,0:T(8,128)(2,1)S(1)} %slice.28.refs_1_), channel_id=1, source_target_pairs={{0,64},{64,128},{128,192},{192,0},{1,65},{65,129},{129,193},{193,1... | collective-permute-start | bytes 2408456 | tf_op jit(solution)/shard_map/ppermute | solution.py:376
  3.5 19.5 %collective-permute-start.1 = (bf16[2,224,896]{2,1,0:T(8,128)(2,1)S(1)}, bf16[2,224,896]{2,1,0:T(8,128)(2,1)}, u32[]{:S(2)}, u32[]{:S(2)}) collective-permute-start(bf16[2,224,896]{2,1,0:T(8,128)(2,1)S(1)} %slice.28.refs_1_), channel_id=1, source_target_pairs={{0,192},{64,0},{128,64},{192,128},{1,193},{65,1},{129,65},{193,129... | collective-permute-start | bytes 2408456 | tf_op jit(solution)/shard_map/ppermute | solution.py:377
  6.8 22.9 %all-to-all-start = ((bf16[8,4,80,224]{3,2,1,0:T(8,128)(2,1)}), bf16[8,4,80,224]{3,2,1,0:T(8,128)(2,1)S(1)}, u32[]{:S(2)}, u32[]{:S(2)}) async-start(bf16[8,4,80,224]{3,2,1,0:T(8,128)(2,1)} %shard_map.122), calls=%async_computation | async-start | bytes 2621440 | tf_op jit(solution)/shard_map/all_to_all | solution.py:392
  23.8 10.2 %collective-permute-start.2 = (bf16[2,112,896]{2,1,0:T(8,128)(2,1)}, bf16[2,112,896]{2,1,0:T(8,128)(2,1)}, u32[]{:S(2)}, u32[]{:S(2)}) collective-permute-start(bf16[2,112,896]{2,1,0:T(8,128)(2,1)} %slice.23), channel_id=1, source_target_pairs={{0,64},{64,128},{128,192},{192,0},{1,65},{65,129},{129,193},{193,1... | collective-permute-start | bytes 1204232 | tf_op jit(solution)/shard_map/ppermute | solution.py:379
  26.8 9.8 %collective-permute-start.3 = (bf16[2,112,896]{2,1,0:T(8,128)(2,1)}, bf16[2,112,896]{2,1,0:T(8,128)(2,1)}, u32[]{:S(2)}, u32[]{:S(2)}) collective-permute-start(bf16[2,112,896]{2,1,0:T(8,128)(2,1)} %slice.24), channel_id=1, source_target_pairs={{0,192},{64,0},{128,64},{192,128},{1,193},{65,1},{129,65},{193,129... | collective-permute-start | bytes 1204232 | tf_op jit(solution)/shard_map/ppermute | solution.py:380
  40.3 2.7 %collective-permute-start.4 = (bf16[4,512,256]{2,1,0:T(8,128)(2,1)S(1)}, bf16[4,512,256]{2,1,0:T(8,128)(2,1)S(1)}, u32[]{:S(2)}, u32[]{:S(2)}) collective-permute-start(bf16[4,512,256]{2,1,0:T(8,128)(2,1)S(1)} %get-tuple-element.31), channel_id=1, source_target_pairs={{0,8},{8,0},{1,9},{9,1},{2,10},{10,2},{3,11},{11,3},{4,12},{12,4},... | collective-permute-start | bytes 3145736 | tf_op jit(solution)/shard_map/ppermute | solution.py:168
  40.4 11.7 %collective-permute-start.5 = (bf16[1,224,896]{2,1,0:T(8,128)(2,1)S(1)}, bf16[1,224,896]{2,1,0:T(8,128)(2,1)S(1)}, u32[]{:S(2)}, u32[]{:S(2)}) collective-permute-start(bf16[1,224,896]{2,1,0:T(8,128)(2,1)S(1)} %slice.29.refs_1_), channel_id=1, source_target_pairs={{0,64},{64,128},{128,192},{192,0},{1,65},{65,129},{129,193},{193,1... | collective-permute-start | bytes 1204232 | tf_op jit(solution)/shard_map/ppermute | solution.py:381
  41.2 12.0 %collective-permute-start.6 = (bf16[1,224,896]{2,1,0:T(8,128)(2,1)S(1)}, bf16[1,224,896]{2,1,0:T(8,128)(2,1)}, u32[]{:S(2)}, u32[]{:S(2)}) collective-permute-start(bf16[1,224,896]{2,1,0:T(8,128)(2,1)S(1)} %slice.29.refs_1_), channel_id=1, source_target_pairs={{0,192},{64,0},{128,64},{192,128},{1,193},{65,1},{129,65},{193,129... | collective-permute-start | bytes 1204232 | tf_op jit(solution)/shard_map/ppermute | solution.py:382
  44.3 22.3 %all-to-all-start.1 = ((bf16[4,512,256]{2,1,0:T(8,128)(2,1)}), bf16[4,512,256]{2,1,0:T(8,128)(2,1)S(1)}, u32[]{:S(2)}, u32[]{:S(2)}) async-start(bf16[4,512,256]{2,1,0:T(8,128)(2,1)} %shard_map.124), calls=%async_computation.1 | async-start | bytes 2097152 | tf_op jit(solution)/shard_map/all_to_all | solution.py:170
  52.1 7.0 %collective-permute-start.7 = (bf16[1,112,896]{2,1,0:T(8,128)(2,1)S(1)}, bf16[1,112,896]{2,1,0:T(8,128)(2,1)S(1)}, u32[]{:S(2)}, u32[]{:S(2)}) collective-permute-start(bf16[1,112,896]{2,1,0:T(8,128)(2,1)S(1)} %slice.30), channel_id=1, source_target_pairs={{0,64},{64,128},{128,192},{192,0},{1,65},{65,129},{129,193},{193,1... | collective-permute-start | bytes 602120 | tf_op jit(solution)/shard_map/ppermute | solution.py:383
  54.1 6.6 %collective-permute-start.8 = (bf16[1,112,896]{2,1,0:T(8,128)(2,1)S(1)}, bf16[1,112,896]{2,1,0:T(8,128)(2,1)S(1)}, u32[]{:S(2)}, u32[]{:S(2)}) collective-permute-start(bf16[1,112,896]{2,1,0:T(8,128)(2,1)S(1)} %slice.31), channel_id=1, source_target_pairs={{0,192},{64,0},{128,64},{192,128},{1,193},{65,1},{129,65},{193,129... | collective-permute-start | bytes 602120 | tf_op jit(solution)/shard_map/ppermute | solution.py:384
  63.7 2.0 collective-permute-start.9
  65.6 6.0 %copy-start.2 = (bf16[896,224]{0,1:T(8,128)(2,1)S(1)}, bf16[896,224]{0,1:T(8,128)(2,1)}, u32[]{:S(2)}) copy-start(bf16[896,224]{0,1:T(8,128)(2,1)} %param.16) | copy-start | bytes 1204228
  65.7 11.9 %copy-start.3 = (f32[3,896]{1,0:T(4,128)S(1)}, f32[3,896]{1,0:T(4,128)}, u32[]{:S(2)}) copy-start(f32[3,896]{1,0:T(4,128)} %bias_ref.3) | copy-start | bytes 32260
  66.6 15.3 %all-to-all-start.2 = ((bf16[4,560,128]{2,1,0:T(8,128)(2,1)}), bf16[4,560,128]{2,1,0:T(8,128)(2,1)S(1)}, u32[]{:S(2)}, u32[]{:S(2)}) async-start(bf16[4,560,128]{2,1,0:T(8,128)(2,1)} %shard_map.127), calls=%async_computation.2 | async-start | bytes 1146880 | tf_op jit(solution)/shard_map/all_to_all | solution.py:170
  71.6 49.0 %collective-permute-start.14 = (bf16[224,896]{1,0:T(8,128)(2,1)S(1)}, bf16[224,896]{1,0:T(8,128)(2,1)}, u32[]{:S(2)}, u32[]{:S(2)}) collective-permute-start(bf16[224,896]{1,0:T(8,128)(2,1)S(1)} %bitcast.11), channel_id=1, source_target_pairs={{0,64},{64,128},{128,192},{192,0},{1,65},{65,129},{129,193},{193,1... | collective-permute-start | bytes 1204232 | tf_op jit(solution)/shard_map/ppermute | solution.py:414
  73.3 47.4 %collective-permute-start.15 = (bf16[224,896]{1,0:T(8,128)(2,1)S(1)}, bf16[224,896]{1,0:T(8,128)(2,1)}, u32[]{:S(2)}, u32[]{:S(2)}) collective-permute-start(bf16[224,896]{1,0:T(8,128)(2,1)S(1)} %bitcast.12), channel_id=1, source_target_pairs={{0,192},{64,0},{128,64},{192,128},{1,193},{65,1},{129,65},{193,129... | collective-permute-start | bytes 1204232 | tf_op jit(solution)/shard_map/ppermute | solution.py:415
  73.6 47.0 %collective-permute-start.16 = (bf16[224,896]{1,0:T(8,128)(2,1)S(1)}, bf16[224,896]{1,0:T(8,128)(2,1)}, u32[]{:S(2)}, u32[]{:S(2)}) collective-permute-start(bf16[224,896]{1,0:T(8,128)(2,1)S(1)} %bitcast.13), channel_id=1, source_target_pairs={{0,128},{64,192},{128,0},{192,64},{1,129},{65,193},{129,1},{193,65... | collective-permute-start | bytes 1204232 | tf_op jit(solution)/shard_map/ppermute | solution.py:416
  78.4 31.5 %collective-permute-start.10 = (bf16[512,256]{1,0:T(8,128)(2,1)}, bf16[512,256]{1,0:T(8,128)(2,1)S(1)}, u32[]{:S(2)}, u32[]{:S(2)}) collective-permute-start(bf16[512,256]{1,0:T(8,128)(2,1)} %shard_map.125.own_ref), channel_id=1, source_target_pairs={{0,64},{128,192},{1,65},{129,193},{2,66},{130,194},{3,67},{131,195... | collective-permute-start | bytes 786440 | tf_op jit(solution)/shard_map/ppermute | solution.py:406
  82.0 25.7 %all-to-all-start.3 = ((bf16[8,64,256]{2,1,0:T(8,128)(2,1)}), bf16[8,64,256]{2,1,0:T(8,128)(2,1)S(1)}, u32[]{:S(2)}, u32[]{:S(2)}) async-start(bf16[8,64,256]{2,1,0:T(8,128)(2,1)} %bitcast.3), calls=%async_computation.3 | async-start | bytes 524288 | tf_op jit(solution)/shard_map/all_to_all | solution.py:428
  85.4 24.5 %copy-start.8 = (s32[2]{0:T(128)S(1)}, s32[2]{0:T(128)}, u32[]{:S(2)}) copy-start(s32[2]{0:T(128)} %offset_ref.1) | copy-start | bytes 28
  85.5 12.8 %collective-permute-start.11 = (bf16[8,2,16,128]{3,2,1,0:T(8,128)(2,1)S(1)}, bf16[8,2,16,128]{3,2,1,0:T(8,128)(2,1)S(1)}, u32[]{:S(2)}, u32[]{:S(2)}) collective-permute-start(bf16[8,2,16,128]{3,2,1,0:T(8,128)(2,1)S(1)} %get-tuple-element.41), channel_id=1, source_target_pairs={{0,64},{64,128},{128,192},{192,0},{1,65},{65,129},{129,193},{193,1... | collective-permute-start | bytes 196616 | tf_op jit(solution)/shard_map/ppermute | solution.py:396
  98.3 4.3 %collective-permute-start.12 = (bf16[8,2,16,128]{3,2,1,0:T(8,128)(2,1)S(1)}, bf16[8,2,16,128]{3,2,1,0:T(8,128)(2,1)S(1)}, u32[]{:S(2)}, u32[]{:S(2)}) collective-permute-start(bf16[8,2,16,128]{3,2,1,0:T(8,128)(2,1)S(1)} %get-tuple-element.42), channel_id=1, source_target_pairs={{0,192},{64,0},{128,64},{192,128},{1,193},{65,1},{129,65},{193,129... | collective-permute-start | bytes 196616 | tf_op jit(solution)/shard_map/ppermute | solution.py:397
  102.6 7.3 %collective-permute-start.13 = (bf16[8,2,16,128]{3,2,1,0:T(8,128)(2,1)S(1)}, bf16[8,2,16,128]{3,2,1,0:T(8,128)(2,1)S(1)}, u32[]{:S(2)}, u32[]{:S(2)}) collective-permute-start(bf16[8,2,16,128]{3,2,1,0:T(8,128)(2,1)S(1)} %get-tuple-element.43), channel_id=1, source_target_pairs={{0,128},{64,192},{128,0},{192,64},{1,129},{65,193},{129,1},{193,65... | collective-permute-start | bytes 196616 | tf_op jit(solution)/shard_map/ppermute | solution.py:398
  107.8 5.4 %copy-start.9 = (s32[2]{0:T(128)S(1)}, s32[2]{0:T(128)}, u32[]{:S(2)}) copy-start(s32[2]{0:T(128)} %len_ref.1) | copy-start | bytes 28
  113.1 3.1 %copy-start = (bf16[2,1024,2,896]{3,2,1,0:T(2,128)(2,1)S(1)}, bf16[2,1024,2,896]{3,2,1,0:T(2,128)(2,1)}, u32[]{:S(2)}) copy-start(bf16[2,1024,2,896]{3,2,1,0:T(2,128)(2,1)} %cache_ref.1) | copy-start | bytes 22020100
  120.7 6.7 %collective-permute-start.17 = (bf16[528,128]{1,0:T(8,128)(2,1)S(1)}, bf16[528,128]{1,0:T(8,128)(2,1)S(1)}, u32[]{:S(2)}, u32[]{:S(2)}) collective-permute-start(bf16[528,128]{1,0:T(8,128)(2,1)S(1)} %shard_map.131.refs_0_), channel_id=1, source_target_pairs={{0,16},{16,32},{32,48},{48,0},{1,17},{17,33},{33,49},{49,1},{2,18}... | collective-permute-start | bytes 405512 | tf_op jit(solution)/shard_map/ppermute | solution.py:444
  122.5 5.0 %collective-permute-start.18 = (bf16[528,128]{1,0:T(8,128)(2,1)S(1)}, bf16[528,128]{1,0:T(8,128)(2,1)S(1)}, u32[]{:S(2)}, u32[]{:S(2)}) collective-permute-start(bf16[528,128]{1,0:T(8,128)(2,1)S(1)} %shard_map.131.refs_0_), channel_id=1, source_target_pairs={{0,48},{16,0},{32,16},{48,32},{1,49},{17,1},{33,17},{49,33},{2,50}... | collective-permute-start | bytes 405512 | tf_op jit(solution)/shard_map/ppermute | solution.py:444
  124.0 6.5 %collective-permute-start.19 = (bf16[528,128]{1,0:T(8,128)(2,1)S(1)}, bf16[528,128]{1,0:T(8,128)(2,1)S(1)}, u32[]{:S(2)}, u32[]{:S(2)}) collective-permute-start(bf16[528,128]{1,0:T(8,128)(2,1)S(1)} %shard_map.131.refs_0_), channel_id=1, source_target_pairs={{0,32},{16,48},{32,0},{48,16},{1,33},{17,49},{33,1},{49,17},{2,34}... | collective-permute-start | bytes 405512 | tf_op jit(solution)/shard_map/ppermute | solution.py:444
  126.0 4.5 %collective-permute-start.20 = (bf16[528,128]{1,0:T(8,128)(2,1)S(1)}, bf16[528,128]{1,0:T(8,128)(2,1)S(1)}, u32[]{:S(2)}, u32[]{:S(2)}) collective-permute-start(bf16[528,128]{1,0:T(8,128)(2,1)S(1)} %shard_map.131.refs_0_), channel_id=1, source_target_pairs={{0,8},{8,0},{1,9},{9,1},{2,10},{10,2},{3,11},{11,3},{4,12},{12,4},... | collective-permute-start | bytes 405512 | tf_op jit(solution)/shard_map/ppermute | solution.py:445
  127.4 3.1 %collective-permute-start.21 = (bf16[528,128]{1,0:T(8,128)(2,1)S(1)}, bf16[528,128]{1,0:T(8,128)(2,1)S(1)}, u32[]{:S(2)}, u32[]{:S(2)}) collective-permute-start(bf16[528,128]{1,0:T(8,128)(2,1)S(1)} %collective-permute-done.17.refs_1_), channel_id=1, source_target_pairs={{0,8},{8,0},{1,9},{9,1},{2,10},{10,2},{3,11},{11,3},{4,12},{12,4},... | collective-permute-start | bytes 405512 | tf_op jit(solution)/shard_map/ppermute | solution.py:445
  127.5 3.0 %collective-permute-start.22 = (bf16[528,128]{1,0:T(8,128)(2,1)S(1)}, bf16[528,128]{1,0:T(8,128)(2,1)S(1)}, u32[]{:S(2)}, u32[]{:S(2)}) collective-permute-start(bf16[528,128]{1,0:T(8,128)(2,1)S(1)} %collective-permute-done.18.refs_2_), channel_id=1, source_target_pairs={{0,8},{8,0},{1,9},{9,1},{2,10},{10,2},{3,11},{11,3},{4,12},{12,4},... | collective-permute-start | bytes 405512 | tf_op jit(solution)/shard_map/ppermute | solution.py:445
  130.5 1.4 collective-permute-start.23
  135.5 36.9 %copy-start.7 = (f32[7168]{0:T(1024)S(1)}, f32[7168]{0:T(1024)}, u32[]{:S(2)}) copy-start(f32[7168]{0:T(1024)} %param.17) | copy-start | bytes 86020
  135.5 36.9 %all-to-all-start.4 = ((bf16[64,8,896]{2,1,0:T(8,128)(2,1)}), bf16[64,8,896]{2,1,0:T(8,128)(2,1)S(1)}, u32[]{:S(2)}, u32[]{:S(2)}) async-start(bf16[64,8,896]{2,1,0:T(8,128)(2,1)} %bitcast.6), calls=%async_computation.4 | async-start | bytes 1835008 | tf_op jit(solution)/shard_map/all_to_all | solution.py:460
  173.6 30.4 %all-to-all-start.5 = ((bf16[8,8,7168]{2,1,0:T(8,128)(2,1)}), bf16[8,8,7168]{2,1,0:T(8,128)(2,1)S(1)}, u32[]{:S(2)}, u32[]{:S(2)}) async-start(bf16[8,8,7168]{2,1,0:T(8,128)(2,1)} %shard_map.133), calls=%async_computation.5 | async-start | bytes 1835008 | tf_op jit(solution)/shard_map/all_to_all | solution.py:469

commit v2 on v1

--- a/solution.py
+++ b/solution.py
@@ -22,8 +22,12 @@
     return [(i, (i + step) % axis_size) for i in range(axis_size)]
 
 
-def in_vmem(kernel, out_shape, scalars, arrays, scratch=()):
+def in_vmem(kernel, out_shape, scalars, arrays, scratch=(), loaded=()):
     vmem = pl.BlockSpec(memory_space=pltpu.VMEM)
+    held = [
+        pltpu.with_memory_space_constraint(a, pltpu.HBM if i in loaded else pltpu.VMEM)
+        for i, a in enumerate(arrays)
+    ]
     return pl.pallas_call(
         kernel,
         out_shape=out_shape,
@@ -31,7 +35,7 @@
         out_specs=jax.tree.map(lambda _: vmem, out_shape),
         scratch_shapes=list(scratch),
         compiler_params=pltpu.CompilerParams(vmem_limit_bytes=SMALL_VMEM),
-    )(*scalars, *[pltpu.with_memory_space_constraint(a, pltpu.VMEM) for a in arrays])
+    )(*scalars, *held)
 
 
 def bf16(*shape):
@@ -85,17 +89,15 @@
     return pl.ds(pl.multiple_of(jnp.minimum(head, heads - 1) * HEAD, HEAD), HEAD)
 
 
-def project_kernel(with_extra, tok_rows, *refs):
+def project_kernel(with_extra, tok_rows, parts, *refs):
+    in_ref, weight_refs = refs[0], refs[1:-3]
+    send_ref, keep_ref, extra_ref = refs[-3:]
     if with_extra:
-        in_ref, own_ref, left_ref, right_ref, far_a_ref, far_b_ref, more_ref = refs[:7]
-    else:
-        in_ref, own_ref, left_ref, right_ref, far_a_ref, far_b_ref = refs[:6]
-    send_ref, keep_ref, extra_ref = refs[-3:]
+        weight_refs, more_ref = weight_refs[:-1], weight_refs[-1]
     core = lax.axis_index("c")
     members, piece = in_ref.shape[0], in_ref.shape[3]
     rows = members * tok_rows
-    parts = own_ref.shape[0]
-    heads = own_ref.shape[2] // HEAD
+    heads = weight_refs[0].shape[1] // HEAD
     together = 2 // parts
     width = parts * HEAD
     requests = extra_ref.shape[1] // (parts * GROUP)
@@ -104,23 +106,27 @@
         return in_ref[:, pl.ds(turned_x(step), 1), :tok_rows].reshape(rows, piece)
 
     inputs = [rows_of(step) for step in (0, 3, 1, 2)]
-    for side, out_ref in ((1 - core, send_ref), (core, keep_ref)):
-        for first in range(0, YS, together):
-            slots = list(range(first, first + together))
+
+    def one_step(step, carry):
+        for side, out_ref in ((1 - core, send_ref), (core, keep_ref)):
+            slots = [together * step + index for index in range(together)]
             columns = [
                 (part, head_lanes(CS * slot + side, heads))
                 for slot in slots
                 for part in range(parts)
             ]
 
-            def wide(ref):
-                return jnp.concatenate([ref[part, :, lanes] for part, lanes in columns], axis=1)
-
-            weights = [wide(own_ref), wide(left_ref), wide(right_ref)]
-            weights.append(jnp.concatenate([wide(far_a_ref), wide(far_b_ref)], axis=0))
-            total = product(inputs[0], weights[0])
-            for left, right in zip(inputs[1:], weights[1:]):
-                total += product(left, right)
+            def wide(index):
+                blocks = []
+                for part, lanes in columns:
+                    held = weight_refs[index * parts + part :]
+                    held = held[:1] if index < XS - 1 or parts > 1 else held
+                    blocks.append(jnp.concatenate([ref[:, lanes] for ref in held], axis=0))
+                return jnp.concatenate(blocks, axis=1)
+
+            total = product(inputs[0], wide(0))
+            for index in range(1, XS):
+                total += product(inputs[index], wide(index))
             for index, slot in enumerate(slots):
                 mine = total[:, index * width : (index + 1) * width]
                 out_ref[slot, :rows] = mine.astype(jnp.bfloat16)
@@ -129,7 +135,11 @@
                     row = by_member[:, tok_rows - requests + request]
                     for part in range(parts):
                         place = (request * parts + part) * GROUP + CS * slot + side
-                        extra_ref[:, pl.ds(place, 1)] = row[:, None, part * HEAD : (part + 1) * HEAD]
+                        lanes = slice(part * HEAD, (part + 1) * HEAD)
+                        extra_ref[:, pl.ds(place, 1)] = row[:, None, lanes]
+        return carry
+
+    lax.fori_loop(0, YS // together, one_step, 0)
     if with_extra:
         for side, out_ref in ((1 - core, send_ref), (core, keep_ref)):
             for slot in range(YS):
@@ -145,17 +155,17 @@
                 out_ref[slot, rows:] = jnp.concatenate(blocks, axis=0)
 
 
-def project(tok_rows, requests, pieces, weights, more=None):
+def project(tok_rows, requests, parts, pieces, weights, more=None):
     rows = pieces.shape[0] * tok_rows
-    parts = weights[0].shape[0]
     extra = 0 if more is None else 3 * GROUP * requests
     out = bf16(YS, rows + extra, parts * HEAD)
     kept = jax.ShapeDtypeStruct((GROUP, parts * GROUP * requests, HEAD), jnp.float32)
     return in_vmem(
-        functools.partial(project_kernel, more is not None, tok_rows),
+        functools.partial(project_kernel, more is not None, tok_rows, parts),
         (out, out, kept),
         [],
         [pieces, *weights] + ([] if more is None else [more]),
+        loaded=range(1, 1 + len(weights)),
     )
 
 
@@ -216,8 +226,10 @@
     key_pos = jnp.concatenate([own_pos, last_pos, old_pos], axis=1)
     prior_keys = jnp.concatenate([ref[:, 0].reshape(old, HEAD) for ref in prior_refs], axis=0)
     prior_values = jnp.concatenate([ref[:, 1].reshape(old, HEAD) for ref in prior_refs], axis=0)
-    for step in range(rows // count):
-        queries = query_ref[step * count : (step + 1) * count]
+
+    def one_step(step, carry):
+        place = pl.ds(pl.multiple_of(step * count, count), count)
+        queries = query_ref[place]
         row = step * count + lax.broadcasted_iota(jnp.int32, (count, 1), 0)
         query_pos = start + odd * half + local(row)
         scores = jnp.concatenate(
@@ -239,7 +251,10 @@
             + product(weights[:, rows : 2 * rows], last_ref[:, HEAD:])
             + product(weights[:, 2 * rows :], prior_values)
         )
-        out_ref[step * count : (step + 1) * count] = (weighted / totals).astype(jnp.bfloat16)
+        out_ref[place] = (weighted / totals).astype(jnp.bfloat16)
+        return carry
+
+    lax.fori_loop(0, rows // count, one_step, 0)
 
 
 def decode_kernel(len_ref, sums_ref, bias_ref, cache_ref, out_ref):
@@ -295,7 +310,7 @@
         out_specs=pl.BlockSpec((1, GROUP, HEAD), lambda r: (r, 0, 0)),
         compiler_params=pltpu.CompilerParams(vmem_limit_bytes=2 * SMALL_VMEM),
         name="decode",
-    )(lengths, sums, bias, cache)
+    )(lengths, sums, bias, pltpu.with_memory_space_constraint(cache, pltpu.HBM))
 
 
 def pack_kernel(prefill_ref, decode_ref, out_ref):
@@ -343,9 +358,13 @@
             first = (block * GROUP + member) * piece
             row_ref[:, first : first + piece] = total[:, block * piece : (block + 1) * piece]
     result = hid_ref[...].astype(jnp.float32) + row_ref[...] + bias_ref[...]
-    result = result.astype(jnp.bfloat16)
-    for target in range(ZS):
-        out_ref[target] = result
+    out_ref[...] = result.astype(jnp.bfloat16)
+
+
+def place_kernel(*refs):
+    part_refs, out_ref = refs[:-1], refs[-1]
+    for step, ref in zip((0, 7, 1, 6, 2, 5, 3, 4), part_refs):
+        out_ref[lax.rem(lax.axis_index("z") + step, ZS)] = ref[...]
 
 
 def on_device(
@@ -371,17 +390,24 @@
     rows = GROUP * tok_rows
     half = w_qkv.shape[0] // 2
 
+    def near(value):
+        left = lax.ppermute(value, "x", shift(XS, 1))
+        return left, lax.ppermute(value, "x", shift(XS, -1))
+
     turned = w_qkv.transpose(1, 0, 2)
-    kv_own, q_own = turned[1:], turned[:1]
-    kv_left = lax.ppermute(kv_own, "x", shift(XS, 1))
-    kv_right = lax.ppermute(kv_own, "x", shift(XS, -1))
-    kv_left, kv_right, q_own = lax.optimization_barrier((kv_left, kv_right, q_own))
-    kv_far_a = lax.ppermute(kv_left[:, :half], "x", shift(XS, 1))
-    kv_far_b = lax.ppermute(kv_right[:, half:], "x", shift(XS, -1))
-    q_left = lax.ppermute(q_own, "x", shift(XS, 1))
-    q_right = lax.ppermute(q_own, "x", shift(XS, -1))
-    q_far_a = lax.ppermute(q_left[:, :half], "x", shift(XS, 1))
-    q_far_b = lax.ppermute(q_right[:, half:], "x", shift(XS, -1))
+    k_own, v_own = turned[1], turned[2]
+    k_left, k_right = near(k_own)
+    v_left, v_right = near(v_own)
+    k_far = lax.ppermute(k_left, "x", shift(XS, 1))
+    v_far = lax.ppermute(v_right, "x", shift(XS, -1))
+    q_own = turned[0]
+    v_left, v_right, q_own = lax.optimization_barrier((v_left, v_right, q_own))
+    q_left, q_right = near(q_own)
+    q_fars = (
+        lax.ppermute(q_left[:half], "x", shift(XS, 1)),
+        lax.ppermute(q_right[half:], "x", shift(XS, -1)),
+    )
+    kv_weights = (k_own, v_own, k_left, v_left, k_right, v_right, k_far, v_far)
 
     pieces = in_vmem(
         norm_kernel,
@@ -399,17 +425,18 @@
     )
 
     kv_send, kv_keep, kv_extra = project(
-        tok_rows, dec_dev, pieces, (kv_own, kv_left, kv_right, kv_far_a, kv_far_b)
+        tok_rows, dec_dev, 2, pieces, kv_weights
     )
     kv_parts = reduce_partial(kv_send, kv_keep)
     own_kv = in_vmem(finish_kv_kernel, bf16(rows, 2 * HEAD), [], [kv_parts, qkv_bias])
     last_kv = lax.ppermute(own_kv, "x", [(0, 1), (2, 3)])
 
-    q_far_a, q_far_b, w_out = lax.optimization_barrier((q_far_a, q_far_b, w_out))
+    q_weights = (q_own, q_left, q_right, *q_fars)
     q_send, q_keep, _ = project(
-        tok_rows, dec_dev, pieces, (q_own, q_left, q_right, q_far_a, q_far_b), kv_extra
+        tok_rows, dec_dev, 1, pieces, q_weights, kv_extra
     )
     q_parts = reduce_partial(q_send, q_keep)
+    last_kv, w_out = lax.optimization_barrier((last_kv, w_out))
     w_own = w_out.T
     w_left = lax.ppermute(w_own, "x", shift(XS, 1))
     w_right = lax.ppermute(w_own, "x", shift(XS, -1))
@@ -461,12 +488,21 @@
     residual = lax.dynamic_slice(hidden, (me_z * slab, 0), (slab, width))
     result = in_vmem(
         final_kernel,
-        bf16(ZS, slab, width),
+        bf16(slab, width),
         [],
         [shares, residual, out_bias[None]],
         [pltpu.VMEM((slab, width), jnp.float32)],
     )
-    result = lax.all_to_all(result, "z", 0, 0, tiled=True).reshape(tok_rows, width)
+    everyone = [result]
+    up = down = result
+    for step in range(ZS // 2):
+        up = lax.ppermute(up, "z", shift(ZS, 1))
+        everyone.append(up)
+        if step < ZS // 2 - 1:
+            down = lax.ppermute(down, "z", shift(ZS, -1))
+            everyone.append(down)
+    result = in_vmem(place_kernel, bf16(ZS, slab, width), [], everyone)
+    result = result.reshape(tok_rows, width)
     return (result, new_kv)
 
 

time: 207 us -> 201 us (0.971)
  waiting for transfers between devices: 106 us -> 95 us
  starting transfers between devices: 61 us -> 64.4 us
  Pallas kernels: 24.7 us -> 27.6 us
    all_to_all x1 -> x0, waiting for transfers between devices: 25.2 us -> none  [on_device(): lax.all_to_all(result, 'z', 0, 0, tiled=True).reshape(tok_rows, width)]
    ppermute x8 -> x17, waiting for transfers between devices: 26.6 us -> 47.2 us  [the longest x3 13.7 us: near(): left = lax.ppermute(value, 'x', shift(XS, 1))]
    ppermute x8 -> x17, starting transfers between devices: 8.62 us -> 21.2 us  [the longest x3 7.61 us: on_device(): down = lax.ppermute(down, 'z', shift(ZS, -1))]
    slice x6 -> x2, local copies, waits for them, and re-layouts: 5.86 us -> 0.03 us  [the longest x1 0.02 us: on_device(): q_right[half:]]
    ppermute x1, waiting for transfers between devices: 0.01 us -> 4.79 us  [on_device(): last_kv = lax.ppermute(own_kv, 'x', [(0, 1), (2, 3)])]
    ppermute x1, waiting for transfers between devices: 11 us -> 6.6 us  [on_device(): lax.ppermute(prior[1], 'x', shift(XS, 1))]
    ppermute x1, waiting for transfers between devices: 4.26 us -> 0.01 us  [on_device(): lax.ppermute(prior[2], 'x', shift(XS, -1))]
    all_to_all x1 -> x0, starting transfers between devices: 4.2 us -> none  [on_device(): lax.all_to_all(result, 'z', 0, 0, tiled=True).reshape(tok_rows, width)]
  transfers between devices with their start and end apart: 30 -> 38, of which waited for: 21 -> 22; matrix products, arithmetic and copies ran while one was open for 3% -> 3% of each run, Pallas kernels for 8% -> 8%
where the time goes in v2:
time: 201 us; the launch traced here: 199 us
  waiting for transfers between devices  95 us (47%)
  starting transfers between devices  64.4 us (32%)
  Pallas kernels  27.6 us (14%)
  local copies, waits for them, and re-layouts  11.1 us (6%)
    all_to_all x1, waiting for transfers between devices, on_device(): shares = lax.all_to_all(shares, ('y', 'c', 'z'), 0, 0, tiled=True)  24.9 us
    pallas_call x13, Pallas kernels, in_vmem(): pl.pallas_call(kernel, out_shape=out_shape, in_specs=[pl.BlockSpec(memory...  21.7 us
    ppermute x3, waiting for transfers between devices, near(): left = lax.ppermute(value, 'x', shift(XS, 1))  13.7 us
    ppermute x4, waiting for transfers between devices, on_device(): up = lax.ppermute(up, 'z', shift(ZS, 1))  13.5 us
    all_to_all x1, starting transfers between devices, on_device(): shares = lax.all_to_all(shares, ('y', 'c', 'z'), 0, 0, tiled=True)  10.3 us
    all_to_all x2, starting transfers between devices, reduce_partial(): return lax.all_to_all(partial, 'y', 0, 0, tiled=True)  8.84 us
    ppermute x3, starting transfers between devices, on_device(): down = lax.ppermute(down, 'z', shift(ZS, -1))  7.61 us
    ppermute x1, waiting for transfers between devices, on_device(): k_far = lax.ppermute(k_left, 'x', shift(XS, 1))  6.65 us
  transfers between devices with their start and end apart: 38, of which 22 were waited for; matrix products, arithmetic and copies ran while one was open for 3% of the time, Pallas kernels for 8%

profile of v2, /device:TPU:2, one launch (start us, length us, event | category | flops | bytes accessed | tf_op | source)
XLA Modules:
  0.0 199.0 jit_solution(4157063724133526771)
XLA Ops:
  0.6 1.2 copy-done
  1.8 0.9 copy-done.5
  2.7 0.7 copy-done.6
  3.5 0.7 copy-done.7
  4.2 2.4 %shard_map.122 = bf16[8,4,80,224]{3,2,1,0:T(8,128)(2,1)} custom-call(bf16[64,7168]{1,0:T(8,128)(2,1)S(1)} %copy-done, f32[1,7168]{1,0:T(1,128)S(1)} %bitcast.21, f32[1,7168]{1,0:T(1,128)S(1)} %bitcast.22, bf16[16,2,2,896]{3,2,1,0:T(2,128)(2,1)S(1)} %copy-done.5), custom_call_target="tpu_custom_call" | custom-call | tf_op jit(solution)/shard_map/pallas_call | solution.py:31
  6.6 4.5 %all-to-all-start = ((bf16[8,4,80,224]{3,2,1,0:T(8,128)(2,1)}), bf16[8,4,80,224]{3,2,1,0:T(8,128)(2,1)S(1)}, u32[]{:S(2)}, u32[]{:S(2)}) async-start(bf16[8,4,80,224]{3,2,1,0:T(8,128)(2,1)} %shard_map.122), calls=%async_computation | async-start | bytes 2621440 | tf_op jit(solution)/shard_map/all_to_all | solution.py:418
  11.1 2.1 %slice_bitcast_fusion = (bf16[224,896]{1,0:T(8,128)(2,1)}, bf16[224,896]{1,0:T(8,128)(2,1)S(1)}, bf16[224,896]{1,0:T(8,128)(2,1)S(1)}) fusion(bf16[3,224,896]{2,1,0:T(8,128)(2,1)} %bitcast.24), kind=kLoop, calls=%fused_computation | loop fusion | bytes 2408448 | tf_op jit(solution)/shard_map/squeeze | solution.py:403
  13.2 1.5 collective-permute-start
  15.2 1.5 collective-permute-start.1
  16.7 1.1 collective-permute-start.3
  17.8 7.6 %collective-permute-done.refs_3_ = bf16[224,896]{1,0:T(8,128)(2,1)S(1)} collective-permute-done((bf16[224,896]{1,0:T(8,128)(2,1)S(1)}, bf16[224,896]{1,0:T(8,128)(2,1)S(1)}, u32[]{:S(2)}, u32[]{:S(2)}) %collective-permute-start) | collective-permute-done | bytes 401440 | tf_op jit(solution)/shard_map/ppermute | solution.py:394
  25.3 1.5 collective-permute-start.4
  26.8 1.2 collective-permute-start.5
  28.0 5.9 %collective-permute-done.1.refs_4_ = bf16[224,896]{1,0:T(8,128)(2,1)S(1)} collective-permute-done((bf16[224,896]{1,0:T(8,128)(2,1)S(1)}, bf16[224,896]{1,0:T(8,128)(2,1)S(1)}, u32[]{:S(2)}, u32[]{:S(2)}) %collective-permute-start.1) | collective-permute-done | bytes 401440 | tf_op jit(solution)/shard_map/ppermute | solution.py:394
  33.9 1.5 collective-permute-done.3.refs_5_
  35.4 6.6 %collective-permute-done.4.refs_7_ = bf16[224,896]{1,0:T(8,128)(2,1)S(1)} collective-permute-done((bf16[224,896]{1,0:T(8,128)(2,1)S(1)}, bf16[224,896]{1,0:T(8,128)(2,1)S(1)}, u32[]{:S(2)}, u32[]{:S(2)}) %collective-permute-start.4) | collective-permute-done | bytes 401440 | tf_op jit(solution)/shard_map/ppermute | solution.py:401
  42.1 0.8 copy-done.19
  43.4 4.8 %shard_map.123 = (bf16[4,512,256]{2,1,0:T(8,128)(2,1)S(1)}, bf16[4,512,256]{2,1,0:T(8,128)(2,1)S(1)}, f32[8,32,128]{2,1,0:T(8,128)S(1)}) custom-call(bf16[8,4,80,224]{3,2,1,0:T(8,128)(2,1)S(1)} %all-to-all-done.refs_0_.in_ref, bf16[224,896]{1,0:T(8,128)(2,1)} %copy-done.12, bf16[224,896]{1,0:T(8,128)(2,1)} %copy-done.11, bf16[224,896]{1,0:T(8,128)(2,1)} %copy-done.15, ...), custom_call_target="tpu_custom_call" | custom-call | tf_op jit(solution)/shard_map/pallas_call | solution.py:31
  48.3 2.0 %collective-permute-start.8 = (bf16[224,896]{1,0:T(8,128)(2,1)}, bf16[224,896]{1,0:T(8,128)(2,1)S(1)}, u32[]{:S(2)}, u32[]{:S(2)}) collective-permute-start(bf16[224,896]{1,0:T(8,128)(2,1)} %get-tuple-element.31.refs_1_), channel_id=1, source_target_pairs={{0,192},{64,0},{128,64},{192,128},{1,193},{65,1},{129,65},{193,129... | collective-permute-start | bytes 1204232 | tf_op jit(solution)/shard_map/ppermute | solution.py:395
  51.0 1.3 shard_map.124
  52.2 4.4 %all-to-all-start.1 = ((bf16[4,512,256]{2,1,0:T(8,128)(2,1)}), bf16[4,512,256]{2,1,0:T(8,128)(2,1)S(1)}, u32[]{:S(2)}, u32[]{:S(2)}) async-start(bf16[4,512,256]{2,1,0:T(8,128)(2,1)} %shard_map.124), calls=%async_computation.1 | async-start | bytes 2097152 | tf_op jit(solution)/shard_map/all_to_all | solution.py:180
  56.6 3.6 %collective-permute-done.8.refs_3_ = bf16[224,896]{1,0:T(8,128)(2,1)S(1)} collective-permute-done((bf16[224,896]{1,0:T(8,128)(2,1)}, bf16[224,896]{1,0:T(8,128)(2,1)S(1)}, u32[]{:S(2)}, u32[]{:S(2)}) %collective-permute-start.8) | collective-permute-done | bytes 401440 | tf_op jit(solution)/shard_map/ppermute | solution.py:395
  60.2 2.0 %collective-permute-start.10 = (bf16[112,896]{1,0:T(8,128)(2,1)S(1)}, bf16[112,896]{1,0:T(8,128)(2,1)S(1)}, u32[]{:S(2)}, u32[]{:S(2)}) collective-permute-start(bf16[112,896]{1,0:T(8,128)(2,1)S(1)} %slice.28), channel_id=1, source_target_pairs={{0,192},{64,0},{128,64},{192,128},{1,193},{65,1},{129,65},{193,129... | collective-permute-start | bytes 602120 | tf_op jit(solution)/shard_map/ppermute | solution.py:408
  62.5 4.6 %collective-permute-done.10.refs_5_ = bf16[112,896]{1,0:T(8,128)(2,1)S(1)} collective-permute-done((bf16[112,896]{1,0:T(8,128)(2,1)S(1)}, bf16[112,896]{1,0:T(8,128)(2,1)S(1)}, u32[]{:S(2)}, u32[]{:S(2)}) %collective-permute-start.10) | collective-permute-done | bytes 200736 | tf_op jit(solution)/shard_map/ppermute | solution.py:408
  67.2 3.1 %collective-permute-done.9.refs_4_ = bf16[112,896]{1,0:T(8,128)(2,1)S(1)} collective-permute-done((bf16[112,896]{1,0:T(8,128)(2,1)S(1)}, bf16[112,896]{1,0:T(8,128)(2,1)S(1)}, u32[]{:S(2)}, u32[]{:S(2)}) %collective-permute-start.9) | collective-permute-done | bytes 200736 | tf_op jit(solution)/shard_map/ppermute | solution.py:407
  70.3 0.7 copy-done.21
  71.0 3.8 %shard_map.126 = (bf16[4,560,128]{2,1,0:T(8,128)(2,1)}, bf16[4,560,128]{2,1,0:T(8,128)(2,1)S(1)}, f32[8,16,128]{2,1,0:T(8,128)}) custom-call(bf16[8,4,80,224]{3,2,1,0:T(8,128)(2,1)S(1)} %all-to-all-done.refs_0_.in_ref, bf16[224,896]{1,0:T(8,128)(2,1)} %get-tuple-element.31.refs_1_, bf16[224,896]{1,0:T(8,128)(2,1)} %copy-done.14, ...), custom_call_target="tpu_custom_call" | custom-call | tf_op jit(solution)/shard_map/pallas_call | solution.py:31
  74.8 0.8 shard_map.125.own_ref
  75.6 1.3 collective-permute-start.12
  76.9 0.9 shard_map.127
  77.9 4.4 %all-to-all-start.2 = ((bf16[4,560,128]{2,1,0:T(8,128)(2,1)}), bf16[4,560,128]{2,1,0:T(8,128)(2,1)S(1)}, u32[]{:S(2)}, u32[]{:S(2)}) async-start(bf16[4,560,128]{2,1,0:T(8,128)(2,1)} %shard_map.127), calls=%async_computation.2 | async-start | bytes 1146880 | tf_op jit(solution)/shard_map/all_to_all | solution.py:180
  82.3 4.8 %collective-permute-done.12.last_ref = bf16[512,256]{1,0:T(8,128)(2,1)} collective-permute-done((bf16[512,256]{1,0:T(8,128)(2,1)}, bf16[512,256]{1,0:T(8,128)(2,1)}, u32[]{:S(2)}, u32[]{:S(2)}) %collective-permute-start.12) | collective-permute-done | bytes 262176 | tf_op jit(solution)/shard_map/ppermute | solution.py:432
  87.1 2.0 %collective-permute-start.17 = (bf16[224,896]{1,0:T(8,128)(2,1)S(1)}, bf16[224,896]{1,0:T(8,128)(2,1)S(1)}, u32[]{:S(2)}, u32[]{:S(2)}) collective-permute-start(bf16[224,896]{1,0:T(8,128)(2,1)S(1)} %bitcast.18), channel_id=1, source_target_pairs={{0,192},{64,0},{128,64},{192,128},{1,193},{65,1},{129,65},{193,129... | collective-permute-start | bytes 1204232 | tf_op jit(solution)/shard_map/ppermute | solution.py:442
  89.1 1.4 collective-permute-start.18
  90.6 2.4 %all-to-all-done.2.partial_ref = bf16[4,560,128]{2,1,0:T(8,128)(2,1)S(1)} async-done(((bf16[4,560,128]{2,1,0:T(8,128)(2,1)}), bf16[4,560,128]{2,1,0:T(8,128)(2,1)S(1)}, u32[]{:S(2)}, u32[]{:S(2)}) %all-to-all-start.2) | async-done | bytes 573472 | tf_op jit(solution)/shard_map/all_to_all | solution.py:180
  93.0 0.6 copy-done.2
  93.7 4.0 %all-to-all-start.3 = ((bf16[8,64,256]{2,1,0:T(8,128)(2,1)}), bf16[8,64,256]{2,1,0:T(8,128)(2,1)}, u32[]{:S(2)}, u32[]{:S(2)}) async-start(bf16[8,64,256]{2,1,0:T(8,128)(2,1)} %bitcast.6), calls=%async_computation.3 | async-start | bytes 524288 | tf_op jit(solution)/shard_map/all_to_all | solution.py:455
  97.9 3.7 %collective-permute-start.13 = (bf16[8,2,16,128]{3,2,1,0:T(8,128)(2,1)S(1)}, bf16[8,2,16,128]{3,2,1,0:T(8,128)(2,1)S(1)}, u32[]{:S(2)}, u32[]{:S(2)}) collective-permute-start(bf16[8,2,16,128]{3,2,1,0:T(8,128)(2,1)S(1)} %get-tuple-element.39), channel_id=1, source_target_pairs={{0,64},{64,128},{128,192},{192,0},{1,65},{65,129},{129,193},{193,1... | collective-permute-start | bytes 196616 | tf_op jit(solution)/shard_map/ppermute | solution.py:422
  101.7 6.6 %collective-permute-done.13.refs_1_ = bf16[8,2,16,128]{3,2,1,0:T(8,128)(2,1)S(1)} collective-permute-done((bf16[8,2,16,128]{3,2,1,0:T(8,128)(2,1)S(1)}, bf16[8,2,16,128]{3,2,1,0:T(8,128)(2,1)S(1)}, u32[]{:S(2)}, u32[]{:S(2)}) %collective-permute-start.13) | collective-permute-done | bytes 65568 | tf_op jit(solution)/shard_map/ppermute | solution.py:422
  108.3 1.1 collective-permute-start.15
  109.4 1.0 slice.29
  110.9 3.1 %collective-permute-done.15.refs_3_ = bf16[8,2,16,128]{3,2,1,0:T(8,128)(2,1)S(1)} collective-permute-done((bf16[8,2,16,128]{3,2,1,0:T(8,128)(2,1)S(1)}, bf16[8,2,16,128]{3,2,1,0:T(8,128)(2,1)S(1)}, u32[]{:S(2)}, u32[]{:S(2)}) %collective-permute-start.15) | collective-permute-done | bytes 65568 | tf_op jit(solution)/shard_map/ppermute | solution.py:424
  114.0 3.9 %shard_map.130.prefill_ref = bf16[512,128]{1,0:T(8,128)(2,1)S(1)} custom-call(s32[2]{0:T(128)S(1)} %copy-done.9, bf16[512,128]{1,0:T(8,128)(2,1)S(1)} %copy-done.3, bf16[512,256]{1,0:T(8,128)(2,1)} %shard_map.125.own_ref, bf16[512,256]{1,0:T(8,128)(2,1)} %collective-permute-done.12.last_ref, bf16[8,2,16,128]{3,2,1,0:T(8,128)(2,1)S(1)} %get-tuple-element.38.refs_0_, ...), custom_call_target="tpu_custom_call" | custom-call | tf_op jit(solution)/shard_map/pallas_call | solution.py:31
  117.9 5.9 %decode.1.decode_ref = f32[2,8,128]{2,1,0:T(8,128)S(1)} custom-call(s32[2]{0:T(128)S(1)} %copy-done.10, f32[48,128]{1,0:T(8,128)S(1)} %get-tuple-element.44.sums_ref, f32[3,8,128]{2,1,0:T(8,128)S(1)} %pad.4.bias_ref, bf16[2,1024,2,896]{3,2,1,0:T(2,128)(2,1)} %cache_ref.1), custom_call_target="tpu_custom_call" | custom-call | tf_op jit(solution)/shard_map/decode/pallas_call | solution.py:300
  123.9 1.7 collective-permute-start.19
  125.6 1.6 collective-permute-start.20
  127.2 2.0 collective-permute-start.21
  129.2 2.4 %collective-permute-done.19.refs_1_ = bf16[528,128]{1,0:T(8,128)(2,1)S(1)} collective-permute-done((bf16[528,128]{1,0:T(8,128)(2,1)S(1)}, bf16[528,128]{1,0:T(8,128)(2,1)S(1)}, u32[]{:S(2)}, u32[]{:S(2)}) %collective-permute-start.19) | collective-permute-done | bytes 135200 | tf_op jit(solution)/shard_map/ppermute | solution.py:471
  132.1 1.6 collective-permute-done.21.refs_3_
  133.7 1.3 collective-permute-done.25.refs_7_
  135.1 2.4 %shard_map.132 = bf16[512,896]{1,0:T(8,128)(2,1)} custom-call(bf16[528,128]{1,0:T(8,128)(2,1)S(1)} %shard_map.131.refs_0_, bf16[528,128]{1,0:T(8,128)(2,1)S(1)} %collective-permute-done.19.refs_1_, bf16[528,128]{1,0:T(8,128)(2,1)S(1)} %collective-permute-done.20.refs_2_, bf16[528,128]{1,0:T(8,128)(2,1)S(1)} %collective-permute-done.21.refs_3_, ...), custom_call_target="tpu_custom_call" | custom-call | tf_op jit(solution)/shard_map/pallas_call | solution.py:31
  137.5 10.3 %all-to-all-start.4 = ((bf16[64,8,896]{2,1,0:T(8,128)(2,1)}), bf16[64,8,896]{2,1,0:T(8,128)(2,1)S(1)}, u32[]{:S(2)}, u32[]{:S(2)}) async-start(bf16[64,8,896]{2,1,0:T(8,128)(2,1)} %bitcast.9), calls=%async_computation.4 | async-start | bytes 1835008 | tf_op jit(solution)/shard_map/all_to_all | solution.py:487
  147.8 0.9 constant_dynamic-slice_fusion.hid_ref
  148.7 24.9 %all-to-all-done.4.in_ref = bf16[64,8,896]{2,1,0:T(8,128)(2,1)S(1)} async-done(((bf16[64,8,896]{2,1,0:T(8,128)(2,1)}), bf16[64,8,896]{2,1,0:T(8,128)(2,1)S(1)}, u32[]{:S(2)}, u32[]{:S(2)}) %all-to-all-start.4) | async-done | bytes 917536 | tf_op jit(solution)/shard_map/all_to_all | solution.py:487
  173.8 1.7 collective-permute-start.26
  175.5 1.6 collective-permute-start.27
  177.1 2.8 %collective-permute-done.26.refs_1_ = bf16[8,7168]{1,0:T(8,128)(2,1)S(1)} collective-permute-done((bf16[8,7168]{1,0:T(8,128)(2,1)S(1)}, bf16[8,7168]{1,0:T(8,128)(2,1)S(1)}, u32[]{:S(2)}, u32[]{:S(2)}) %collective-permute-start.26) | collective-permute-done | bytes 114720 | tf_op jit(solution)/shard_map/ppermute | solution.py:499
  180.3 2.8 %collective-permute-start.29 = (bf16[8,7168]{1,0:T(8,128)(2,1)S(1)}, bf16[8,7168]{1,0:T(8,128)(2,1)S(1)}, u32[]{:S(2)}, u32[]{:S(2)}) collective-permute-start(bf16[8,7168]{1,0:T(8,128)(2,1)S(1)} %collective-permute-done.27.refs_2_), channel_id=1, source_target_pairs={{0,7},{1,0},{2,1},{3,2},{4,3},{5,4},{6,5},{7,6},{8,15},{9,8},{10,9... | collective-permute-start | bytes 344072 | tf_op jit(solution)/shard_map/ppermute | solution.py:502
  183.1 2.8 %collective-permute-done.28.refs_3_ = bf16[8,7168]{1,0:T(8,128)(2,1)S(1)} collective-permute-done((bf16[8,7168]{1,0:T(8,128)(2,1)S(1)}, bf16[8,7168]{1,0:T(8,128)(2,1)S(1)}, u32[]{:S(2)}, u32[]{:S(2)}) %collective-permute-start.28) | collective-permute-done | bytes 114720 | tf_op jit(solution)/shard_map/ppermute | solution.py:499
  185.9 3.2 %collective-permute-start.31 = (bf16[8,7168]{1,0:T(8,128)(2,1)S(1)}, bf16[8,7168]{1,0:T(8,128)(2,1)S(1)}, u32[]{:S(2)}, u32[]{:S(2)}) collective-permute-start(bf16[8,7168]{1,0:T(8,128)(2,1)S(1)} %collective-permute-done.29.refs_4_), channel_id=1, source_target_pairs={{0,7},{1,0},{2,1},{3,2},{4,3},{5,4},{6,5},{7,6},{8,15},{9,8},{10,9... | collective-permute-start | bytes 344072 | tf_op jit(solution)/shard_map/ppermute | solution.py:502
  189.1 2.9 %collective-permute-done.30.refs_5_ = bf16[8,7168]{1,0:T(8,128)(2,1)S(1)} collective-permute-done((bf16[8,7168]{1,0:T(8,128)(2,1)S(1)}, bf16[8,7168]{1,0:T(8,128)(2,1)S(1)}, u32[]{:S(2)}, u32[]{:S(2)}) %collective-permute-start.30) | collective-permute-done | bytes 114720 | tf_op jit(solution)/shard_map/ppermute | solution.py:499
  192.0 0.9 copy.16
  192.9 5.1 %collective-permute-done.32.refs_7_ = bf16[8,7168]{1,0:T(8,128)(2,1)S(1)} collective-permute-done((bf16[8,7168]{1,0:T(8,128)(2,1)S(1)}, bf16[8,7168]{1,0:T(8,128)(2,1)S(1)}, u32[]{:S(2)}, u32[]{:S(2)}) %collective-permute-start.32) | collective-permute-done | bytes 114720 | tf_op jit(solution)/shard_map/ppermute | solution.py:499
  198.0 1.0 shard_map.134
  (81 shorter events, 4.3 us)
Async XLA Ops:
  0.6 1.2 copy-start
  1.8 0.9 copy-start.5
  2.7 0.7 copy-start.6
  3.5 0.7 copy-start.7
  6.6 36.8 %all-to-all-start = ((bf16[8,4,80,224]{3,2,1,0:T(8,128)(2,1)}), bf16[8,4,80,224]{3,2,1,0:T(8,128)(2,1)S(1)}, u32[]{:S(2)}, u32[]{:S(2)}) async-start(bf16[8,4,80,224]{3,2,1,0:T(8,128)(2,1)} %shard_map.122), calls=%async_computation | async-start | bytes 2621440 | tf_op jit(solution)/shard_map/all_to_all | solution.py:418
  13.2 30.2 %copy-start.11 = (bf16[224,896]{1,0:T(8,128)(2,1)}, bf16[224,896]{1,0:T(8,128)(2,1)S(1)}, u32[]{:S(2)}) copy-start(bf16[224,896]{1,0:T(8,128)(2,1)S(1)} %get-tuple-element.57.refs_2_) | copy-start | bytes 1204228
  13.2 30.2 %copy-start.12 = (bf16[224,896]{1,0:T(8,128)(2,1)}, bf16[224,896]{1,0:T(8,128)(2,1)S(1)}, u32[]{:S(2)}) copy-start(bf16[224,896]{1,0:T(8,128)(2,1)S(1)} %get-tuple-element.58.refs_1_) | copy-start | bytes 1204228
  13.2 12.2 %collective-permute-start = (bf16[224,896]{1,0:T(8,128)(2,1)S(1)}, bf16[224,896]{1,0:T(8,128)(2,1)S(1)}, u32[]{:S(2)}, u32[]{:S(2)}) collective-permute-start(bf16[224,896]{1,0:T(8,128)(2,1)S(1)} %get-tuple-element.58.refs_1_), channel_id=1, source_target_pairs={{0,64},{64,128},{128,192},{192,0},{1,65},{65,129},{129,193},{193,1... | collective-permute-start | bytes 1204232 | tf_op jit(solution)/shard_map/ppermute | solution.py:394
  14.7 12.2 %collective-permute-start.2 = (bf16[224,896]{1,0:T(8,128)(2,1)S(1)}, bf16[224,896]{1,0:T(8,128)(2,1)S(1)}, u32[]{:S(2)}, u32[]{:S(2)}) collective-permute-start(bf16[224,896]{1,0:T(8,128)(2,1)S(1)} %get-tuple-element.57.refs_2_), channel_id=1, source_target_pairs={{0,192},{64,0},{128,64},{192,128},{1,193},{65,1},{129,65},{193,129... | collective-permute-start | bytes 1204232 | tf_op jit(solution)/shard_map/ppermute | solution.py:395
  15.2 18.7 %collective-permute-start.1 = (bf16[224,896]{1,0:T(8,128)(2,1)S(1)}, bf16[224,896]{1,0:T(8,128)(2,1)S(1)}, u32[]{:S(2)}, u32[]{:S(2)}) collective-permute-start(bf16[224,896]{1,0:T(8,128)(2,1)S(1)} %get-tuple-element.57.refs_2_), channel_id=1, source_target_pairs={{0,64},{64,128},{128,192},{192,0},{1,65},{65,129},{129,193},{193,1... | collective-permute-start | bytes 1204232 | tf_op jit(solution)/shard_map/ppermute | solution.py:394
  16.7 18.7 %collective-permute-start.3 = (bf16[224,896]{1,0:T(8,128)(2,1)S(1)}, bf16[224,896]{1,0:T(8,128)(2,1)S(1)}, u32[]{:S(2)}, u32[]{:S(2)}) collective-permute-start(bf16[224,896]{1,0:T(8,128)(2,1)S(1)} %get-tuple-element.58.refs_1_), channel_id=1, source_target_pairs={{0,192},{64,0},{128,64},{192,128},{1,193},{65,1},{129,65},{193,129... | collective-permute-start | bytes 1204232 | tf_op jit(solution)/shard_map/ppermute | solution.py:395
  25.3 18.1 %copy-start.15 = (bf16[224,896]{1,0:T(8,128)(2,1)}, bf16[224,896]{1,0:T(8,128)(2,1)S(1)}, u32[]{:S(2)}) copy-start(bf16[224,896]{1,0:T(8,128)(2,1)S(1)} %collective-permute-done.refs_3_) | copy-start | bytes 1204228
  25.3 16.7 %collective-permute-start.4 = (bf16[224,896]{1,0:T(8,128)(2,1)S(1)}, bf16[224,896]{1,0:T(8,128)(2,1)S(1)}, u32[]{:S(2)}, u32[]{:S(2)}) collective-permute-start(bf16[224,896]{1,0:T(8,128)(2,1)S(1)} %collective-permute-done.refs_3_), channel_id=1, source_target_pairs={{0,64},{64,128},{128,192},{192,0},{1,65},{65,129},{129,193},{193,1... | collective-permute-start | bytes 1204232 | tf_op jit(solution)/shard_map/ppermute | solution.py:401
  26.8 16.6 %copy-start.16 = (bf16[224,896]{1,0:T(8,128)(2,1)}, bf16[224,896]{1,0:T(8,128)(2,1)S(1)}, u32[]{:S(2)}) copy-start(bf16[224,896]{1,0:T(8,128)(2,1)S(1)} %collective-permute-done.2.refs_6_) | copy-start | bytes 1204228
  26.8 16.6 %collective-permute-start.5 = (bf16[224,896]{1,0:T(8,128)(2,1)S(1)}, bf16[224,896]{1,0:T(8,128)(2,1)}, u32[]{:S(2)}, u32[]{:S(2)}) collective-permute-start(bf16[224,896]{1,0:T(8,128)(2,1)S(1)} %collective-permute-done.2.refs_6_), channel_id=1, source_target_pairs={{0,192},{64,0},{128,64},{192,128},{1,193},{65,1},{129,65},{193,129... | collective-permute-start | bytes 1204232 | tf_op jit(solution)/shard_map/ppermute | solution.py:402
  33.9 8.1 %copy-start.17 = (bf16[224,896]{1,0:T(8,128)(2,1)}, bf16[224,896]{1,0:T(8,128)(2,1)S(1)}, u32[]{:S(2)}) copy-start(bf16[224,896]{1,0:T(8,128)(2,1)S(1)} %collective-permute-done.1.refs_4_) | copy-start | bytes 1204228
  35.4 6.7 %copy-start.18 = (bf16[224,896]{1,0:T(8,128)(2,1)}, bf16[224,896]{1,0:T(8,128)(2,1)S(1)}, u32[]{:S(2)}) copy-start(bf16[224,896]{1,0:T(8,128)(2,1)S(1)} %collective-permute-done.3.refs_5_) | copy-start | bytes 1204228
  42.1 0.8 copy-start.19
  48.2 2.7 %collective-permute-start.6 = (bf16[4,512,256]{2,1,0:T(8,128)(2,1)S(1)}, bf16[4,512,256]{2,1,0:T(8,128)(2,1)S(1)}, u32[]{:S(2)}, u32[]{:S(2)}) collective-permute-start(bf16[4,512,256]{2,1,0:T(8,128)(2,1)S(1)} %get-tuple-element.30), channel_id=1, source_target_pairs={{0,8},{8,0},{1,9},{9,1},{2,10},{10,2},{3,11},{11,3},{4,12},{12,4},... | collective-permute-start | bytes 3145736 | tf_op jit(solution)/shard_map/ppermute | solution.py:178
  48.3 11.9 %collective-permute-start.8 = (bf16[224,896]{1,0:T(8,128)(2,1)}, bf16[224,896]{1,0:T(8,128)(2,1)S(1)}, u32[]{:S(2)}, u32[]{:S(2)}) collective-permute-start(bf16[224,896]{1,0:T(8,128)(2,1)} %get-tuple-element.31.refs_1_), channel_id=1, source_target_pairs={{0,192},{64,0},{128,64},{192,128},{1,193},{65,1},{129,65},{193,129... | collective-permute-start | bytes 1204232 | tf_op jit(solution)/shard_map/ppermute | solution.py:395
  50.3 12.1 %collective-permute-start.7 = (bf16[224,896]{1,0:T(8,128)(2,1)}, bf16[224,896]{1,0:T(8,128)(2,1)S(1)}, u32[]{:S(2)}, u32[]{:S(2)}) collective-permute-start(bf16[224,896]{1,0:T(8,128)(2,1)} %get-tuple-element.31.refs_1_), channel_id=1, source_target_pairs={{0,64},{64,128},{128,192},{192,0},{1,65},{65,129},{129,193},{193,1... | collective-permute-start | bytes 1204232 | tf_op jit(solution)/shard_map/ppermute | solution.py:394
  52.2 22.5 %all-to-all-start.1 = ((bf16[4,512,256]{2,1,0:T(8,128)(2,1)}), bf16[4,512,256]{2,1,0:T(8,128)(2,1)S(1)}, u32[]{:S(2)}, u32[]{:S(2)}) async-start(bf16[4,512,256]{2,1,0:T(8,128)(2,1)} %shard_map.124), calls=%async_computation.1 | async-start | bytes 2097152 | tf_op jit(solution)/shard_map/all_to_all | solution.py:180
  60.2 10.1 %copy-start.13 = (bf16[224,896]{1,0:T(8,128)(2,1)}, bf16[224,896]{1,0:T(8,128)(2,1)S(1)}, u32[]{:S(2)}) copy-start(bf16[224,896]{1,0:T(8,128)(2,1)S(1)} %collective-permute-done.8.refs_3_) | copy-start | bytes 1204228
  60.2 6.9 %collective-permute-start.10 = (bf16[112,896]{1,0:T(8,128)(2,1)S(1)}, bf16[112,896]{1,0:T(8,128)(2,1)S(1)}, u32[]{:S(2)}, u32[]{:S(2)}) collective-permute-start(bf16[112,896]{1,0:T(8,128)(2,1)S(1)} %slice.28), channel_id=1, source_target_pairs={{0,192},{64,0},{128,64},{192,128},{1,193},{65,1},{129,65},{193,129... | collective-permute-start | bytes 602120 | tf_op jit(solution)/shard_map/ppermute | solution.py:408
  62.4 7.8 %copy-start.14 = (bf16[224,896]{1,0:T(8,128)(2,1)}, bf16[224,896]{1,0:T(8,128)(2,1)S(1)}, u32[]{:S(2)}) copy-start(bf16[224,896]{1,0:T(8,128)(2,1)S(1)} %collective-permute-done.7.refs_2_) | copy-start | bytes 1204228
  62.5 7.8 %collective-permute-start.9 = (bf16[112,896]{1,0:T(8,128)(2,1)S(1)}, bf16[112,896]{1,0:T(8,128)(2,1)S(1)}, u32[]{:S(2)}, u32[]{:S(2)}) collective-permute-start(bf16[112,896]{1,0:T(8,128)(2,1)S(1)} %slice.27), channel_id=1, source_target_pairs={{0,64},{64,128},{128,192},{192,0},{1,65},{65,129},{129,193},{193,1... | collective-permute-start | bytes 602120 | tf_op jit(solution)/shard_map/ppermute | solution.py:407
  67.2 3.1 %copy-start.20 = (bf16[112,896]{1,0:T(8,128)(2,1)}, bf16[112,896]{1,0:T(8,128)(2,1)S(1)}, u32[]{:S(2)}) copy-start(bf16[112,896]{1,0:T(8,128)(2,1)S(1)} %collective-permute-done.10.refs_5_) | copy-start | bytes 602116
  70.3 0.7 copy-start.21
  71.0 3.8 %copy-start.4 = (f32[3,896]{1,0:T(4,128)S(1)}, f32[3,896]{1,0:T(4,128)}, u32[]{:S(2)}) copy-start(f32[3,896]{1,0:T(4,128)} %bias_ref.3) | copy-start | bytes 32260
  74.7 2.2 %collective-permute-start.11 = (bf16[4,560,128]{2,1,0:T(8,128)(2,1)}, bf16[4,560,128]{2,1,0:T(8,128)(2,1)S(1)}, u32[]{:S(2)}, u32[]{:S(2)}) collective-permute-start(bf16[4,560,128]{2,1,0:T(8,128)(2,1)} %get-tuple-element.34), channel_id=1, source_target_pairs={{0,8},{8,0},{1,9},{9,1},{2,10},{10,2},{3,11},{11,3},{4,12},{12,4},... | collective-permute-start | bytes 1720328 | tf_op jit(solution)/shard_map/ppermute | solution.py:178
  75.6 11.5 %collective-permute-start.12 = (bf16[512,256]{1,0:T(8,128)(2,1)}, bf16[512,256]{1,0:T(8,128)(2,1)}, u32[]{:S(2)}, u32[]{:S(2)}) collective-permute-start(bf16[512,256]{1,0:T(8,128)(2,1)} %shard_map.125.own_ref), channel_id=1, source_target_pairs={{0,64},{128,192},{1,65},{129,193},{2,66},{130,194},{3,67},{131,195... | collective-permute-start | bytes 786440 | tf_op jit(solution)/shard_map/ppermute | solution.py:432
  76.9 10.2 %copy-start.1 = (bf16[896,224]{0,1:T(8,128)(2,1)S(1)}, bf16[896,224]{0,1:T(8,128)(2,1)}, u32[]{:S(2)}) copy-start(bf16[896,224]{0,1:T(8,128)(2,1)} %param.16) | copy-start | bytes 1204228
  77.9 15.1 %all-to-all-start.2 = ((bf16[4,560,128]{2,1,0:T(8,128)(2,1)}), bf16[4,560,128]{2,1,0:T(8,128)(2,1)S(1)}, u32[]{:S(2)}, u32[]{:S(2)}) async-start(bf16[4,560,128]{2,1,0:T(8,128)(2,1)} %shard_map.127), calls=%async_computation.2 | async-start | bytes 1146880 | tf_op jit(solution)/shard_map/all_to_all | solution.py:180
  87.1 36.8 %collective-permute-start.16 = (bf16[224,896]{1,0:T(8,128)(2,1)S(1)}, bf16[224,896]{1,0:T(8,128)(2,1)S(1)}, u32[]{:S(2)}, u32[]{:S(2)}) collective-permute-start(bf16[224,896]{1,0:T(8,128)(2,1)S(1)} %bitcast.17), channel_id=1, source_target_pairs={{0,64},{64,128},{128,192},{192,0},{1,65},{65,129},{129,193},{193,1... | collective-permute-start | bytes 1204232 | tf_op jit(solution)/shard_map/ppermute | solution.py:441
  87.1 36.8 %collective-permute-start.17 = (bf16[224,896]{1,0:T(8,128)(2,1)S(1)}, bf16[224,896]{1,0:T(8,128)(2,1)S(1)}, u32[]{:S(2)}, u32[]{:S(2)}) collective-permute-start(bf16[224,896]{1,0:T(8,128)(2,1)S(1)} %bitcast.18), channel_id=1, source_target_pairs={{0,192},{64,0},{128,64},{192,128},{1,193},{65,1},{129,65},{193,129... | collective-permute-start | bytes 1204232 | tf_op jit(solution)/shard_map/ppermute | solution.py:442
  89.1 34.8 %collective-permute-start.18 = (bf16[224,896]{1,0:T(8,128)(2,1)S(1)}, bf16[224,896]{1,0:T(8,128)(2,1)S(1)}, u32[]{:S(2)}, u32[]{:S(2)}) collective-permute-start(bf16[224,896]{1,0:T(8,128)(2,1)S(1)} %bitcast.19), channel_id=1, source_target_pairs={{0,128},{64,192},{128,0},{192,64},{1,129},{65,193},{129,1},{193,65... | collective-permute-start | bytes 1204232 | tf_op jit(solution)/shard_map/ppermute | solution.py:443
  93.0 0.7 copy-start.2
  93.7 15.7 %all-to-all-start.3 = ((bf16[8,64,256]{2,1,0:T(8,128)(2,1)}), bf16[8,64,256]{2,1,0:T(8,128)(2,1)}, u32[]{:S(2)}, u32[]{:S(2)}) async-start(bf16[8,64,256]{2,1,0:T(8,128)(2,1)} %bitcast.6), calls=%async_computation.3 | async-start | bytes 524288 | tf_op jit(solution)/shard_map/all_to_all | solution.py:455
  97.7 16.3 %copy-start.3 = (bf16[512,128]{1,0:T(8,128)(2,1)S(1)}, bf16[512,128]{1,0:T(8,128)(2,1)}, u32[]{:S(2)}) copy-start(bf16[512,128]{1,0:T(8,128)(2,1)} %copy-done.2) | copy-start | bytes 393220
  97.8 16.3 %copy-start.9 = (s32[2]{0:T(128)S(1)}, s32[2]{0:T(128)}, u32[]{:S(2)}) copy-start(s32[2]{0:T(128)} %offset_ref.1) | copy-start | bytes 28
  97.9 10.4 %collective-permute-start.13 = (bf16[8,2,16,128]{3,2,1,0:T(8,128)(2,1)S(1)}, bf16[8,2,16,128]{3,2,1,0:T(8,128)(2,1)S(1)}, u32[]{:S(2)}, u32[]{:S(2)}) collective-permute-start(bf16[8,2,16,128]{3,2,1,0:T(8,128)(2,1)S(1)} %get-tuple-element.39), channel_id=1, source_target_pairs={{0,64},{64,128},{128,192},{192,0},{1,65},{65,129},{129,193},{193,1... | collective-permute-start | bytes 196616 | tf_op jit(solution)/shard_map/ppermute | solution.py:422
  101.5 9.3 %collective-permute-start.14 = (bf16[8,2,16,128]{3,2,1,0:T(8,128)(2,1)S(1)}, bf16[8,2,16,128]{3,2,1,0:T(8,128)(2,1)S(1)}, u32[]{:S(2)}, u32[]{:S(2)}) collective-permute-start(bf16[8,2,16,128]{3,2,1,0:T(8,128)(2,1)S(1)} %get-tuple-element.40), channel_id=1, source_target_pairs={{0,192},{64,0},{128,64},{192,128},{1,193},{65,1},{129,65},{193,129... | collective-permute-start | bytes 196616 | tf_op jit(solution)/shard_map/ppermute | solution.py:423
  108.3 5.8 %collective-permute-start.15 = (bf16[8,2,16,128]{3,2,1,0:T(8,128)(2,1)S(1)}, bf16[8,2,16,128]{3,2,1,0:T(8,128)(2,1)S(1)}, u32[]{:S(2)}, u32[]{:S(2)}) collective-permute-start(bf16[8,2,16,128]{3,2,1,0:T(8,128)(2,1)S(1)} %get-tuple-element.41), channel_id=1, source_target_pairs={{0,128},{64,192},{128,0},{192,64},{1,129},{65,193},{129,1},{193,65... | collective-permute-start | bytes 196616 | tf_op jit(solution)/shard_map/ppermute | solution.py:424
  110.4 7.6 %copy-start.10 = (s32[2]{0:T(128)S(1)}, s32[2]{0:T(128)}, u32[]{:S(2)}) copy-start(s32[2]{0:T(128)} %len_ref.1) | copy-start | bytes 28
  123.9 7.7 %collective-permute-start.19 = (bf16[528,128]{1,0:T(8,128)(2,1)S(1)}, bf16[528,128]{1,0:T(8,128)(2,1)S(1)}, u32[]{:S(2)}, u32[]{:S(2)}) collective-permute-start(bf16[528,128]{1,0:T(8,128)(2,1)S(1)} %shard_map.131.refs_0_), channel_id=1, source_target_pairs={{0,16},{16,32},{32,48},{48,0},{1,17},{17,33},{33,49},{49,1},{2,18}... | collective-permute-start | bytes 405512 | tf_op jit(solution)/shard_map/ppermute | solution.py:471
  125.6 6.0 %collective-permute-start.20 = (bf16[528,128]{1,0:T(8,128)(2,1)S(1)}, bf16[528,128]{1,0:T(8,128)(2,1)S(1)}, u32[]{:S(2)}, u32[]{:S(2)}) collective-permute-start(bf16[528,128]{1,0:T(8,128)(2,1)S(1)} %shard_map.131.refs_0_), channel_id=1, source_target_pairs={{0,48},{16,0},{32,16},{48,32},{1,49},{17,1},{33,17},{49,33},{2,50}... | collective-permute-start | bytes 405512 | tf_op jit(solution)/shard_map/ppermute | solution.py:471
  127.2 6.5 %collective-permute-start.21 = (bf16[528,128]{1,0:T(8,128)(2,1)S(1)}, bf16[528,128]{1,0:T(8,128)(2,1)S(1)}, u32[]{:S(2)}, u32[]{:S(2)}) collective-permute-start(bf16[528,128]{1,0:T(8,128)(2,1)S(1)} %shard_map.131.refs_0_), channel_id=1, source_target_pairs={{0,32},{16,48},{32,0},{48,16},{1,33},{17,49},{33,1},{49,17},{2,34}... | collective-permute-start | bytes 405512 | tf_op jit(solution)/shard_map/ppermute | solution.py:471
  129.1 4.6 %collective-permute-start.22 = (bf16[528,128]{1,0:T(8,128)(2,1)S(1)}, bf16[528,128]{1,0:T(8,128)(2,1)S(1)}, u32[]{:S(2)}, u32[]{:S(2)}) collective-permute-start(bf16[528,128]{1,0:T(8,128)(2,1)S(1)} %shard_map.131.refs_0_), channel_id=1, source_target_pairs={{0,8},{8,0},{1,9},{9,1},{2,10},{10,2},{3,11},{11,3},{4,12},{12,4},... | collective-permute-start | bytes 405512 | tf_op jit(solution)/shard_map/ppermute | solution.py:472
  131.6 2.2 %collective-permute-start.23 = (bf16[528,128]{1,0:T(8,128)(2,1)S(1)}, bf16[528,128]{1,0:T(8,128)(2,1)S(1)}, u32[]{:S(2)}, u32[]{:S(2)}) collective-permute-start(bf16[528,128]{1,0:T(8,128)(2,1)S(1)} %collective-permute-done.19.refs_1_), channel_id=1, source_target_pairs={{0,8},{8,0},{1,9},{9,1},{2,10},{10,2},{3,11},{11,3},{4,12},{12,4},... | collective-permute-start | bytes 405512 | tf_op jit(solution)/shard_map/ppermute | solution.py:472
  131.6 2.2 %collective-permute-start.24 = (bf16[528,128]{1,0:T(8,128)(2,1)S(1)}, bf16[528,128]{1,0:T(8,128)(2,1)S(1)}, u32[]{:S(2)}, u32[]{:S(2)}) collective-permute-start(bf16[528,128]{1,0:T(8,128)(2,1)S(1)} %collective-permute-done.20.refs_2_), channel_id=1, source_target_pairs={{0,8},{8,0},{1,9},{9,1},{2,10},{10,2},{3,11},{11,3},{4,12},{12,4},... | collective-permute-start | bytes 405512 | tf_op jit(solution)/shard_map/ppermute | solution.py:472
  133.7 1.4 collective-permute-start.25
  137.5 36.1 %copy-start.8 = (f32[7168]{0:T(1024)S(1)}, f32[7168]{0:T(1024)}, u32[]{:S(2)}) copy-start(f32[7168]{0:T(1024)} %param.17) | copy-start | bytes 86020
  137.5 36.1 %all-to-all-start.4 = ((bf16[64,8,896]{2,1,0:T(8,128)(2,1)}), bf16[64,8,896]{2,1,0:T(8,128)(2,1)S(1)}, u32[]{:S(2)}, u32[]{:S(2)}) async-start(bf16[64,8,896]{2,1,0:T(8,128)(2,1)} %bitcast.9), calls=%async_computation.4 | async-start | bytes 1835008 | tf_op jit(solution)/shard_map/all_to_all | solution.py:487
  173.8 6.1 %collective-permute-start.26 = (bf16[8,7168]{1,0:T(8,128)(2,1)S(1)}, bf16[8,7168]{1,0:T(8,128)(2,1)S(1)}, u32[]{:S(2)}, u32[]{:S(2)}) collective-permute-start(bf16[8,7168]{1,0:T(8,128)(2,1)S(1)} %shard_map.133.refs_0_), channel_id=1, source_target_pairs={{0,1},{1,2},{2,3},{3,4},{4,5},{5,6},{6,7},{7,0},{8,9},{9,10},{10,1... | collective-permute-start | bytes 344072 | tf_op jit(solution)/shard_map/ppermute | solution.py:499
  175.5 4.8 %collective-permute-start.27 = (bf16[8,7168]{1,0:T(8,128)(2,1)S(1)}, bf16[8,7168]{1,0:T(8,128)(2,1)S(1)}, u32[]{:S(2)}, u32[]{:S(2)}) collective-permute-start(bf16[8,7168]{1,0:T(8,128)(2,1)S(1)} %shard_map.133.refs_0_), channel_id=1, source_target_pairs={{0,7},{1,0},{2,1},{3,2},{4,3},{5,4},{6,5},{7,6},{8,15},{9,8},{10,9... | collective-permute-start | bytes 344072 | tf_op jit(solution)/shard_map/ppermute | solution.py:502
  179.9 6.0 %collective-permute-start.28 = (bf16[8,7168]{1,0:T(8,128)(2,1)S(1)}, bf16[8,7168]{1,0:T(8,128)(2,1)S(1)}, u32[]{:S(2)}, u32[]{:S(2)}) collective-permute-start(bf16[8,7168]{1,0:T(8,128)(2,1)S(1)} %collective-permute-done.26.refs_1_), channel_id=1, source_target_pairs={{0,1},{1,2},{2,3},{3,4},{4,5},{5,6},{6,7},{7,0},{8,9},{9,10},{10,1... | collective-permute-start | bytes 344072 | tf_op jit(solution)/shard_map/ppermute | solution.py:499
  180.3 5.6 %collective-permute-start.29 = (bf16[8,7168]{1,0:T(8,128)(2,1)S(1)}, bf16[8,7168]{1,0:T(8,128)(2,1)S(1)}, u32[]{:S(2)}, u32[]{:S(2)}) collective-permute-start(bf16[8,7168]{1,0:T(8,128)(2,1)S(1)} %collective-permute-done.27.refs_2_), channel_id=1, source_target_pairs={{0,7},{1,0},{2,1},{3,2},{4,3},{5,4},{6,5},{7,6},{8,15},{9,8},{10,9... | collective-permute-start | bytes 344072 | tf_op jit(solution)/shard_map/ppermute | solution.py:502
  185.9 6.1 %collective-permute-start.30 = (bf16[8,7168]{1,0:T(8,128)(2,1)S(1)}, bf16[8,7168]{1,0:T(8,128)(2,1)S(1)}, u32[]{:S(2)}, u32[]{:S(2)}) collective-permute-start(bf16[8,7168]{1,0:T(8,128)(2,1)S(1)} %collective-permute-done.28.refs_3_), channel_id=1, source_target_pairs={{0,1},{1,2},{2,3},{3,4},{4,5},{5,6},{6,7},{7,0},{8,9},{9,10},{10,1... | collective-permute-start | bytes 344072 | tf_op jit(solution)/shard_map/ppermute | solution.py:499
  185.9 7.0 %collective-permute-start.31 = (bf16[8,7168]{1,0:T(8,128)(2,1)S(1)}, bf16[8,7168]{1,0:T(8,128)(2,1)S(1)}, u32[]{:S(2)}, u32[]{:S(2)}) collective-permute-start(bf16[8,7168]{1,0:T(8,128)(2,1)S(1)} %collective-permute-done.29.refs_4_), channel_id=1, source_target_pairs={{0,7},{1,0},{2,1},{3,2},{4,3},{5,4},{6,5},{7,6},{8,15},{9,8},{10,9... | collective-permute-start | bytes 344072 | tf_op jit(solution)/shard_map/ppermute | solution.py:502
  192.0 6.0 %collective-permute-start.32 = (bf16[8,7168]{1,0:T(8,128)(2,1)S(1)}, bf16[8,7168]{1,0:T(8,128)(2,1)S(1)}, u32[]{:S(2)}, u32[]{:S(2)}) collective-permute-start(bf16[8,7168]{1,0:T(8,128)(2,1)S(1)} %collective-permute-done.30.refs_5_), channel_id=1, source_target_pairs={{0,1},{1,2},{2,3},{3,4},{4,5},{5,6},{6,7},{7,0},{8,9},{9,10},{10,1... | collective-permute-start | bytes 344072 | tf_op jit(solution)/shard_map/ppermute | solution.py:499

commit v3 on v2

--- a/solution.py
+++ b/solution.py
@@ -395,7 +395,8 @@
         return left, lax.ppermute(value, "x", shift(XS, -1))
 
     turned = w_qkv.transpose(1, 0, 2)
-    k_own, v_own = turned[1], turned[2]
+    k_own, turned = lax.optimization_barrier((turned[1], turned))
+    v_own = turned[2]
     k_left, k_right = near(k_own)
     v_left, v_right = near(v_own)
     k_far = lax.ppermute(k_left, "x", shift(XS, 1))
@@ -453,8 +454,6 @@
     )
     tied_kv, queries = lax.optimization_barrier((own_kv, queries))
     mine = lax.all_to_all(tied_kv.reshape(GROUP, tok_rows, 2 * HEAD), ("y", "c"), 0, 0, tiled=True)
-    new_kv = mine[:heads].reshape(heads, tok_rows, 2, HEAD)
-    new_kv = new_kv.transpose(1, 2, 0, 3).reshape(tok_rows, 2, head_width)
     prefilled = in_vmem(
         functools.partial(attend_kernel, pre_dev),
         bf16(rows, HEAD),
@@ -465,9 +464,11 @@
     prefilled, sums = lax.optimization_barrier((prefilled, sums))
     decoded = decode(dec_len, sums, head_bias, dec_cache)
     payload = in_vmem(pack_kernel, bf16(rows + dec_dev * GROUP, HEAD), [], [prefilled, decoded])
-    payload, new_kv, w_left, w_right, w_far = lax.optimization_barrier(
-        (payload, new_kv, w_left, w_right, w_far)
-    )
+    payload, mine, w_left, w_right, w_far = lax.optimization_barrier(
+        (payload, mine, w_left, w_right, w_far)
+    )
+    new_kv = mine[:heads].reshape(heads, tok_rows, 2, HEAD)
+    new_kv = new_kv.transpose(1, 2, 0, 3).reshape(tok_rows, 2, head_width)
     gathered = [payload] + [lax.ppermute(payload, "y", shift(YS, s)) for s in (1, -1, 2)]
     gathered += [lax.ppermute(part, "c", [(0, 1), (1, 0)]) for part in gathered]
     piece = w_own.shape[0]

time: 201 us -> 203 us (level)
    ppermute x3, waiting for transfers between devices: 5.08 us -> 11.9 us  [near(): return (left, lax.ppermute(value, 'x', shift(XS, -1)))]
    ppermute x1, waiting for transfers between devices: 0.54 us -> 6.78 us  [on_device(): v_far = lax.ppermute(v_right, 'x', shift(XS, -1))]
    ppermute x1, waiting for transfers between devices: 6.65 us -> 0.61 us  [on_device(): k_far = lax.ppermute(k_left, 'x', shift(XS, 1))]
    ppermute x3, waiting for transfers between devices: 13.7 us -> 7.92 us  [near(): left = lax.ppermute(value, 'x', shift(XS, 1))]
  transfers between devices with their start and end apart: 38 -> 38, of which waited for: 22 -> 19; matrix products, arithmetic and copies ran while one was open for 3% -> 3% of each run, Pallas kernels for 8% -> 8%
where the time goes in v3:
time: 203 us; the launch traced here: 201 us
  waiting for transfers between devices  94.9 us (47%)
  starting transfers between devices  65.4 us (32%)
  Pallas kernels  27.6 us (14%)
  local copies, waits for them, and re-layouts  11.6 us (6%)
    all_to_all x1, waiting for transfers between devices, on_device(): shares = lax.all_to_all(shares, ('y', 'c', 'z'), 0, 0, tiled=True)  24.9 us
    pallas_call x13, Pallas kernels, in_vmem(): pl.pallas_call(kernel, out_shape=out_shape, in_specs=[pl.BlockSpec(memory...  21.7 us
    ppermute x4, waiting for transfers between devices, on_device(): up = lax.ppermute(up, 'z', shift(ZS, 1))  12.4 us
    ppermute x3, waiting for transfers between devices, near(): return (left, lax.ppermute(value, 'x', shift(XS, -1)))  11.9 us
    all_to_all x1, starting transfers between devices, on_device(): shares = lax.all_to_all(shares, ('y', 'c', 'z'), 0, 0, tiled=True)  11 us
    all_to_all x2, starting transfers between devices, reduce_partial(): return lax.all_to_all(partial, 'y', 0, 0, tiled=True)  8.81 us
    ppermute x3, waiting for transfers between devices, near(): left = lax.ppermute(value, 'x', shift(XS, 1))  7.92 us
    ppermute x3, starting transfers between devices, on_device(): down = lax.ppermute(down, 'z', shift(ZS, -1))  7.68 us
  transfers between devices with their start and end apart: 38, of which 19 were waited for; matrix products, arithmetic and copies ran while one was open for 3% of the time, Pallas kernels for 8%

profile of v3, /device:TPU:2, one launch (start us, length us, event | category | flops | bytes accessed | tf_op | source)
XLA Modules:
  0.0 200.5 jit_solution(14661720598144805910)
XLA Ops:
  0.6 1.2 copy-done
  1.8 0.9 copy-done.5
  2.7 0.7 copy-done.6
  3.5 0.7 copy-done.7
  4.2 2.4 %shard_map.122 = bf16[8,4,80,224]{3,2,1,0:T(8,128)(2,1)} custom-call(bf16[64,7168]{1,0:T(8,128)(2,1)S(1)} %copy-done, f32[1,7168]{1,0:T(1,128)S(1)} %bitcast.24, f32[1,7168]{1,0:T(1,128)S(1)} %bitcast.25, bf16[16,2,2,896]{3,2,1,0:T(2,128)(2,1)S(1)} %copy-done.5), custom_call_target="tpu_custom_call" | custom-call | tf_op jit(solution)/shard_map/pallas_call | solution.py:31
  6.6 4.5 %all-to-all-start = ((bf16[8,4,80,224]{3,2,1,0:T(8,128)(2,1)}), bf16[8,4,80,224]{3,2,1,0:T(8,128)(2,1)S(1)}, u32[]{:S(2)}, u32[]{:S(2)}) async-start(bf16[8,4,80,224]{3,2,1,0:T(8,128)(2,1)} %shard_map.122), calls=%async_computation | async-start | bytes 2621440 | tf_op jit(solution)/shard_map/all_to_all | solution.py:419
  11.1 1.0 slice_bitcast_fusion.refs_1_
  12.1 2.1 %slice_bitcast_fusion.1 = (bf16[224,896]{1,0:T(8,128)(2,1)}, bf16[224,896]{1,0:T(8,128)(2,1)S(1)}) fusion(bf16[3,224,896]{2,1,0:T(8,128)(2,1)} %bitcast.28), kind=kLoop, calls=%fused_computation.1 | loop fusion | bytes 1605632 | tf_op jit(solution)/shard_map/squeeze | solution.py:404
  14.2 1.4 collective-permute-start.2
  15.6 0.7 collective-permute-start
  16.2 1.5 collective-permute-start.1
  18.3 8.1 %collective-permute-done.2.refs_6_ = bf16[224,896]{1,0:T(8,128)(2,1)S(1)} collective-permute-done((bf16[224,896]{1,0:T(8,128)(2,1)S(1)}, bf16[224,896]{1,0:T(8,128)(2,1)S(1)}, u32[]{:S(2)}, u32[]{:S(2)}) %collective-permute-start.2) | collective-permute-done | bytes 401440 | tf_op jit(solution)/shard_map/ppermute | solution.py:395
  26.4 1.4 collective-permute-start.5
  27.7 0.7 collective-permute-start.4
  28.4 7.9 %collective-permute-done.1.refs_4_ = bf16[224,896]{1,0:T(8,128)(2,1)S(1)} collective-permute-done((bf16[224,896]{1,0:T(8,128)(2,1)S(1)}, bf16[224,896]{1,0:T(8,128)(2,1)S(1)}, u32[]{:S(2)}, u32[]{:S(2)}) %collective-permute-start.1) | collective-permute-done | bytes 401440 | tf_op jit(solution)/shard_map/ppermute | solution.py:394
  36.3 6.8 %collective-permute-done.5.refs_8_ = bf16[224,896]{1,0:T(8,128)(2,1)S(1)} collective-permute-done((bf16[224,896]{1,0:T(8,128)(2,1)S(1)}, bf16[224,896]{1,0:T(8,128)(2,1)S(1)}, u32[]{:S(2)}, u32[]{:S(2)}) %collective-permute-start.5) | collective-permute-done | bytes 401440 | tf_op jit(solution)/shard_map/ppermute | solution.py:403
  43.1 0.8 copy-done.19
  44.5 4.8 %shard_map.123 = (bf16[4,512,256]{2,1,0:T(8,128)(2,1)S(1)}, bf16[4,512,256]{2,1,0:T(8,128)(2,1)S(1)}, f32[8,32,128]{2,1,0:T(8,128)S(1)}) custom-call(bf16[8,4,80,224]{3,2,1,0:T(8,128)(2,1)S(1)} %all-to-all-done.refs_0_.in_ref, bf16[224,896]{1,0:T(8,128)(2,1)} %copy-done.11, bf16[224,896]{1,0:T(8,128)(2,1)} %copy-done.12, bf16[224,896]{1,0:T(8,128)(2,1)} %copy-done.16, ...), custom_call_target="tpu_custom_call" | custom-call | tf_op jit(solution)/shard_map/pallas_call | solution.py:31
  49.4 3.0 %collective-permute-start.8 = (bf16[224,896]{1,0:T(8,128)(2,1)}, bf16[224,896]{1,0:T(8,128)(2,1)S(1)}, u32[]{:S(2)}, u32[]{:S(2)}) collective-permute-start(bf16[224,896]{1,0:T(8,128)(2,1)} %get-tuple-element.35.refs_1_), channel_id=1, source_target_pairs={{0,192},{64,0},{128,64},{192,128},{1,193},{65,1},{129,65},{193,129... | collective-permute-start | bytes 1204232 | tf_op jit(solution)/shard_map/ppermute | solution.py:395
  52.5 1.3 shard_map.124
  53.7 4.4 %all-to-all-start.1 = ((bf16[4,512,256]{2,1,0:T(8,128)(2,1)}), bf16[4,512,256]{2,1,0:T(8,128)(2,1)S(1)}, u32[]{:S(2)}, u32[]{:S(2)}) async-start(bf16[4,512,256]{2,1,0:T(8,128)(2,1)} %shard_map.124), calls=%async_computation.1 | async-start | bytes 2097152 | tf_op jit(solution)/shard_map/all_to_all | solution.py:180
  58.1 3.8 %collective-permute-done.8.refs_3_ = bf16[224,896]{1,0:T(8,128)(2,1)S(1)} collective-permute-done((bf16[224,896]{1,0:T(8,128)(2,1)}, bf16[224,896]{1,0:T(8,128)(2,1)S(1)}, u32[]{:S(2)}, u32[]{:S(2)}) %collective-permute-start.8) | collective-permute-done | bytes 401440 | tf_op jit(solution)/shard_map/ppermute | solution.py:395
  61.9 2.5 %collective-permute-start.10 = (bf16[112,896]{1,0:T(8,128)(2,1)S(1)}, bf16[112,896]{1,0:T(8,128)(2,1)S(1)}, u32[]{:S(2)}, u32[]{:S(2)}) collective-permute-start(bf16[112,896]{1,0:T(8,128)(2,1)S(1)} %slice.26), channel_id=1, source_target_pairs={{0,192},{64,0},{128,64},{192,128},{1,193},{65,1},{129,65},{193,129... | collective-permute-start | bytes 602120 | tf_op jit(solution)/shard_map/ppermute | solution.py:409
  64.5 4.0 %collective-permute-done.10.refs_5_ = bf16[112,896]{1,0:T(8,128)(2,1)S(1)} collective-permute-done((bf16[112,896]{1,0:T(8,128)(2,1)S(1)}, bf16[112,896]{1,0:T(8,128)(2,1)S(1)}, u32[]{:S(2)}, u32[]{:S(2)}) %collective-permute-start.10) | collective-permute-done | bytes 200736 | tf_op jit(solution)/shard_map/ppermute | solution.py:409
  68.5 2.6 %collective-permute-done.9.refs_4_ = bf16[112,896]{1,0:T(8,128)(2,1)S(1)} collective-permute-done((bf16[112,896]{1,0:T(8,128)(2,1)S(1)}, bf16[112,896]{1,0:T(8,128)(2,1)S(1)}, u32[]{:S(2)}, u32[]{:S(2)}) %collective-permute-start.9) | collective-permute-done | bytes 200736 | tf_op jit(solution)/shard_map/ppermute | solution.py:408
  71.1 0.7 copy-done.21
  71.8 3.8 %shard_map.126 = (bf16[4,560,128]{2,1,0:T(8,128)(2,1)}, bf16[4,560,128]{2,1,0:T(8,128)(2,1)S(1)}, f32[8,16,128]{2,1,0:T(8,128)}) custom-call(bf16[8,4,80,224]{3,2,1,0:T(8,128)(2,1)S(1)} %all-to-all-done.refs_0_.in_ref, bf16[224,896]{1,0:T(8,128)(2,1)} %get-tuple-element.35.refs_1_, bf16[224,896]{1,0:T(8,128)(2,1)} %copy-done.14, ...), custom_call_target="tpu_custom_call" | custom-call | tf_op jit(solution)/shard_map/pallas_call | solution.py:31
  75.6 0.8 shard_map.125.own_ref
  76.4 1.3 collective-permute-start.12
  77.7 0.9 shard_map.127
  78.7 4.4 %all-to-all-start.2 = ((bf16[4,560,128]{2,1,0:T(8,128)(2,1)}), bf16[4,560,128]{2,1,0:T(8,128)(2,1)S(1)}, u32[]{:S(2)}, u32[]{:S(2)}) async-start(bf16[4,560,128]{2,1,0:T(8,128)(2,1)} %shard_map.127), calls=%async_computation.2 | async-start | bytes 1146880 | tf_op jit(solution)/shard_map/all_to_all | solution.py:180
  83.1 4.8 %collective-permute-done.12.last_ref = bf16[512,256]{1,0:T(8,128)(2,1)} collective-permute-done((bf16[512,256]{1,0:T(8,128)(2,1)}, bf16[512,256]{1,0:T(8,128)(2,1)}, u32[]{:S(2)}, u32[]{:S(2)}) %collective-permute-start.12) | collective-permute-done | bytes 262176 | tf_op jit(solution)/shard_map/ppermute | solution.py:433
  87.9 2.0 %collective-permute-start.17 = (bf16[224,896]{1,0:T(8,128)(2,1)S(1)}, bf16[224,896]{1,0:T(8,128)(2,1)S(1)}, u32[]{:S(2)}, u32[]{:S(2)}) collective-permute-start(bf16[224,896]{1,0:T(8,128)(2,1)S(1)} %bitcast.21), channel_id=1, source_target_pairs={{0,192},{64,0},{128,64},{192,128},{1,193},{65,1},{129,65},{193,129... | collective-permute-start | bytes 1204232 | tf_op jit(solution)/shard_map/ppermute | solution.py:443
  89.9 1.4 collective-permute-start.18
  91.4 2.4 %all-to-all-done.2.partial_ref = bf16[4,560,128]{2,1,0:T(8,128)(2,1)S(1)} async-done(((bf16[4,560,128]{2,1,0:T(8,128)(2,1)}), bf16[4,560,128]{2,1,0:T(8,128)(2,1)S(1)}, u32[]{:S(2)}, u32[]{:S(2)}) %all-to-all-start.2) | async-done | bytes 573472 | tf_op jit(solution)/shard_map/all_to_all | solution.py:180
  93.8 0.6 copy-done.2
  94.5 4.2 %all-to-all-start.3 = ((bf16[8,64,256]{2,1,0:T(8,128)(2,1)}), bf16[8,64,256]{2,1,0:T(8,128)(2,1)}, u32[]{:S(2)}, u32[]{:S(2)}) async-start(bf16[8,64,256]{2,1,0:T(8,128)(2,1)} %bitcast.6), calls=%async_computation.3 | async-start | bytes 524288 | tf_op jit(solution)/shard_map/all_to_all | solution.py:456
  98.8 3.7 %collective-permute-start.13 = (bf16[8,2,16,128]{3,2,1,0:T(8,128)(2,1)S(1)}, bf16[8,2,16,128]{3,2,1,0:T(8,128)(2,1)S(1)}, u32[]{:S(2)}, u32[]{:S(2)}) collective-permute-start(bf16[8,2,16,128]{3,2,1,0:T(8,128)(2,1)S(1)} %get-tuple-element.43), channel_id=1, source_target_pairs={{0,64},{64,128},{128,192},{192,0},{1,65},{65,129},{129,193},{193,1... | collective-permute-start | bytes 196616 | tf_op jit(solution)/shard_map/ppermute | solution.py:423
  102.6 6.5 %collective-permute-done.13.refs_1_ = bf16[8,2,16,128]{3,2,1,0:T(8,128)(2,1)S(1)} collective-permute-done((bf16[8,2,16,128]{3,2,1,0:T(8,128)(2,1)S(1)}, bf16[8,2,16,128]{3,2,1,0:T(8,128)(2,1)S(1)}, u32[]{:S(2)}, u32[]{:S(2)}) %collective-permute-start.13) | collective-permute-done | bytes 65568 | tf_op jit(solution)/shard_map/ppermute | solution.py:423
  109.1 1.1 collective-permute-start.15
  110.2 4.6 %collective-permute-done.15.refs_3_ = bf16[8,2,16,128]{3,2,1,0:T(8,128)(2,1)S(1)} collective-permute-done((bf16[8,2,16,128]{3,2,1,0:T(8,128)(2,1)S(1)}, bf16[8,2,16,128]{3,2,1,0:T(8,128)(2,1)S(1)}, u32[]{:S(2)}, u32[]{:S(2)}) %collective-permute-start.15) | collective-permute-done | bytes 65568 | tf_op jit(solution)/shard_map/ppermute | solution.py:425
  114.8 3.9 %shard_map.130.prefill_ref = bf16[512,128]{1,0:T(8,128)(2,1)S(1)} custom-call(s32[2]{0:T(128)S(1)} %copy-done.9, bf16[512,128]{1,0:T(8,128)(2,1)S(1)} %copy-done.3, bf16[512,256]{1,0:T(8,128)(2,1)} %shard_map.125.own_ref, bf16[512,256]{1,0:T(8,128)(2,1)} %collective-permute-done.12.last_ref, bf16[8,2,16,128]{3,2,1,0:T(8,128)(2,1)S(1)} %get-tuple-element.42.refs_0_, ...), custom_call_target="tpu_custom_call" | custom-call | tf_op jit(solution)/shard_map/pallas_call | solution.py:31
  118.7 5.9 %decode.1.decode_ref = f32[2,8,128]{2,1,0:T(8,128)S(1)} custom-call(s32[2]{0:T(128)S(1)} %copy-done.10, f32[48,128]{1,0:T(8,128)S(1)} %get-tuple-element.48.sums_ref, f32[3,8,128]{2,1,0:T(8,128)S(1)} %pad.4.bias_ref, bf16[2,1024,2,896]{3,2,1,0:T(2,128)(2,1)} %cache_ref.1), custom_call_target="tpu_custom_call" | custom-call | tf_op jit(solution)/shard_map/decode/pallas_call | solution.py:300
  124.7 1.7 collective-permute-start.19
  126.4 1.6 collective-permute-start.20
  128.0 1.9 collective-permute-start.21
  129.9 2.4 %collective-permute-done.19.refs_1_ = bf16[528,128]{1,0:T(8,128)(2,1)S(1)} collective-permute-done((bf16[528,128]{1,0:T(8,128)(2,1)S(1)}, bf16[528,128]{1,0:T(8,128)(2,1)S(1)}, u32[]{:S(2)}, u32[]{:S(2)}) %collective-permute-start.19) | collective-permute-done | bytes 135200 | tf_op jit(solution)/shard_map/ppermute | solution.py:472
  132.9 1.7 collective-permute-done.21.refs_3_
  134.5 1.3 collective-permute-done.25.refs_7_
  135.9 2.4 %shard_map.132 = bf16[512,896]{1,0:T(8,128)(2,1)} custom-call(bf16[528,128]{1,0:T(8,128)(2,1)S(1)} %shard_map.131.refs_0_, bf16[528,128]{1,0:T(8,128)(2,1)S(1)} %collective-permute-done.19.refs_1_, bf16[528,128]{1,0:T(8,128)(2,1)S(1)} %collective-permute-done.20.refs_2_, bf16[528,128]{1,0:T(8,128)(2,1)S(1)} %collective-permute-done.21.refs_3_, ...), custom_call_target="tpu_custom_call" | custom-call | tf_op jit(solution)/shard_map/pallas_call | solution.py:31
  138.3 11.0 %all-to-all-start.4 = ((bf16[64,8,896]{2,1,0:T(8,128)(2,1)}), bf16[64,8,896]{2,1,0:T(8,128)(2,1)S(1)}, u32[]{:S(2)}, u32[]{:S(2)}) async-start(bf16[64,8,896]{2,1,0:T(8,128)(2,1)} %bitcast.8), calls=%async_computation.4 | async-start | bytes 1835008 | tf_op jit(solution)/shard_map/all_to_all | solution.py:488
  149.3 0.9 constant_dynamic-slice_fusion.hid_ref
  150.2 24.9 %all-to-all-done.4.in_ref = bf16[64,8,896]{2,1,0:T(8,128)(2,1)S(1)} async-done(((bf16[64,8,896]{2,1,0:T(8,128)(2,1)}), bf16[64,8,896]{2,1,0:T(8,128)(2,1)S(1)}, u32[]{:S(2)}, u32[]{:S(2)}) %all-to-all-start.4) | async-done | bytes 917536 | tf_op jit(solution)/shard_map/all_to_all | solution.py:488
  175.3 1.7 collective-permute-start.26
  177.0 1.6 collective-permute-start.27
  178.6 2.8 %collective-permute-done.26.refs_1_ = bf16[8,7168]{1,0:T(8,128)(2,1)S(1)} collective-permute-done((bf16[8,7168]{1,0:T(8,128)(2,1)S(1)}, bf16[8,7168]{1,0:T(8,128)(2,1)S(1)}, u32[]{:S(2)}, u32[]{:S(2)}) %collective-permute-start.26) | collective-permute-done | bytes 114720 | tf_op jit(solution)/shard_map/ppermute | solution.py:500
  181.8 2.8 %collective-permute-start.29 = (bf16[8,7168]{1,0:T(8,128)(2,1)S(1)}, bf16[8,7168]{1,0:T(8,128)(2,1)S(1)}, u32[]{:S(2)}, u32[]{:S(2)}) collective-permute-start(bf16[8,7168]{1,0:T(8,128)(2,1)S(1)} %collective-permute-done.27.refs_2_), channel_id=1, source_target_pairs={{0,7},{1,0},{2,1},{3,2},{4,3},{5,4},{6,5},{7,6},{8,15},{9,8},{10,9... | collective-permute-start | bytes 344072 | tf_op jit(solution)/shard_map/ppermute | solution.py:503
  184.6 2.8 %collective-permute-done.28.refs_3_ = bf16[8,7168]{1,0:T(8,128)(2,1)S(1)} collective-permute-done((bf16[8,7168]{1,0:T(8,128)(2,1)S(1)}, bf16[8,7168]{1,0:T(8,128)(2,1)S(1)}, u32[]{:S(2)}, u32[]{:S(2)}) %collective-permute-start.28) | collective-permute-done | bytes 114720 | tf_op jit(solution)/shard_map/ppermute | solution.py:500
  187.4 1.0 slice.23
  188.4 3.3 %collective-permute-start.31 = (bf16[8,7168]{1,0:T(8,128)(2,1)S(1)}, bf16[8,7168]{1,0:T(8,128)(2,1)S(1)}, u32[]{:S(2)}, u32[]{:S(2)}) collective-permute-start(bf16[8,7168]{1,0:T(8,128)(2,1)S(1)} %collective-permute-done.29.refs_4_), channel_id=1, source_target_pairs={{0,7},{1,0},{2,1},{3,2},{4,3},{5,4},{6,5},{7,6},{8,15},{9,8},{10,9... | collective-permute-start | bytes 344072 | tf_op jit(solution)/shard_map/ppermute | solution.py:503
  191.7 1.8 collective-permute-done.30.refs_5_
  193.5 0.8 copy_bitcast_fusion
  194.4 5.1 %collective-permute-done.32.refs_7_ = bf16[8,7168]{1,0:T(8,128)(2,1)S(1)} collective-permute-done((bf16[8,7168]{1,0:T(8,128)(2,1)S(1)}, bf16[8,7168]{1,0:T(8,128)(2,1)S(1)}, u32[]{:S(2)}, u32[]{:S(2)}) %collective-permute-start.32) | collective-permute-done | bytes 114720 | tf_op jit(solution)/shard_map/ppermute | solution.py:500
  199.5 1.0 shard_map.134
  (80 shorter events, 3.1 us)
Async XLA Ops:
  0.6 1.2 copy-start
  1.8 0.9 copy-start.5
  2.7 0.7 copy-start.6
  3.5 0.7 copy-start.7
  6.6 37.9 %all-to-all-start = ((bf16[8,4,80,224]{3,2,1,0:T(8,128)(2,1)}), bf16[8,4,80,224]{3,2,1,0:T(8,128)(2,1)S(1)}, u32[]{:S(2)}, u32[]{:S(2)}) async-start(bf16[8,4,80,224]{3,2,1,0:T(8,128)(2,1)} %shard_map.122), calls=%async_computation | async-start | bytes 2621440 | tf_op jit(solution)/shard_map/all_to_all | solution.py:419
  12.1 32.4 %copy-start.11 = (bf16[224,896]{1,0:T(8,128)(2,1)}, bf16[224,896]{1,0:T(8,128)(2,1)S(1)}, u32[]{:S(2)}) copy-start(bf16[224,896]{1,0:T(8,128)(2,1)S(1)} %slice_bitcast_fusion.refs_1_) | copy-start | bytes 1204228
  14.2 30.3 %copy-start.12 = (bf16[224,896]{1,0:T(8,128)(2,1)}, bf16[224,896]{1,0:T(8,128)(2,1)S(1)}, u32[]{:S(2)}) copy-start(bf16[224,896]{1,0:T(8,128)(2,1)S(1)} %get-tuple-element.61.refs_2_) | copy-start | bytes 1204228
  14.2 12.2 %collective-permute-start.2 = (bf16[224,896]{1,0:T(8,128)(2,1)S(1)}, bf16[224,896]{1,0:T(8,128)(2,1)S(1)}, u32[]{:S(2)}, u32[]{:S(2)}) collective-permute-start(bf16[224,896]{1,0:T(8,128)(2,1)S(1)} %get-tuple-element.61.refs_2_), channel_id=1, source_target_pairs={{0,192},{64,0},{128,64},{192,128},{1,193},{65,1},{129,65},{193,129... | collective-permute-start | bytes 1204232 | tf_op jit(solution)/shard_map/ppermute | solution.py:395
  15.6 12.2 %collective-permute-start = (bf16[224,896]{1,0:T(8,128)(2,1)S(1)}, bf16[224,896]{1,0:T(8,128)(2,1)S(1)}, u32[]{:S(2)}, u32[]{:S(2)}) collective-permute-start(bf16[224,896]{1,0:T(8,128)(2,1)S(1)} %slice_bitcast_fusion.refs_1_), channel_id=1, source_target_pairs={{0,64},{64,128},{128,192},{192,0},{1,65},{65,129},{129,193},{193,1... | collective-permute-start | bytes 1204232 | tf_op jit(solution)/shard_map/ppermute | solution.py:394
  16.2 20.1 %collective-permute-start.1 = (bf16[224,896]{1,0:T(8,128)(2,1)S(1)}, bf16[224,896]{1,0:T(8,128)(2,1)S(1)}, u32[]{:S(2)}, u32[]{:S(2)}) collective-permute-start(bf16[224,896]{1,0:T(8,128)(2,1)S(1)} %get-tuple-element.61.refs_2_), channel_id=1, source_target_pairs={{0,64},{64,128},{128,192},{192,0},{1,65},{65,129},{129,193},{193,1... | collective-permute-start | bytes 1204232 | tf_op jit(solution)/shard_map/ppermute | solution.py:394
  17.7 18.6 %collective-permute-start.3 = (bf16[224,896]{1,0:T(8,128)(2,1)S(1)}, bf16[224,896]{1,0:T(8,128)(2,1)S(1)}, u32[]{:S(2)}, u32[]{:S(2)}) collective-permute-start(bf16[224,896]{1,0:T(8,128)(2,1)S(1)} %slice_bitcast_fusion.refs_1_), channel_id=1, source_target_pairs={{0,192},{64,0},{128,64},{192,128},{1,193},{65,1},{129,65},{193,129... | collective-permute-start | bytes 1204232 | tf_op jit(solution)/shard_map/ppermute | solution.py:395
  26.4 18.1 %copy-start.15 = (bf16[224,896]{1,0:T(8,128)(2,1)}, bf16[224,896]{1,0:T(8,128)(2,1)S(1)}, u32[]{:S(2)}) copy-start(bf16[224,896]{1,0:T(8,128)(2,1)S(1)} %collective-permute-done.2.refs_6_) | copy-start | bytes 1204228
  26.4 16.7 %collective-permute-start.5 = (bf16[224,896]{1,0:T(8,128)(2,1)S(1)}, bf16[224,896]{1,0:T(8,128)(2,1)S(1)}, u32[]{:S(2)}, u32[]{:S(2)}) collective-permute-start(bf16[224,896]{1,0:T(8,128)(2,1)S(1)} %collective-permute-done.2.refs_6_), channel_id=1, source_target_pairs={{0,192},{64,0},{128,64},{192,128},{1,193},{65,1},{129,65},{193,129... | collective-permute-start | bytes 1204232 | tf_op jit(solution)/shard_map/ppermute | solution.py:403
  27.7 16.8 %copy-start.16 = (bf16[224,896]{1,0:T(8,128)(2,1)}, bf16[224,896]{1,0:T(8,128)(2,1)S(1)}, u32[]{:S(2)}) copy-start(bf16[224,896]{1,0:T(8,128)(2,1)S(1)} %collective-permute-done.refs_3_) | copy-start | bytes 1204228
  27.7 16.8 %collective-permute-start.4 = (bf16[224,896]{1,0:T(8,128)(2,1)S(1)}, bf16[224,896]{1,0:T(8,128)(2,1)}, u32[]{:S(2)}, u32[]{:S(2)}) collective-permute-start(bf16[224,896]{1,0:T(8,128)(2,1)S(1)} %collective-permute-done.refs_3_), channel_id=1, source_target_pairs={{0,64},{64,128},{128,192},{192,0},{1,65},{65,129},{129,193},{193,1... | collective-permute-start | bytes 1204232 | tf_op jit(solution)/shard_map/ppermute | solution.py:402
  36.3 6.8 %copy-start.17 = (bf16[224,896]{1,0:T(8,128)(2,1)}, bf16[224,896]{1,0:T(8,128)(2,1)S(1)}, u32[]{:S(2)}) copy-start(bf16[224,896]{1,0:T(8,128)(2,1)S(1)} %collective-permute-done.1.refs_4_) | copy-start | bytes 1204228
  36.3 6.8 %copy-start.18 = (bf16[224,896]{1,0:T(8,128)(2,1)}, bf16[224,896]{1,0:T(8,128)(2,1)S(1)}, u32[]{:S(2)}) copy-start(bf16[224,896]{1,0:T(8,128)(2,1)S(1)} %collective-permute-done.3.refs_5_) | copy-start | bytes 1204228
  43.1 0.8 copy-start.19
  49.3 3.1 %collective-permute-start.6 = (bf16[4,512,256]{2,1,0:T(8,128)(2,1)S(1)}, bf16[4,512,256]{2,1,0:T(8,128)(2,1)S(1)}, u32[]{:S(2)}, u32[]{:S(2)}) collective-permute-start(bf16[4,512,256]{2,1,0:T(8,128)(2,1)S(1)} %get-tuple-element.34), channel_id=1, source_target_pairs={{0,8},{8,0},{1,9},{9,1},{2,10},{10,2},{3,11},{11,3},{4,12},{12,4},... | collective-permute-start | bytes 3145736 | tf_op jit(solution)/shard_map/ppermute | solution.py:178
  49.4 12.5 %collective-permute-start.8 = (bf16[224,896]{1,0:T(8,128)(2,1)}, bf16[224,896]{1,0:T(8,128)(2,1)S(1)}, u32[]{:S(2)}, u32[]{:S(2)}) collective-permute-start(bf16[224,896]{1,0:T(8,128)(2,1)} %get-tuple-element.35.refs_1_), channel_id=1, source_target_pairs={{0,192},{64,0},{128,64},{192,128},{1,193},{65,1},{129,65},{193,129... | collective-permute-start | bytes 1204232 | tf_op jit(solution)/shard_map/ppermute | solution.py:395
  52.5 11.9 %collective-permute-start.7 = (bf16[224,896]{1,0:T(8,128)(2,1)}, bf16[224,896]{1,0:T(8,128)(2,1)S(1)}, u32[]{:S(2)}, u32[]{:S(2)}) collective-permute-start(bf16[224,896]{1,0:T(8,128)(2,1)} %get-tuple-element.35.refs_1_), channel_id=1, source_target_pairs={{0,64},{64,128},{128,192},{192,0},{1,65},{65,129},{129,193},{193,1... | collective-permute-start | bytes 1204232 | tf_op jit(solution)/shard_map/ppermute | solution.py:394
  53.7 21.8 %all-to-all-start.1 = ((bf16[4,512,256]{2,1,0:T(8,128)(2,1)}), bf16[4,512,256]{2,1,0:T(8,128)(2,1)S(1)}, u32[]{:S(2)}, u32[]{:S(2)}) async-start(bf16[4,512,256]{2,1,0:T(8,128)(2,1)} %shard_map.124), calls=%async_computation.1 | async-start | bytes 2097152 | tf_op jit(solution)/shard_map/all_to_all | solution.py:180
  61.9 9.2 %copy-start.13 = (bf16[224,896]{1,0:T(8,128)(2,1)}, bf16[224,896]{1,0:T(8,128)(2,1)S(1)}, u32[]{:S(2)}) copy-start(bf16[224,896]{1,0:T(8,128)(2,1)S(1)} %collective-permute-done.8.refs_3_) | copy-start | bytes 1204228
  61.9 6.5 %collective-permute-start.10 = (bf16[112,896]{1,0:T(8,128)(2,1)S(1)}, bf16[112,896]{1,0:T(8,128)(2,1)S(1)}, u32[]{:S(2)}, u32[]{:S(2)}) collective-permute-start(bf16[112,896]{1,0:T(8,128)(2,1)S(1)} %slice.26), channel_id=1, source_target_pairs={{0,192},{64,0},{128,64},{192,128},{1,193},{65,1},{129,65},{193,129... | collective-permute-start | bytes 602120 | tf_op jit(solution)/shard_map/ppermute | solution.py:409
  64.4 6.7 %copy-start.14 = (bf16[224,896]{1,0:T(8,128)(2,1)}, bf16[224,896]{1,0:T(8,128)(2,1)S(1)}, u32[]{:S(2)}) copy-start(bf16[224,896]{1,0:T(8,128)(2,1)S(1)} %collective-permute-done.7.refs_2_) | copy-start | bytes 1204228
  64.4 6.7 %collective-permute-start.9 = (bf16[112,896]{1,0:T(8,128)(2,1)S(1)}, bf16[112,896]{1,0:T(8,128)(2,1)S(1)}, u32[]{:S(2)}, u32[]{:S(2)}) collective-permute-start(bf16[112,896]{1,0:T(8,128)(2,1)S(1)} %slice.25), channel_id=1, source_target_pairs={{0,64},{64,128},{128,192},{192,0},{1,65},{65,129},{129,193},{193,1... | collective-permute-start | bytes 602120 | tf_op jit(solution)/shard_map/ppermute | solution.py:408
  68.5 2.6 %copy-start.20 = (bf16[112,896]{1,0:T(8,128)(2,1)}, bf16[112,896]{1,0:T(8,128)(2,1)S(1)}, u32[]{:S(2)}) copy-start(bf16[112,896]{1,0:T(8,128)(2,1)S(1)} %collective-permute-done.10.refs_5_) | copy-start | bytes 602116
  71.1 0.7 copy-start.21
  71.8 3.8 %copy-start.4 = (f32[3,896]{1,0:T(4,128)S(1)}, f32[3,896]{1,0:T(4,128)}, u32[]{:S(2)}) copy-start(f32[3,896]{1,0:T(4,128)} %bias_ref.3) | copy-start | bytes 32260
  75.5 2.2 %collective-permute-start.11 = (bf16[4,560,128]{2,1,0:T(8,128)(2,1)}, bf16[4,560,128]{2,1,0:T(8,128)(2,1)S(1)}, u32[]{:S(2)}, u32[]{:S(2)}) collective-permute-start(bf16[4,560,128]{2,1,0:T(8,128)(2,1)} %get-tuple-element.38), channel_id=1, source_target_pairs={{0,8},{8,0},{1,9},{9,1},{2,10},{10,2},{3,11},{11,3},{4,12},{12,4},... | collective-permute-start | bytes 1720328 | tf_op jit(solution)/shard_map/ppermute | solution.py:178
  76.4 11.5 %collective-permute-start.12 = (bf16[512,256]{1,0:T(8,128)(2,1)}, bf16[512,256]{1,0:T(8,128)(2,1)}, u32[]{:S(2)}, u32[]{:S(2)}) collective-permute-start(bf16[512,256]{1,0:T(8,128)(2,1)} %shard_map.125.own_ref), channel_id=1, source_target_pairs={{0,64},{128,192},{1,65},{129,193},{2,66},{130,194},{3,67},{131,195... | collective-permute-start | bytes 786440 | tf_op jit(solution)/shard_map/ppermute | solution.py:433
  77.7 10.2 %copy-start.1 = (bf16[896,224]{0,1:T(8,128)(2,1)S(1)}, bf16[896,224]{0,1:T(8,128)(2,1)}, u32[]{:S(2)}) copy-start(bf16[896,224]{0,1:T(8,128)(2,1)} %param.16) | copy-start | bytes 1204228
  78.7 15.1 %all-to-all-start.2 = ((bf16[4,560,128]{2,1,0:T(8,128)(2,1)}), bf16[4,560,128]{2,1,0:T(8,128)(2,1)S(1)}, u32[]{:S(2)}, u32[]{:S(2)}) async-start(bf16[4,560,128]{2,1,0:T(8,128)(2,1)} %shard_map.127), calls=%async_computation.2 | async-start | bytes 1146880 | tf_op jit(solution)/shard_map/all_to_all | solution.py:180
  83.1 31.8 %copy-start.9 = (s32[2]{0:T(128)S(1)}, s32[2]{0:T(128)}, u32[]{:S(2)}) copy-start(s32[2]{0:T(128)} %offset_ref.1) | copy-start | bytes 28
  87.9 36.8 %collective-permute-start.16 = (bf16[224,896]{1,0:T(8,128)(2,1)S(1)}, bf16[224,896]{1,0:T(8,128)(2,1)S(1)}, u32[]{:S(2)}, u32[]{:S(2)}) collective-permute-start(bf16[224,896]{1,0:T(8,128)(2,1)S(1)} %bitcast.20), channel_id=1, source_target_pairs={{0,64},{64,128},{128,192},{192,0},{1,65},{65,129},{129,193},{193,1... | collective-permute-start | bytes 1204232 | tf_op jit(solution)/shard_map/ppermute | solution.py:442
  87.9 36.8 %collective-permute-start.17 = (bf16[224,896]{1,0:T(8,128)(2,1)S(1)}, bf16[224,896]{1,0:T(8,128)(2,1)S(1)}, u32[]{:S(2)}, u32[]{:S(2)}) collective-permute-start(bf16[224,896]{1,0:T(8,128)(2,1)S(1)} %bitcast.21), channel_id=1, source_target_pairs={{0,192},{64,0},{128,64},{192,128},{1,193},{65,1},{129,65},{193,129... | collective-permute-start | bytes 1204232 | tf_op jit(solution)/shard_map/ppermute | solution.py:443
  89.9 34.8 %collective-permute-start.18 = (bf16[224,896]{1,0:T(8,128)(2,1)S(1)}, bf16[224,896]{1,0:T(8,128)(2,1)S(1)}, u32[]{:S(2)}, u32[]{:S(2)}) collective-permute-start(bf16[224,896]{1,0:T(8,128)(2,1)S(1)} %bitcast.22), channel_id=1, source_target_pairs={{0,128},{64,192},{128,0},{192,64},{1,129},{65,193},{129,1},{193,65... | collective-permute-start | bytes 1204232 | tf_op jit(solution)/shard_map/ppermute | solution.py:444
  93.8 0.7 copy-start.2
  94.5 20.4 %copy-start.3 = (bf16[512,128]{1,0:T(8,128)(2,1)S(1)}, bf16[512,128]{1,0:T(8,128)(2,1)}, u32[]{:S(2)}) copy-start(bf16[512,128]{1,0:T(8,128)(2,1)} %copy-done.2) | copy-start | bytes 393220
  94.5 30.2 %all-to-all-start.3 = ((bf16[8,64,256]{2,1,0:T(8,128)(2,1)}), bf16[8,64,256]{2,1,0:T(8,128)(2,1)}, u32[]{:S(2)}, u32[]{:S(2)}) async-start(bf16[8,64,256]{2,1,0:T(8,128)(2,1)} %bitcast.6), calls=%async_computation.3 | async-start | bytes 524288 | tf_op jit(solution)/shard_map/all_to_all | solution.py:456
  98.7 20.0 %copy-start.10 = (s32[2]{0:T(128)S(1)}, s32[2]{0:T(128)}, u32[]{:S(2)}) copy-start(s32[2]{0:T(128)} %len_ref.1) | copy-start | bytes 28
  98.8 10.3 %collective-permute-start.13 = (bf16[8,2,16,128]{3,2,1,0:T(8,128)(2,1)S(1)}, bf16[8,2,16,128]{3,2,1,0:T(8,128)(2,1)S(1)}, u32[]{:S(2)}, u32[]{:S(2)}) collective-permute-start(bf16[8,2,16,128]{3,2,1,0:T(8,128)(2,1)S(1)} %get-tuple-element.43), channel_id=1, source_target_pairs={{0,64},{64,128},{128,192},{192,0},{1,65},{65,129},{129,193},{193,1... | collective-permute-start | bytes 196616 | tf_op jit(solution)/shard_map/ppermute | solution.py:423
  102.4 7.8 %collective-permute-start.14 = (bf16[8,2,16,128]{3,2,1,0:T(8,128)(2,1)S(1)}, bf16[8,2,16,128]{3,2,1,0:T(8,128)(2,1)S(1)}, u32[]{:S(2)}, u32[]{:S(2)}) collective-permute-start(bf16[8,2,16,128]{3,2,1,0:T(8,128)(2,1)S(1)} %get-tuple-element.44), channel_id=1, source_target_pairs={{0,192},{64,0},{128,64},{192,128},{1,193},{65,1},{129,65},{193,129... | collective-permute-start | bytes 196616 | tf_op jit(solution)/shard_map/ppermute | solution.py:424
  109.1 5.8 %collective-permute-start.15 = (bf16[8,2,16,128]{3,2,1,0:T(8,128)(2,1)S(1)}, bf16[8,2,16,128]{3,2,1,0:T(8,128)(2,1)S(1)}, u32[]{:S(2)}, u32[]{:S(2)}) collective-permute-start(bf16[8,2,16,128]{3,2,1,0:T(8,128)(2,1)S(1)} %get-tuple-element.45), channel_id=1, source_target_pairs={{0,128},{64,192},{128,0},{192,64},{1,129},{65,193},{129,1},{193,65... | collective-permute-start | bytes 196616 | tf_op jit(solution)/shard_map/ppermute | solution.py:425
  124.7 7.7 %collective-permute-start.19 = (bf16[528,128]{1,0:T(8,128)(2,1)S(1)}, bf16[528,128]{1,0:T(8,128)(2,1)S(1)}, u32[]{:S(2)}, u32[]{:S(2)}) collective-permute-start(bf16[528,128]{1,0:T(8,128)(2,1)S(1)} %shard_map.131.refs_0_), channel_id=1, source_target_pairs={{0,16},{16,32},{32,48},{48,0},{1,17},{17,33},{33,49},{49,1},{2,18}... | collective-permute-start | bytes 405512 | tf_op jit(solution)/shard_map/ppermute | solution.py:472
  126.4 6.0 %collective-permute-start.20 = (bf16[528,128]{1,0:T(8,128)(2,1)S(1)}, bf16[528,128]{1,0:T(8,128)(2,1)S(1)}, u32[]{:S(2)}, u32[]{:S(2)}) collective-permute-start(bf16[528,128]{1,0:T(8,128)(2,1)S(1)} %shard_map.131.refs_0_), channel_id=1, source_target_pairs={{0,48},{16,0},{32,16},{48,32},{1,49},{17,1},{33,17},{49,33},{2,50}... | collective-permute-start | bytes 405512 | tf_op jit(solution)/shard_map/ppermute | solution.py:472
  128.0 6.5 %collective-permute-start.21 = (bf16[528,128]{1,0:T(8,128)(2,1)S(1)}, bf16[528,128]{1,0:T(8,128)(2,1)S(1)}, u32[]{:S(2)}, u32[]{:S(2)}) collective-permute-start(bf16[528,128]{1,0:T(8,128)(2,1)S(1)} %shard_map.131.refs_0_), channel_id=1, source_target_pairs={{0,32},{16,48},{32,0},{48,16},{1,33},{17,49},{33,1},{49,17},{2,34}... | collective-permute-start | bytes 405512 | tf_op jit(solution)/shard_map/ppermute | solution.py:472
  129.9 4.6 %collective-permute-start.22 = (bf16[528,128]{1,0:T(8,128)(2,1)S(1)}, bf16[528,128]{1,0:T(8,128)(2,1)S(1)}, u32[]{:S(2)}, u32[]{:S(2)}) collective-permute-start(bf16[528,128]{1,0:T(8,128)(2,1)S(1)} %shard_map.131.refs_0_), channel_id=1, source_target_pairs={{0,8},{8,0},{1,9},{9,1},{2,10},{10,2},{3,11},{11,3},{4,12},{12,4},... | collective-permute-start | bytes 405512 | tf_op jit(solution)/shard_map/ppermute | solution.py:473
  132.4 2.2 %collective-permute-start.23 = (bf16[528,128]{1,0:T(8,128)(2,1)S(1)}, bf16[528,128]{1,0:T(8,128)(2,1)S(1)}, u32[]{:S(2)}, u32[]{:S(2)}) collective-permute-start(bf16[528,128]{1,0:T(8,128)(2,1)S(1)} %collective-permute-done.19.refs_1_), channel_id=1, source_target_pairs={{0,8},{8,0},{1,9},{9,1},{2,10},{10,2},{3,11},{11,3},{4,12},{12,4},... | collective-permute-start | bytes 405512 | tf_op jit(solution)/shard_map/ppermute | solution.py:473
  132.4 2.2 %collective-permute-start.24 = (bf16[528,128]{1,0:T(8,128)(2,1)S(1)}, bf16[528,128]{1,0:T(8,128)(2,1)S(1)}, u32[]{:S(2)}, u32[]{:S(2)}) collective-permute-start(bf16[528,128]{1,0:T(8,128)(2,1)S(1)} %collective-permute-done.20.refs_2_), channel_id=1, source_target_pairs={{0,8},{8,0},{1,9},{9,1},{2,10},{10,2},{3,11},{11,3},{4,12},{12,4},... | collective-permute-start | bytes 405512 | tf_op jit(solution)/shard_map/ppermute | solution.py:473
  134.5 1.4 collective-permute-start.25
  138.3 36.8 %copy-start.8 = (f32[7168]{0:T(1024)S(1)}, f32[7168]{0:T(1024)}, u32[]{:S(2)}) copy-start(f32[7168]{0:T(1024)} %param.17) | copy-start | bytes 86020
  138.3 36.8 %all-to-all-start.4 = ((bf16[64,8,896]{2,1,0:T(8,128)(2,1)}), bf16[64,8,896]{2,1,0:T(8,128)(2,1)S(1)}, u32[]{:S(2)}, u32[]{:S(2)}) async-start(bf16[64,8,896]{2,1,0:T(8,128)(2,1)} %bitcast.8), calls=%async_computation.4 | async-start | bytes 1835008 | tf_op jit(solution)/shard_map/all_to_all | solution.py:488
  175.3 6.1 %collective-permute-start.26 = (bf16[8,7168]{1,0:T(8,128)(2,1)S(1)}, bf16[8,7168]{1,0:T(8,128)(2,1)S(1)}, u32[]{:S(2)}, u32[]{:S(2)}) collective-permute-start(bf16[8,7168]{1,0:T(8,128)(2,1)S(1)} %shard_map.133.refs_0_), channel_id=1, source_target_pairs={{0,1},{1,2},{2,3},{3,4},{4,5},{5,6},{6,7},{7,0},{8,9},{9,10},{10,1... | collective-permute-start | bytes 344072 | tf_op jit(solution)/shard_map/ppermute | solution.py:500
  177.0 4.8 %collective-permute-start.27 = (bf16[8,7168]{1,0:T(8,128)(2,1)S(1)}, bf16[8,7168]{1,0:T(8,128)(2,1)S(1)}, u32[]{:S(2)}, u32[]{:S(2)}) collective-permute-start(bf16[8,7168]{1,0:T(8,128)(2,1)S(1)} %shard_map.133.refs_0_), channel_id=1, source_target_pairs={{0,7},{1,0},{2,1},{3,2},{4,3},{5,4},{6,5},{7,6},{8,15},{9,8},{10,9... | collective-permute-start | bytes 344072 | tf_op jit(solution)/shard_map/ppermute | solution.py:503
  181.4 6.0 %collective-permute-start.28 = (bf16[8,7168]{1,0:T(8,128)(2,1)S(1)}, bf16[8,7168]{1,0:T(8,128)(2,1)S(1)}, u32[]{:S(2)}, u32[]{:S(2)}) collective-permute-start(bf16[8,7168]{1,0:T(8,128)(2,1)S(1)} %collective-permute-done.26.refs_1_), channel_id=1, source_target_pairs={{0,1},{1,2},{2,3},{3,4},{4,5},{5,6},{6,7},{7,0},{8,9},{9,10},{10,1... | collective-permute-start | bytes 344072 | tf_op jit(solution)/shard_map/ppermute | solution.py:500
  181.8 6.6 %collective-permute-start.29 = (bf16[8,7168]{1,0:T(8,128)(2,1)S(1)}, bf16[8,7168]{1,0:T(8,128)(2,1)S(1)}, u32[]{:S(2)}, u32[]{:S(2)}) collective-permute-start(bf16[8,7168]{1,0:T(8,128)(2,1)S(1)} %collective-permute-done.27.refs_2_), channel_id=1, source_target_pairs={{0,7},{1,0},{2,1},{3,2},{4,3},{5,4},{6,5},{7,6},{8,15},{9,8},{10,9... | collective-permute-start | bytes 344072 | tf_op jit(solution)/shard_map/ppermute | solution.py:503
  187.4 6.1 %collective-permute-start.30 = (bf16[8,7168]{1,0:T(8,128)(2,1)S(1)}, bf16[8,7168]{1,0:T(8,128)(2,1)S(1)}, u32[]{:S(2)}, u32[]{:S(2)}) collective-permute-start(bf16[8,7168]{1,0:T(8,128)(2,1)S(1)} %collective-permute-done.28.refs_3_), channel_id=1, source_target_pairs={{0,1},{1,2},{2,3},{3,4},{4,5},{5,6},{6,7},{7,0},{8,9},{9,10},{10,1... | collective-permute-start | bytes 344072 | tf_op jit(solution)/shard_map/ppermute | solution.py:500
  188.4 5.9 %collective-permute-start.31 = (bf16[8,7168]{1,0:T(8,128)(2,1)S(1)}, bf16[8,7168]{1,0:T(8,128)(2,1)S(1)}, u32[]{:S(2)}, u32[]{:S(2)}) collective-permute-start(bf16[8,7168]{1,0:T(8,128)(2,1)S(1)} %collective-permute-done.29.refs_4_), channel_id=1, source_target_pairs={{0,7},{1,0},{2,1},{3,2},{4,3},{5,4},{6,5},{7,6},{8,15},{9,8},{10,9... | collective-permute-start | bytes 344072 | tf_op jit(solution)/shard_map/ppermute | solution.py:503
  193.5 6.0 %collective-permute-start.32 = (bf16[8,7168]{1,0:T(8,128)(2,1)S(1)}, bf16[8,7168]{1,0:T(8,128)(2,1)S(1)}, u32[]{:S(2)}, u32[]{:S(2)}) collective-permute-start(bf16[8,7168]{1,0:T(8,128)(2,1)S(1)} %collective-permute-done.30.refs_5_), channel_id=1, source_target_pairs={{0,1},{1,2},{2,3},{3,4},{4,5},{5,6},{6,7},{7,0},{8,9},{9,10},{10,1... | collective-permute-start | bytes 344072 | tf_op jit(solution)/shard_map/ppermute | solution.py:500

commit v4 on v3

--- a/solution.py
+++ b/solution.py
@@ -100,6 +100,7 @@
     heads = weight_refs[0].shape[1] // HEAD
     together = 2 // parts
     width = parts * HEAD
+    segments = len(weight_refs) // (XS * parts)
     requests = extra_ref.shape[1] // (parts * GROUP)
 
     def rows_of(step):
@@ -119,8 +120,8 @@
             def wide(index):
                 blocks = []
                 for part, lanes in columns:
-                    held = weight_refs[index * parts + part :]
-                    held = held[:1] if index < XS - 1 or parts > 1 else held
+                    first_ref = (index * parts + part) * segments
+                    held = weight_refs[first_ref : first_ref + segments]
                     blocks.append(jnp.concatenate([ref[:, lanes] for ref in held], axis=0))
                 return jnp.concatenate(blocks, axis=1)
 
@@ -401,12 +402,12 @@
     v_left, v_right = near(v_own)
     k_far = lax.ppermute(k_left, "x", shift(XS, 1))
     v_far = lax.ppermute(v_right, "x", shift(XS, -1))
-    q_own = turned[0]
-    v_left, v_right, q_own = lax.optimization_barrier((v_left, v_right, q_own))
-    q_left, q_right = near(q_own)
+    q_halves = (turned[0, :half], turned[0, half:])
+    v_left, v_right, q_halves = lax.optimization_barrier((v_left, v_right, q_halves))
+    q_lefts, q_rights = zip(*[near(part) for part in q_halves])
     q_fars = (
-        lax.ppermute(q_left[:half], "x", shift(XS, 1)),
-        lax.ppermute(q_right[half:], "x", shift(XS, -1)),
+        lax.ppermute(q_lefts[0], "x", shift(XS, 1)),
+        lax.ppermute(q_rights[1], "x", shift(XS, -1)),
     )
     kv_weights = (k_own, v_own, k_left, v_left, k_right, v_right, k_far, v_far)
 
@@ -432,12 +433,12 @@
     own_kv = in_vmem(finish_kv_kernel, bf16(rows, 2 * HEAD), [], [kv_parts, qkv_bias])
     last_kv = lax.ppermute(own_kv, "x", [(0, 1), (2, 3)])
 
-    q_weights = (q_own, q_left, q_right, *q_fars)
+    q_weights = (*q_halves, *q_lefts, *q_rights, *q_fars)
     q_send, q_keep, _ = project(
         tok_rows, dec_dev, 1, pieces, q_weights, kv_extra
     )
     q_parts = reduce_partial(q_send, q_keep)
-    last_kv, w_out = lax.optimization_barrier((last_kv, w_out))
+    q_fars, w_out = lax.optimization_barrier((q_fars, w_out))
     w_own = w_out.T
     w_left = lax.ppermute(w_own, "x", shift(XS, 1))
     w_right = lax.ppermute(w_own, "x", shift(XS, -1))
@@ -464,11 +465,7 @@
     prefilled, sums = lax.optimization_barrier((prefilled, sums))
     decoded = decode(dec_len, sums, head_bias, dec_cache)
     payload = in_vmem(pack_kernel, bf16(rows + dec_dev * GROUP, HEAD), [], [prefilled, decoded])
-    payload, mine, w_left, w_right, w_far = lax.optimization_barrier(
-        (payload, mine, w_left, w_right, w_far)
-    )
-    new_kv = mine[:heads].reshape(heads, tok_rows, 2, HEAD)
-    new_kv = new_kv.transpose(1, 2, 0, 3).reshape(tok_rows, 2, head_width)
+    payload, w_left, w_right, w_far = lax.optimization_barrier((payload, w_left, w_right, w_far))
     gathered = [payload] + [lax.ppermute(payload, "y", shift(YS, s)) for s in (1, -1, 2)]
     gathered += [lax.ppermute(part, "c", [(0, 1), (1, 0)]) for part in gathered]
     piece = w_own.shape[0]
@@ -483,6 +480,9 @@
             pltpu.VMEM((XS, piece, head_width), jnp.bfloat16),
         ],
     )
+    shares, mine = lax.optimization_barrier((shares, mine))
+    new_kv = mine[:heads].reshape(heads, tok_rows, 2, HEAD)
+    new_kv = new_kv.transpose(1, 2, 0, 3).reshape(tok_rows, 2, head_width)
     slab = tok_rows // ZS
     shares = shares.reshape(GROUP * ZS, slab, XS * piece)
     shares = lax.all_to_all(shares, ("y", "c", "z"), 0, 0, tiled=True)

time: 203 us -> 209 us (1.030)
  starting transfers between devices: 65.4 us -> 74.2 us
  local copies, waits for them, and re-layouts: 11.6 us -> 7.8 us
    ppermute x1, waiting for transfers between devices: 6.5 us -> 17.6 us  [on_device(): lax.ppermute(prior[1], 'x', shift(XS, 1))]
    ppermute x1, waiting for transfers between devices: 4.81 us -> 0.01 us  [on_device(): last_kv = lax.ppermute(own_kv, 'x', [(0, 1), (2, 3)])]
    ppermute x1, waiting for transfers between devices: 0.01 us -> 4.26 us  [on_device(): lax.ppermute(prior[2], 'x', shift(XS, -1))]
    ppermute x3, waiting for transfers between devices: 4.07 us -> 0.13 us  [on_device(): lax.ppermute(payload, 'y', shift(YS, s))]
    ppermute x3 -> x4, waiting for transfers between devices: 11.9 us -> 8.12 us  [near(): return (left, lax.ppermute(value, 'x', shift(XS, -1)))]
    ppermute x1, starting transfers between devices: 1.11 us -> 4.67 us  [on_device(): lax.ppermute(prior[3], 'x', shift(XS, 2))]
    ppermute x2, waiting for transfers between devices: 6.58 us -> 3.18 us  [the longest x1 3.18 us: on_device(): lax.ppermute(q_lefts[0], 'x', shift(XS, 1))]
    ppermute x1, waiting for transfers between devices: 4.64 us -> 2.12 us  [on_device(): lax.ppermute(prior[3], 'x', shift(XS, 2))]
  transfers between devices with their start and end apart: 38 -> 40, of which waited for: 19 -> 21; matrix products, arithmetic and copies ran while one was open for 3% -> 1% of each run, Pallas kernels for 8% -> 10%
where the time goes in v4:
time: 209 us; the launch traced here: 207 us
  waiting for transfers between devices  95 us (45%)
  starting transfers between devices  74.2 us (36%)
  Pallas kernels  28.6 us (14%)
  local copies, waits for them, and re-layouts  7.8 us (4%)
    all_to_all x1, waiting for transfers between devices, on_device(): shares = lax.all_to_all(shares, ('y', 'c', 'z'), 0, 0, tiled=True)  24.9 us
    pallas_call x13, Pallas kernels, in_vmem(): pl.pallas_call(kernel, out_shape=out_shape, in_specs=[pl.BlockSpec(memory...  22.7 us
    ppermute x1, waiting for transfers between devices, on_device(): lax.ppermute(prior[1], 'x', shift(XS, 1))  17.6 us
    ppermute x4, waiting for transfers between devices, on_device(): up = lax.ppermute(up, 'z', shift(ZS, 1))  13.4 us
    all_to_all x1, starting transfers between devices, on_device(): shares = lax.all_to_all(shares, ('y', 'c', 'z'), 0, 0, tiled=True)  10.9 us
    ppermute x4, waiting for transfers between devices, near(): left = lax.ppermute(value, 'x', shift(XS, 1))  9.44 us
    all_to_all x2, starting transfers between devices, reduce_partial(): return lax.all_to_all(partial, 'y', 0, 0, tiled=True)  8.92 us
    ppermute x4, waiting for transfers between devices, near(): return (left, lax.ppermute(value, 'x', shift(XS, -1)))  8.12 us
  transfers between devices with their start and end apart: 40, of which 21 were waited for; matrix products, arithmetic and copies ran while one was open for 1% of the time, Pallas kernels for 10%

profile of v4, /device:TPU:2, one launch (start us, length us, event | category | flops | bytes accessed | tf_op | source)
XLA Modules:
  0.0 206.7 jit_solution(5098588083706549711)
XLA Ops:
  0.6 1.2 copy-done
  1.8 0.9 copy-done.3
  2.7 0.7 copy-done.4
  3.5 0.7 copy-done.5
  4.2 2.4 %shard_map.122 = bf16[8,4,80,224]{3,2,1,0:T(8,128)(2,1)} custom-call(bf16[64,7168]{1,0:T(8,128)(2,1)S(1)} %copy-done, f32[1,7168]{1,0:T(1,128)S(1)} %bitcast.26, f32[1,7168]{1,0:T(1,128)S(1)} %bitcast.27, bf16[16,2,2,896]{3,2,1,0:T(2,128)(2,1)S(1)} %copy-done.3), custom_call_target="tpu_custom_call" | custom-call | tf_op jit(solution)/shard_map/pallas_call | solution.py:31
  6.6 4.6 %all-to-all-start = ((bf16[8,4,80,224]{3,2,1,0:T(8,128)(2,1)}), bf16[8,4,80,224]{3,2,1,0:T(8,128)(2,1)S(1)}, u32[]{:S(2)}, u32[]{:S(2)}) async-start(bf16[8,4,80,224]{3,2,1,0:T(8,128)(2,1)} %shard_map.122), calls=%async_computation | async-start | bytes 2621440 | tf_op jit(solution)/shard_map/all_to_all | solution.py:420
  11.3 1.4 collective-permute-start.2
  12.8 0.7 collective-permute-start
  13.4 1.5 collective-permute-start.1
  14.9 0.5 collective-permute-start.3
  15.5 8.1 %collective-permute-done.2.refs_6_ = bf16[224,896]{1,0:T(8,128)(2,1)S(1)} collective-permute-done((bf16[224,896]{1,0:T(8,128)(2,1)S(1)}, bf16[224,896]{1,0:T(8,128)(2,1)S(1)}, u32[]{:S(2)}, u32[]{:S(2)}) %collective-permute-start.2) | collective-permute-done | bytes 401440 | tf_op jit(solution)/shard_map/ppermute | solution.py:396
  23.6 1.4 collective-permute-start.5
  24.9 0.7 collective-permute-start.4
  25.6 0.8 slice_bitcast_fusion.2
  26.4 7.1 %collective-permute-done.1.refs_4_ = bf16[224,896]{1,0:T(8,128)(2,1)S(1)} collective-permute-done((bf16[224,896]{1,0:T(8,128)(2,1)S(1)}, bf16[224,896]{1,0:T(8,128)(2,1)S(1)}, u32[]{:S(2)}, u32[]{:S(2)}) %collective-permute-start.1) | collective-permute-done | bytes 401440 | tf_op jit(solution)/shard_map/ppermute | solution.py:395
  33.6 6.8 %collective-permute-done.5.refs_8_ = bf16[224,896]{1,0:T(8,128)(2,1)S(1)} collective-permute-done((bf16[224,896]{1,0:T(8,128)(2,1)S(1)}, bf16[224,896]{1,0:T(8,128)(2,1)S(1)}, u32[]{:S(2)}, u32[]{:S(2)}) %collective-permute-start.5) | collective-permute-done | bytes 401440 | tf_op jit(solution)/shard_map/ppermute | solution.py:404
  40.3 0.7 copy-done.18
  41.1 0.6 collective-permute-done.4.refs_7_
  41.7 4.8 %shard_map.123 = (bf16[4,512,256]{2,1,0:T(8,128)(2,1)S(1)}, bf16[4,512,256]{2,1,0:T(8,128)(2,1)S(1)}, f32[8,32,128]{2,1,0:T(8,128)S(1)}) custom-call(bf16[8,4,80,224]{3,2,1,0:T(8,128)(2,1)S(1)} %all-to-all-done.refs_0_.in_ref, bf16[224,896]{1,0:T(8,128)(2,1)} %copy-done.9, bf16[224,896]{1,0:T(8,128)(2,1)} %copy-done.10, bf16[224,896]{1,0:T(8,128)(2,1)} %copy-done.15, ...), custom_call_target="tpu_custom_call" | custom-call | tf_op jit(solution)/shard_map/pallas_call | solution.py:31
  46.6 1.0 collective-permute-start.7
  47.6 2.2 %collective-permute-start.10 = (bf16[112,896]{1,0:T(8,128)(2,1)S(1)}, bf16[112,896]{1,0:T(8,128)(2,1)S(1)}, u32[]{:S(2)}, u32[]{:S(2)}) collective-permute-start(bf16[112,896]{1,0:T(8,128)(2,1)S(1)} %copy-done.12), channel_id=1, source_target_pairs={{0,192},{64,0},{128,64},{192,128},{1,193},{65,1},{129,65},{193,129... | collective-permute-start | bytes 602120 | tf_op jit(solution)/shard_map/ppermute | solution.py:396
  49.7 1.3 shard_map.124
  51.0 4.4 %all-to-all-start.1 = ((bf16[4,512,256]{2,1,0:T(8,128)(2,1)}), bf16[4,512,256]{2,1,0:T(8,128)(2,1)S(1)}, u32[]{:S(2)}, u32[]{:S(2)}) async-start(bf16[4,512,256]{2,1,0:T(8,128)(2,1)} %shard_map.124), calls=%async_computation.1 | async-start | bytes 2097152 | tf_op jit(solution)/shard_map/all_to_all | solution.py:181
  55.8 2.7 %collective-permute-start.9 = (bf16[112,896]{1,0:T(8,128)(2,1)S(1)}, bf16[112,896]{1,0:T(8,128)(2,1)S(1)}, u32[]{:S(2)}, u32[]{:S(2)}) collective-permute-start(bf16[112,896]{1,0:T(8,128)(2,1)S(1)} %copy-done.13), channel_id=1, source_target_pairs={{0,192},{64,0},{128,64},{192,128},{1,193},{65,1},{129,65},{193,129... | collective-permute-start | bytes 602120 | tf_op jit(solution)/shard_map/ppermute | solution.py:396
  58.6 3.5 %collective-permute-start.12 = (bf16[112,896]{1,0:T(8,128)(2,1)S(1)}, bf16[112,896]{1,0:T(8,128)(2,1)S(1)}, u32[]{:S(2)}, u32[]{:S(2)}) collective-permute-start(bf16[112,896]{1,0:T(8,128)(2,1)S(1)} %collective-permute-done.10.refs_6_), channel_id=1, source_target_pairs={{0,192},{64,0},{128,64},{192,128},{1,193},{65,1},{129,65},{193,129... | collective-permute-start | bytes 602120 | tf_op jit(solution)/shard_map/ppermute | solution.py:410
  62.1 2.3 %collective-permute-done.8.refs_4_ = bf16[112,896]{1,0:T(8,128)(2,1)S(1)} collective-permute-done((bf16[112,896]{1,0:T(8,128)(2,1)S(1)}, bf16[112,896]{1,0:T(8,128)(2,1)S(1)}, u32[]{:S(2)}, u32[]{:S(2)}) %collective-permute-start.8) | collective-permute-done | bytes 200736 | tf_op jit(solution)/shard_map/ppermute | solution.py:395
  64.4 3.2 %collective-permute-done.11.refs_7_ = bf16[112,896]{1,0:T(8,128)(2,1)S(1)} collective-permute-done((bf16[112,896]{1,0:T(8,128)(2,1)S(1)}, bf16[112,896]{1,0:T(8,128)(2,1)S(1)}, u32[]{:S(2)}, u32[]{:S(2)}) %collective-permute-start.11) | collective-permute-done | bytes 200736 | tf_op jit(solution)/shard_map/ppermute | solution.py:409
  67.6 0.6 copy-done.23
  68.3 3.6 %shard_map.126 = (bf16[4,560,128]{2,1,0:T(8,128)(2,1)S(1)}, bf16[4,560,128]{2,1,0:T(8,128)(2,1)S(1)}, f32[8,16,128]{2,1,0:T(8,128)}) custom-call(bf16[8,4,80,224]{3,2,1,0:T(8,128)(2,1)S(1)} %all-to-all-done.refs_0_.in_ref, bf16[112,896]{1,0:T(8,128)(2,1)} %get-tuple-element.36.refs_1_, bf16[112,896]{1,0:T(8,128)(2,1)} %get-tuple-element.37.refs_2_, ...), custom_call_target="tpu_custom_call" | custom-call | tf_op jit(solution)/shard_map/pallas_call | solution.py:31
  71.9 2.0 collective-permute-done.13.right_ref
  73.9 0.9 shard_map.127
  74.9 4.5 %all-to-all-start.2 = ((bf16[4,560,128]{2,1,0:T(8,128)(2,1)}), bf16[4,560,128]{2,1,0:T(8,128)(2,1)S(1)}, u32[]{:S(2)}, u32[]{:S(2)}) async-start(bf16[4,560,128]{2,1,0:T(8,128)(2,1)} %shard_map.127), calls=%async_computation.2 | async-start | bytes 1146880 | tf_op jit(solution)/shard_map/all_to_all | solution.py:181
  79.4 2.3 %collective-permute-start.18 = (bf16[224,896]{1,0:T(8,128)(2,1)S(1)}, bf16[224,896]{1,0:T(8,128)(2,1)}, u32[]{:S(2)}, u32[]{:S(2)}) collective-permute-start(bf16[224,896]{1,0:T(8,128)(2,1)S(1)} %bitcast.22), channel_id=1, source_target_pairs={{0,64},{64,128},{128,192},{192,0},{1,65},{65,129},{129,193},{193,1... | collective-permute-start | bytes 1204232 | tf_op jit(solution)/shard_map/ppermute | solution.py:443
  81.7 0.8 collective-permute-start.19
  82.4 3.7 %collective-permute-start.20 = (bf16[224,896]{1,0:T(8,128)(2,1)S(1)}, bf16[224,896]{1,0:T(8,128)(2,1)}, u32[]{:S(2)}, u32[]{:S(2)}) collective-permute-start(bf16[224,896]{1,0:T(8,128)(2,1)S(1)} %bitcast.24), channel_id=1, source_target_pairs={{0,128},{64,192},{128,0},{192,64},{1,129},{65,193},{129,1},{193,65... | collective-permute-start | bytes 1204232 | tf_op jit(solution)/shard_map/ppermute | solution.py:445
  86.1 0.8 shard_map.125.own_ref
  86.9 1.4 collective-permute-start.14
  88.4 1.3 collective-permute-start.15
  89.7 17.6 %collective-permute-done.15.refs_1_ = bf16[8,2,16,128]{3,2,1,0:T(8,128)(2,1)S(1)} collective-permute-done((bf16[8,2,16,128]{3,2,1,0:T(8,128)(2,1)S(1)}, bf16[8,2,16,128]{3,2,1,0:T(8,128)(2,1)S(1)}, u32[]{:S(2)}, u32[]{:S(2)}) %collective-permute-start.15) | collective-permute-done | bytes 65568 | tf_op jit(solution)/shard_map/ppermute | solution.py:424
  107.3 4.3 %collective-permute-done.16.refs_2_ = bf16[8,2,16,128]{3,2,1,0:T(8,128)(2,1)S(1)} collective-permute-done((bf16[8,2,16,128]{3,2,1,0:T(8,128)(2,1)S(1)}, bf16[8,2,16,128]{3,2,1,0:T(8,128)(2,1)S(1)}, u32[]{:S(2)}, u32[]{:S(2)}) %collective-permute-start.16) | collective-permute-done | bytes 65568 | tf_op jit(solution)/shard_map/ppermute | solution.py:425
  111.6 4.7 %collective-permute-start.17 = (bf16[8,2,16,128]{3,2,1,0:T(8,128)(2,1)S(1)}, bf16[8,2,16,128]{3,2,1,0:T(8,128)(2,1)S(1)}, u32[]{:S(2)}, u32[]{:S(2)}) collective-permute-start(bf16[8,2,16,128]{3,2,1,0:T(8,128)(2,1)S(1)} %get-tuple-element.46), channel_id=1, source_target_pairs={{0,128},{64,192},{128,0},{192,64},{1,129},{65,193},{129,1},{193,65... | collective-permute-start | bytes 196616 | tf_op jit(solution)/shard_map/ppermute | solution.py:426
  116.4 2.1 %collective-permute-done.17.refs_3_ = bf16[8,2,16,128]{3,2,1,0:T(8,128)(2,1)S(1)} collective-permute-done((bf16[8,2,16,128]{3,2,1,0:T(8,128)(2,1)S(1)}, bf16[8,2,16,128]{3,2,1,0:T(8,128)(2,1)S(1)}, u32[]{:S(2)}, u32[]{:S(2)}) %collective-permute-start.17) | collective-permute-done | bytes 65568 | tf_op jit(solution)/shard_map/ppermute | solution.py:426
  118.5 3.8 %shard_map.130.prefill_ref = bf16[512,128]{1,0:T(8,128)(2,1)S(1)} custom-call(s32[2]{0:T(128)S(1)} %copy-done.7, bf16[512,128]{1,0:T(8,128)(2,1)S(1)} %get-tuple-element.42.query_ref, bf16[512,256]{1,0:T(8,128)(2,1)} %shard_map.125.own_ref, bf16[512,256]{1,0:T(8,128)(2,1)S(1)} %collective-permute-done.14.last_ref, ...), custom_call_target="tpu_custom_call" | custom-call | tf_op jit(solution)/shard_map/pallas_call | solution.py:31
  122.3 5.9 %decode.1.decode_ref = f32[2,8,128]{2,1,0:T(8,128)S(1)} custom-call(s32[2]{0:T(128)S(1)} %copy-done.8, f32[48,128]{1,0:T(8,128)S(1)} %get-tuple-element.49.sums_ref, f32[3,8,128]{2,1,0:T(8,128)S(1)} %pad.4.bias_ref, bf16[2,1024,2,896]{3,2,1,0:T(2,128)(2,1)} %cache_ref.1), custom_call_target="tpu_custom_call" | custom-call | tf_op jit(solution)/shard_map/decode/pallas_call | solution.py:301
  128.3 1.8 collective-permute-start.21
  130.1 1.5 collective-permute-start.22
  131.6 2.0 collective-permute-start.23
  133.6 3.4 %all-to-all-start.3 = ((bf16[8,64,256]{2,1,0:T(8,128)(2,1)}), bf16[8,64,256]{2,1,0:T(8,128)(2,1)S(1)}, u32[]{:S(2)}, u32[]{:S(2)}) async-start(bf16[8,64,256]{2,1,0:T(8,128)(2,1)} %bitcast.8), calls=%async_computation.3 | async-start | bytes 524288 | tf_op jit(solution)/shard_map/all_to_all | solution.py:457
  139.0 0.4 collective-permute-done.27.refs_7_
  139.5 3.7 %shard_map.132 = bf16[512,896]{1,0:T(8,128)(2,1)} custom-call(bf16[528,128]{1,0:T(8,128)(2,1)S(1)} %shard_map.131.refs_0_, bf16[528,128]{1,0:T(8,128)(2,1)S(1)} %collective-permute-done.21.refs_1_, bf16[528,128]{1,0:T(8,128)(2,1)S(1)} %collective-permute-done.22.refs_2_, bf16[528,128]{1,0:T(8,128)(2,1)S(1)} %collective-permute-done.23.refs_3_, ...), custom_call_target="tpu_custom_call" | custom-call | tf_op jit(solution)/shard_map/pallas_call | solution.py:31
  143.1 1.3 all-to-all-done.3
  144.5 10.9 %all-to-all-start.4 = ((bf16[64,8,896]{2,1,0:T(8,128)(2,1)}), bf16[64,8,896]{2,1,0:T(8,128)(2,1)S(1)}, u32[]{:S(2)}, u32[]{:S(2)}) async-start(bf16[64,8,896]{2,1,0:T(8,128)(2,1)} %bitcast.9), calls=%async_computation.4 | async-start | bytes 1835008 | tf_op jit(solution)/shard_map/all_to_all | solution.py:488
  155.4 0.9 constant_dynamic-slice_fusion.hid_ref
  156.3 24.9 %all-to-all-done.4.in_ref = bf16[64,8,896]{2,1,0:T(8,128)(2,1)S(1)} async-done(((bf16[64,8,896]{2,1,0:T(8,128)(2,1)}), bf16[64,8,896]{2,1,0:T(8,128)(2,1)S(1)}, u32[]{:S(2)}, u32[]{:S(2)}) %all-to-all-start.4) | async-done | bytes 917536 | tf_op jit(solution)/shard_map/all_to_all | solution.py:488
  181.5 1.7 collective-permute-start.28
  183.2 1.6 collective-permute-start.29
  184.8 2.8 %collective-permute-done.28.refs_1_ = bf16[8,7168]{1,0:T(8,128)(2,1)S(1)} collective-permute-done((bf16[8,7168]{1,0:T(8,128)(2,1)S(1)}, bf16[8,7168]{1,0:T(8,128)(2,1)S(1)}, u32[]{:S(2)}, u32[]{:S(2)}) %collective-permute-start.28) | collective-permute-done | bytes 114720 | tf_op jit(solution)/shard_map/ppermute | solution.py:500
  188.0 2.8 %collective-permute-start.31 = (bf16[8,7168]{1,0:T(8,128)(2,1)S(1)}, bf16[8,7168]{1,0:T(8,128)(2,1)S(1)}, u32[]{:S(2)}, u32[]{:S(2)}) collective-permute-start(bf16[8,7168]{1,0:T(8,128)(2,1)S(1)} %collective-permute-done.29.refs_2_), channel_id=1, source_target_pairs={{0,7},{1,0},{2,1},{3,2},{4,3},{5,4},{6,5},{7,6},{8,15},{9,8},{10,9... | collective-permute-start | bytes 344072 | tf_op jit(solution)/shard_map/ppermute | solution.py:503
  190.8 2.8 %collective-permute-done.30.refs_3_ = bf16[8,7168]{1,0:T(8,128)(2,1)S(1)} collective-permute-done((bf16[8,7168]{1,0:T(8,128)(2,1)S(1)}, bf16[8,7168]{1,0:T(8,128)(2,1)S(1)}, u32[]{:S(2)}, u32[]{:S(2)}) %collective-permute-start.30) | collective-permute-done | bytes 114720 | tf_op jit(solution)/shard_map/ppermute | solution.py:500
  193.7 3.3 %collective-permute-start.33 = (bf16[8,7168]{1,0:T(8,128)(2,1)S(1)}, bf16[8,7168]{1,0:T(8,128)(2,1)S(1)}, u32[]{:S(2)}, u32[]{:S(2)}) collective-permute-start(bf16[8,7168]{1,0:T(8,128)(2,1)S(1)} %collective-permute-done.31.refs_4_), channel_id=1, source_target_pairs={{0,7},{1,0},{2,1},{3,2},{4,3},{5,4},{6,5},{7,6},{8,15},{9,8},{10,9... | collective-permute-start | bytes 344072 | tf_op jit(solution)/shard_map/ppermute | solution.py:503
  197.0 2.7 %collective-permute-done.32.refs_5_ = bf16[8,7168]{1,0:T(8,128)(2,1)S(1)} collective-permute-done((bf16[8,7168]{1,0:T(8,128)(2,1)S(1)}, bf16[8,7168]{1,0:T(8,128)(2,1)S(1)}, u32[]{:S(2)}, u32[]{:S(2)}) %collective-permute-start.32) | collective-permute-done | bytes 114720 | tf_op jit(solution)/shard_map/ppermute | solution.py:500
  199.7 0.8 copy_bitcast_fusion
  200.5 5.1 %collective-permute-done.34.refs_7_ = bf16[8,7168]{1,0:T(8,128)(2,1)S(1)} collective-permute-done((bf16[8,7168]{1,0:T(8,128)(2,1)S(1)}, bf16[8,7168]{1,0:T(8,128)(2,1)S(1)}, u32[]{:S(2)}, u32[]{:S(2)}) %collective-permute-start.34) | collective-permute-done | bytes 114720 | tf_op jit(solution)/shard_map/ppermute | solution.py:500
  205.7 1.0 shard_map.134
  (89 shorter events, 3.7 us)
Async XLA Ops:
  0.6 1.2 copy-start
  1.8 0.9 copy-start.3
  2.7 0.7 copy-start.4
  3.5 0.7 copy-start.5
  6.6 4.6 %copy-start.11 = (bf16[224,3,896]{2,0,1:T(8,128)(2,1)S(1)}, bf16[224,3,896]{2,0,1:T(8,128)(2,1)}, u32[]{:S(2)}) copy-start(bf16[224,3,896]{2,0,1:T(8,128)(2,1)} %param.14) | copy-start | bytes 3612676
  6.6 35.1 %all-to-all-start = ((bf16[8,4,80,224]{3,2,1,0:T(8,128)(2,1)}), bf16[8,4,80,224]{3,2,1,0:T(8,128)(2,1)S(1)}, u32[]{:S(2)}, u32[]{:S(2)}) async-start(bf16[8,4,80,224]{3,2,1,0:T(8,128)(2,1)} %shard_map.122), calls=%async_computation | async-start | bytes 2621440 | tf_op jit(solution)/shard_map/all_to_all | solution.py:420
  11.3 30.4 %copy-start.9 = (bf16[224,896]{1,0:T(8,128)(2,1)}, bf16[224,896]{1,0:T(8,128)(2,1)S(1)}, u32[]{:S(2)}) copy-start(bf16[224,896]{1,0:T(8,128)(2,1)S(1)} %slice_bitcast_fusion.refs_1_) | copy-start | bytes 1204228
  11.3 30.4 %copy-start.10 = (bf16[224,896]{1,0:T(8,128)(2,1)}, bf16[224,896]{1,0:T(8,128)(2,1)S(1)}, u32[]{:S(2)}) copy-start(bf16[224,896]{1,0:T(8,128)(2,1)S(1)} %slice_bitcast_fusion.1.refs_2_) | copy-start | bytes 1204228
  11.3 12.2 %collective-permute-start.2 = (bf16[224,896]{1,0:T(8,128)(2,1)S(1)}, bf16[224,896]{1,0:T(8,128)(2,1)S(1)}, u32[]{:S(2)}, u32[]{:S(2)}) collective-permute-start(bf16[224,896]{1,0:T(8,128)(2,1)S(1)} %slice_bitcast_fusion.1.refs_2_), channel_id=1, source_target_pairs={{0,192},{64,0},{128,64},{192,128},{1,193},{65,1},{129,65},{193,129... | collective-permute-start | bytes 1204232 | tf_op jit(solution)/shard_map/ppermute | solution.py:396
  12.8 12.2 %collective-permute-start = (bf16[224,896]{1,0:T(8,128)(2,1)S(1)}, bf16[224,896]{1,0:T(8,128)(2,1)S(1)}, u32[]{:S(2)}, u32[]{:S(2)}) collective-permute-start(bf16[224,896]{1,0:T(8,128)(2,1)S(1)} %slice_bitcast_fusion.refs_1_), channel_id=1, source_target_pairs={{0,64},{64,128},{128,192},{192,0},{1,65},{65,129},{129,193},{193,1... | collective-permute-start | bytes 1204232 | tf_op jit(solution)/shard_map/ppermute | solution.py:395
  13.4 20.1 %collective-permute-start.1 = (bf16[224,896]{1,0:T(8,128)(2,1)S(1)}, bf16[224,896]{1,0:T(8,128)(2,1)S(1)}, u32[]{:S(2)}, u32[]{:S(2)}) collective-permute-start(bf16[224,896]{1,0:T(8,128)(2,1)S(1)} %slice_bitcast_fusion.1.refs_2_), channel_id=1, source_target_pairs={{0,64},{64,128},{128,192},{192,0},{1,65},{65,129},{129,193},{193,1... | collective-permute-start | bytes 1204232 | tf_op jit(solution)/shard_map/ppermute | solution.py:395
  14.9 18.6 %collective-permute-start.3 = (bf16[224,896]{1,0:T(8,128)(2,1)S(1)}, bf16[224,896]{1,0:T(8,128)(2,1)S(1)}, u32[]{:S(2)}, u32[]{:S(2)}) collective-permute-start(bf16[224,896]{1,0:T(8,128)(2,1)S(1)} %slice_bitcast_fusion.refs_1_), channel_id=1, source_target_pairs={{0,192},{64,0},{128,64},{192,128},{1,193},{65,1},{129,65},{193,129... | collective-permute-start | bytes 1204232 | tf_op jit(solution)/shard_map/ppermute | solution.py:396
  23.6 16.7 %copy-start.14 = (bf16[224,896]{1,0:T(8,128)(2,1)}, bf16[224,896]{1,0:T(8,128)(2,1)S(1)}, u32[]{:S(2)}) copy-start(bf16[224,896]{1,0:T(8,128)(2,1)S(1)} %collective-permute-done.2.refs_6_) | copy-start | bytes 1204228
  23.6 16.7 %collective-permute-start.5 = (bf16[224,896]{1,0:T(8,128)(2,1)S(1)}, bf16[224,896]{1,0:T(8,128)(2,1)S(1)}, u32[]{:S(2)}, u32[]{:S(2)}) collective-permute-start(bf16[224,896]{1,0:T(8,128)(2,1)S(1)} %collective-permute-done.2.refs_6_), channel_id=1, source_target_pairs={{0,192},{64,0},{128,64},{192,128},{1,193},{65,1},{129,65},{193,129... | collective-permute-start | bytes 1204232 | tf_op jit(solution)/shard_map/ppermute | solution.py:404
  24.9 15.4 %copy-start.15 = (bf16[224,896]{1,0:T(8,128)(2,1)}, bf16[224,896]{1,0:T(8,128)(2,1)S(1)}, u32[]{:S(2)}) copy-start(bf16[224,896]{1,0:T(8,128)(2,1)S(1)} %collective-permute-done.refs_3_) | copy-start | bytes 1204228
  24.9 16.7 %collective-permute-start.4 = (bf16[224,896]{1,0:T(8,128)(2,1)S(1)}, bf16[224,896]{1,0:T(8,128)(2,1)}, u32[]{:S(2)}, u32[]{:S(2)}) collective-permute-start(bf16[224,896]{1,0:T(8,128)(2,1)S(1)} %collective-permute-done.refs_3_), channel_id=1, source_target_pairs={{0,64},{64,128},{128,192},{192,0},{1,65},{65,129},{129,193},{193,1... | collective-permute-start | bytes 1204232 | tf_op jit(solution)/shard_map/ppermute | solution.py:403
  33.5 6.8 %copy-start.16 = (bf16[224,896]{1,0:T(8,128)(2,1)}, bf16[224,896]{1,0:T(8,128)(2,1)S(1)}, u32[]{:S(2)}) copy-start(bf16[224,896]{1,0:T(8,128)(2,1)S(1)} %collective-permute-done.1.refs_4_) | copy-start | bytes 1204228
  33.5 13.1 %copy-start.13 = (bf16[112,896]{1,0:T(8,128)(2,1)S(1)}, bf16[112,896]{1,0:T(8,128)(2,1)}, u32[]{:S(2)}) copy-start(bf16[112,896]{1,0:T(8,128)(2,1)} %get-tuple-element.36.refs_1_) | copy-start | bytes 602116
  33.5 14.0 %copy-start.12 = (bf16[112,896]{1,0:T(8,128)(2,1)S(1)}, bf16[112,896]{1,0:T(8,128)(2,1)}, u32[]{:S(2)}) copy-start(bf16[112,896]{1,0:T(8,128)(2,1)} %get-tuple-element.37.refs_2_) | copy-start | bytes 602116
  33.5 6.8 %copy-start.17 = (bf16[224,896]{1,0:T(8,128)(2,1)}, bf16[224,896]{1,0:T(8,128)(2,1)S(1)}, u32[]{:S(2)}) copy-start(bf16[224,896]{1,0:T(8,128)(2,1)S(1)} %collective-permute-done.3.refs_5_) | copy-start | bytes 1204228
  40.3 0.7 copy-start.18
  46.5 3.2 %collective-permute-start.6 = (bf16[4,512,256]{2,1,0:T(8,128)(2,1)S(1)}, bf16[4,512,256]{2,1,0:T(8,128)(2,1)S(1)}, u32[]{:S(2)}, u32[]{:S(2)}) collective-permute-start(bf16[4,512,256]{2,1,0:T(8,128)(2,1)S(1)} %get-tuple-element.35), channel_id=1, source_target_pairs={{0,8},{8,0},{1,9},{9,1},{2,10},{10,2},{3,11},{11,3},{4,12},{12,4},... | collective-permute-start | bytes 3145736 | tf_op jit(solution)/shard_map/ppermute | solution.py:179
  46.6 11.9 %collective-permute-start.7 = (bf16[112,896]{1,0:T(8,128)(2,1)S(1)}, bf16[112,896]{1,0:T(8,128)(2,1)S(1)}, u32[]{:S(2)}, u32[]{:S(2)}) collective-permute-start(bf16[112,896]{1,0:T(8,128)(2,1)S(1)} %copy-done.13), channel_id=1, source_target_pairs={{0,64},{64,128},{128,192},{192,0},{1,65},{65,129},{129,193},{193,1... | collective-permute-start | bytes 602120 | tf_op jit(solution)/shard_map/ppermute | solution.py:395
  47.6 11.0 %collective-permute-start.10 = (bf16[112,896]{1,0:T(8,128)(2,1)S(1)}, bf16[112,896]{1,0:T(8,128)(2,1)S(1)}, u32[]{:S(2)}, u32[]{:S(2)}) collective-permute-start(bf16[112,896]{1,0:T(8,128)(2,1)S(1)} %copy-done.12), channel_id=1, source_target_pairs={{0,192},{64,0},{128,64},{192,128},{1,193},{65,1},{129,65},{193,129... | collective-permute-start | bytes 602120 | tf_op jit(solution)/shard_map/ppermute | solution.py:396
  51.0 23.9 %all-to-all-start.1 = ((bf16[4,512,256]{2,1,0:T(8,128)(2,1)}), bf16[4,512,256]{2,1,0:T(8,128)(2,1)S(1)}, u32[]{:S(2)}, u32[]{:S(2)}) async-start(bf16[4,512,256]{2,1,0:T(8,128)(2,1)} %shard_map.124), calls=%async_computation.1 | async-start | bytes 2097152 | tf_op jit(solution)/shard_map/all_to_all | solution.py:181
  55.4 9.0 %collective-permute-start.8 = (bf16[112,896]{1,0:T(8,128)(2,1)S(1)}, bf16[112,896]{1,0:T(8,128)(2,1)S(1)}, u32[]{:S(2)}, u32[]{:S(2)}) collective-permute-start(bf16[112,896]{1,0:T(8,128)(2,1)S(1)} %copy-done.12), channel_id=1, source_target_pairs={{0,64},{64,128},{128,192},{192,0},{1,65},{65,129},{129,193},{193,1... | collective-permute-start | bytes 602120 | tf_op jit(solution)/shard_map/ppermute | solution.py:395
  55.8 8.6 %collective-permute-start.9 = (bf16[112,896]{1,0:T(8,128)(2,1)S(1)}, bf16[112,896]{1,0:T(8,128)(2,1)S(1)}, u32[]{:S(2)}, u32[]{:S(2)}) collective-permute-start(bf16[112,896]{1,0:T(8,128)(2,1)S(1)} %copy-done.13), channel_id=1, source_target_pairs={{0,192},{64,0},{128,64},{192,128},{1,193},{65,1},{129,65},{193,129... | collective-permute-start | bytes 602120 | tf_op jit(solution)/shard_map/ppermute | solution.py:396
  58.6 9.0 %copy-start.19 = (bf16[112,896]{1,0:T(8,128)(2,1)}, bf16[112,896]{1,0:T(8,128)(2,1)S(1)}, u32[]{:S(2)}) copy-start(bf16[112,896]{1,0:T(8,128)(2,1)S(1)} %collective-permute-done.7.refs_3_) | copy-start | bytes 602116
  58.6 9.0 %collective-permute-start.11 = (bf16[112,896]{1,0:T(8,128)(2,1)S(1)}, bf16[112,896]{1,0:T(8,128)(2,1)S(1)}, u32[]{:S(2)}, u32[]{:S(2)}) collective-permute-start(bf16[112,896]{1,0:T(8,128)(2,1)S(1)} %collective-permute-done.7.refs_3_), channel_id=1, source_target_pairs={{0,64},{64,128},{128,192},{192,0},{1,65},{65,129},{129,193},{193,1... | collective-permute-start | bytes 602120 | tf_op jit(solution)/shard_map/ppermute | solution.py:409
  58.6 9.0 %copy-start.20 = (bf16[112,896]{1,0:T(8,128)(2,1)}, bf16[112,896]{1,0:T(8,128)(2,1)S(1)}, u32[]{:S(2)}) copy-start(bf16[112,896]{1,0:T(8,128)(2,1)S(1)} %collective-permute-done.10.refs_6_) | copy-start | bytes 602116
  58.6 9.0 %collective-permute-start.12 = (bf16[112,896]{1,0:T(8,128)(2,1)S(1)}, bf16[112,896]{1,0:T(8,128)(2,1)S(1)}, u32[]{:S(2)}, u32[]{:S(2)}) collective-permute-start(bf16[112,896]{1,0:T(8,128)(2,1)S(1)} %collective-permute-done.10.refs_6_), channel_id=1, source_target_pairs={{0,192},{64,0},{128,64},{192,128},{1,193},{65,1},{129,65},{193,129... | collective-permute-start | bytes 602120 | tf_op jit(solution)/shard_map/ppermute | solution.py:410
  64.4 3.2 %copy-start.21 = (bf16[112,896]{1,0:T(8,128)(2,1)}, bf16[112,896]{1,0:T(8,128)(2,1)S(1)}, u32[]{:S(2)}) copy-start(bf16[112,896]{1,0:T(8,128)(2,1)S(1)} %collective-permute-done.8.refs_4_) | copy-start | bytes 602116
  64.4 3.2 %copy-start.22 = (bf16[112,896]{1,0:T(8,128)(2,1)}, bf16[112,896]{1,0:T(8,128)(2,1)S(1)}, u32[]{:S(2)}) copy-start(bf16[112,896]{1,0:T(8,128)(2,1)S(1)} %collective-permute-done.9.refs_5_) | copy-start | bytes 602116
  67.6 0.8 copy-start.24
  71.9 2.0 collective-permute-start.13
  73.9 5.5 %copy-start.1 = (bf16[896,224]{0,1:T(8,128)(2,1)S(1)}, bf16[896,224]{0,1:T(8,128)(2,1)}, u32[]{:S(2)}) copy-start(bf16[896,224]{0,1:T(8,128)(2,1)} %param.16) | copy-start | bytes 1204228
  73.9 12.2 %copy-start.2 = (f32[3,896]{1,0:T(4,128)S(1)}, f32[3,896]{1,0:T(4,128)}, u32[]{:S(2)}) copy-start(f32[3,896]{1,0:T(4,128)} %bias_ref.3) | copy-start | bytes 32260
  74.9 41.4 %all-to-all-start.2 = ((bf16[4,560,128]{2,1,0:T(8,128)(2,1)}), bf16[4,560,128]{2,1,0:T(8,128)(2,1)S(1)}, u32[]{:S(2)}, u32[]{:S(2)}) async-start(bf16[4,560,128]{2,1,0:T(8,128)(2,1)} %shard_map.127), calls=%async_computation.2 | async-start | bytes 1146880 | tf_op jit(solution)/shard_map/all_to_all | solution.py:181
  79.4 48.9 %collective-permute-start.18 = (bf16[224,896]{1,0:T(8,128)(2,1)S(1)}, bf16[224,896]{1,0:T(8,128)(2,1)}, u32[]{:S(2)}, u32[]{:S(2)}) collective-permute-start(bf16[224,896]{1,0:T(8,128)(2,1)S(1)} %bitcast.22), channel_id=1, source_target_pairs={{0,64},{64,128},{128,192},{192,0},{1,65},{65,129},{129,193},{193,1... | collective-permute-start | bytes 1204232 | tf_op jit(solution)/shard_map/ppermute | solution.py:443
  81.7 46.6 %collective-permute-start.19 = (bf16[224,896]{1,0:T(8,128)(2,1)S(1)}, bf16[224,896]{1,0:T(8,128)(2,1)}, u32[]{:S(2)}, u32[]{:S(2)}) collective-permute-start(bf16[224,896]{1,0:T(8,128)(2,1)S(1)} %bitcast.23), channel_id=1, source_target_pairs={{0,192},{64,0},{128,64},{192,128},{1,193},{65,1},{129,65},{193,129... | collective-permute-start | bytes 1204232 | tf_op jit(solution)/shard_map/ppermute | solution.py:444
  82.4 45.8 %collective-permute-start.20 = (bf16[224,896]{1,0:T(8,128)(2,1)S(1)}, bf16[224,896]{1,0:T(8,128)(2,1)}, u32[]{:S(2)}, u32[]{:S(2)}) collective-permute-start(bf16[224,896]{1,0:T(8,128)(2,1)S(1)} %bitcast.24), channel_id=1, source_target_pairs={{0,128},{64,192},{128,0},{192,64},{1,129},{65,193},{129,1},{193,65... | collective-permute-start | bytes 1204232 | tf_op jit(solution)/shard_map/ppermute | solution.py:445
  86.9 31.6 %copy-start.7 = (s32[2]{0:T(128)S(1)}, s32[2]{0:T(128)}, u32[]{:S(2)}) copy-start(s32[2]{0:T(128)} %offset_ref.1) | copy-start | bytes 28
  86.9 35.4 %copy-start.8 = (s32[2]{0:T(128)S(1)}, s32[2]{0:T(128)}, u32[]{:S(2)}) copy-start(s32[2]{0:T(128)} %len_ref.1) | copy-start | bytes 28
  86.9 31.6 %collective-permute-start.14 = (bf16[512,256]{1,0:T(8,128)(2,1)}, bf16[512,256]{1,0:T(8,128)(2,1)S(1)}, u32[]{:S(2)}, u32[]{:S(2)}) collective-permute-start(bf16[512,256]{1,0:T(8,128)(2,1)} %shard_map.125.own_ref), channel_id=1, source_target_pairs={{0,64},{128,192},{1,65},{129,193},{2,66},{130,194},{3,67},{131,195... | collective-permute-start | bytes 786440 | tf_op jit(solution)/shard_map/ppermute | solution.py:434
  88.4 18.9 %collective-permute-start.15 = (bf16[8,2,16,128]{3,2,1,0:T(8,128)(2,1)S(1)}, bf16[8,2,16,128]{3,2,1,0:T(8,128)(2,1)S(1)}, u32[]{:S(2)}, u32[]{:S(2)}) collective-permute-start(bf16[8,2,16,128]{3,2,1,0:T(8,128)(2,1)S(1)} %get-tuple-element.44), channel_id=1, source_target_pairs={{0,64},{64,128},{128,192},{192,0},{1,65},{65,129},{129,193},{193,1... | collective-permute-start | bytes 196616 | tf_op jit(solution)/shard_map/ppermute | solution.py:424
  107.3 4.3 %collective-permute-start.16 = (bf16[8,2,16,128]{3,2,1,0:T(8,128)(2,1)S(1)}, bf16[8,2,16,128]{3,2,1,0:T(8,128)(2,1)S(1)}, u32[]{:S(2)}, u32[]{:S(2)}) collective-permute-start(bf16[8,2,16,128]{3,2,1,0:T(8,128)(2,1)S(1)} %get-tuple-element.45), channel_id=1, source_target_pairs={{0,192},{64,0},{128,64},{192,128},{1,193},{65,1},{129,65},{193,129... | collective-permute-start | bytes 196616 | tf_op jit(solution)/shard_map/ppermute | solution.py:425
  111.6 6.9 %collective-permute-start.17 = (bf16[8,2,16,128]{3,2,1,0:T(8,128)(2,1)S(1)}, bf16[8,2,16,128]{3,2,1,0:T(8,128)(2,1)S(1)}, u32[]{:S(2)}, u32[]{:S(2)}) collective-permute-start(bf16[8,2,16,128]{3,2,1,0:T(8,128)(2,1)S(1)} %get-tuple-element.46), channel_id=1, source_target_pairs={{0,128},{64,192},{128,0},{192,64},{1,129},{65,193},{129,1},{193,65... | collective-permute-start | bytes 196616 | tf_op jit(solution)/shard_map/ppermute | solution.py:426
  128.3 9.2 %collective-permute-start.21 = (bf16[528,128]{1,0:T(8,128)(2,1)S(1)}, bf16[528,128]{1,0:T(8,128)(2,1)S(1)}, u32[]{:S(2)}, u32[]{:S(2)}) collective-permute-start(bf16[528,128]{1,0:T(8,128)(2,1)S(1)} %shard_map.131.refs_0_), channel_id=1, source_target_pairs={{0,16},{16,32},{32,48},{48,0},{1,17},{17,33},{33,49},{49,1},{2,18}... | collective-permute-start | bytes 405512 | tf_op jit(solution)/shard_map/ppermute | solution.py:469
  130.1 7.6 %collective-permute-start.22 = (bf16[528,128]{1,0:T(8,128)(2,1)S(1)}, bf16[528,128]{1,0:T(8,128)(2,1)S(1)}, u32[]{:S(2)}, u32[]{:S(2)}) collective-permute-start(bf16[528,128]{1,0:T(8,128)(2,1)S(1)} %shard_map.131.refs_0_), channel_id=1, source_target_pairs={{0,48},{16,0},{32,16},{48,32},{1,49},{17,1},{33,17},{49,33},{2,50}... | collective-permute-start | bytes 405512 | tf_op jit(solution)/shard_map/ppermute | solution.py:469
  131.6 6.5 %collective-permute-start.23 = (bf16[528,128]{1,0:T(8,128)(2,1)S(1)}, bf16[528,128]{1,0:T(8,128)(2,1)S(1)}, u32[]{:S(2)}, u32[]{:S(2)}) collective-permute-start(bf16[528,128]{1,0:T(8,128)(2,1)S(1)} %shard_map.131.refs_0_), channel_id=1, source_target_pairs={{0,32},{16,48},{32,0},{48,16},{1,33},{17,49},{33,1},{49,17},{2,34}... | collective-permute-start | bytes 405512 | tf_op jit(solution)/shard_map/ppermute | solution.py:469
  133.6 10.8 %all-to-all-start.3 = ((bf16[8,64,256]{2,1,0:T(8,128)(2,1)}), bf16[8,64,256]{2,1,0:T(8,128)(2,1)S(1)}, u32[]{:S(2)}, u32[]{:S(2)}) async-start(bf16[8,64,256]{2,1,0:T(8,128)(2,1)} %bitcast.8), calls=%async_computation.3 | async-start | bytes 524288 | tf_op jit(solution)/shard_map/all_to_all | solution.py:457
  137.1 1.5 collective-permute-start.24
  137.5 1.4 collective-permute-start.25
  137.7 1.4 collective-permute-start.26
  138.1 1.4 collective-permute-start.27
  143.1 38.1 %copy-start.6 = (f32[7168]{0:T(1024)S(1)}, f32[7168]{0:T(1024)}, u32[]{:S(2)}) copy-start(f32[7168]{0:T(1024)} %param.17) | copy-start | bytes 86020
  144.5 36.8 %all-to-all-start.4 = ((bf16[64,8,896]{2,1,0:T(8,128)(2,1)}), bf16[64,8,896]{2,1,0:T(8,128)(2,1)S(1)}, u32[]{:S(2)}, u32[]{:S(2)}) async-start(bf16[64,8,896]{2,1,0:T(8,128)(2,1)} %bitcast.9), calls=%async_computation.4 | async-start | bytes 1835008 | tf_op jit(solution)/shard_map/all_to_all | solution.py:488
  181.5 6.1 %collective-permute-start.28 = (bf16[8,7168]{1,0:T(8,128)(2,1)S(1)}, bf16[8,7168]{1,0:T(8,128)(2,1)S(1)}, u32[]{:S(2)}, u32[]{:S(2)}) collective-permute-start(bf16[8,7168]{1,0:T(8,128)(2,1)S(1)} %shard_map.133.refs_0_), channel_id=1, source_target_pairs={{0,1},{1,2},{2,3},{3,4},{4,5},{5,6},{6,7},{7,0},{8,9},{9,10},{10,1... | collective-permute-start | bytes 344072 | tf_op jit(solution)/shard_map/ppermute | solution.py:500
  183.2 4.8 %collective-permute-start.29 = (bf16[8,7168]{1,0:T(8,128)(2,1)S(1)}, bf16[8,7168]{1,0:T(8,128)(2,1)S(1)}, u32[]{:S(2)}, u32[]{:S(2)}) collective-permute-start(bf16[8,7168]{1,0:T(8,128)(2,1)S(1)} %shard_map.133.refs_0_), channel_id=1, source_target_pairs={{0,7},{1,0},{2,1},{3,2},{4,3},{5,4},{6,5},{7,6},{8,15},{9,8},{10,9... | collective-permute-start | bytes 344072 | tf_op jit(solution)/shard_map/ppermute | solution.py:503
  187.6 6.0 %collective-permute-start.30 = (bf16[8,7168]{1,0:T(8,128)(2,1)S(1)}, bf16[8,7168]{1,0:T(8,128)(2,1)S(1)}, u32[]{:S(2)}, u32[]{:S(2)}) collective-permute-start(bf16[8,7168]{1,0:T(8,128)(2,1)S(1)} %collective-permute-done.28.refs_1_), channel_id=1, source_target_pairs={{0,1},{1,2},{2,3},{3,4},{4,5},{5,6},{6,7},{7,0},{8,9},{9,10},{10,1... | collective-permute-start | bytes 344072 | tf_op jit(solution)/shard_map/ppermute | solution.py:500
  188.0 5.6 %collective-permute-start.31 = (bf16[8,7168]{1,0:T(8,128)(2,1)S(1)}, bf16[8,7168]{1,0:T(8,128)(2,1)S(1)}, u32[]{:S(2)}, u32[]{:S(2)}) collective-permute-start(bf16[8,7168]{1,0:T(8,128)(2,1)S(1)} %collective-permute-done.29.refs_2_), channel_id=1, source_target_pairs={{0,7},{1,0},{2,1},{3,2},{4,3},{5,4},{6,5},{7,6},{8,15},{9,8},{10,9... | collective-permute-start | bytes 344072 | tf_op jit(solution)/shard_map/ppermute | solution.py:503
  193.6 6.1 %collective-permute-start.32 = (bf16[8,7168]{1,0:T(8,128)(2,1)S(1)}, bf16[8,7168]{1,0:T(8,128)(2,1)S(1)}, u32[]{:S(2)}, u32[]{:S(2)}) collective-permute-start(bf16[8,7168]{1,0:T(8,128)(2,1)S(1)} %collective-permute-done.30.refs_3_), channel_id=1, source_target_pairs={{0,1},{1,2},{2,3},{3,4},{4,5},{5,6},{6,7},{7,0},{8,9},{9,10},{10,1... | collective-permute-start | bytes 344072 | tf_op jit(solution)/shard_map/ppermute | solution.py:500
  193.7 6.9 %collective-permute-start.33 = (bf16[8,7168]{1,0:T(8,128)(2,1)S(1)}, bf16[8,7168]{1,0:T(8,128)(2,1)S(1)}, u32[]{:S(2)}, u32[]{:S(2)}) collective-permute-start(bf16[8,7168]{1,0:T(8,128)(2,1)S(1)} %collective-permute-done.31.refs_4_), channel_id=1, source_target_pairs={{0,7},{1,0},{2,1},{3,2},{4,3},{5,4},{6,5},{7,6},{8,15},{9,8},{10,9... | collective-permute-start | bytes 344072 | tf_op jit(solution)/shard_map/ppermute | solution.py:503
  199.7 6.0 %collective-permute-start.34 = (bf16[8,7168]{1,0:T(8,128)(2,1)S(1)}, bf16[8,7168]{1,0:T(8,128)(2,1)S(1)}, u32[]{:S(2)}, u32[]{:S(2)}) collective-permute-start(bf16[8,7168]{1,0:T(8,128)(2,1)S(1)} %collective-permute-done.32.refs_5_), channel_id=1, source_target_pairs={{0,1},{1,2},{2,3},{3,4},{4,5},{5,6},{6,7},{7,0},{8,9},{9,10},{10,1... | collective-permute-start | bytes 344072 | tf_op jit(solution)/shard_map/ppermute | solution.py:500
  (1 other events, 0.7 us)

commit v5 on v4

--- a/solution.py
+++ b/solution.py
@@ -453,19 +453,17 @@
         [],
         [q_parts, qkv_bias],
     )
-    tied_kv, queries = lax.optimization_barrier((own_kv, queries))
-    mine = lax.all_to_all(tied_kv.reshape(GROUP, tok_rows, 2 * HEAD), ("y", "c"), 0, 0, tiled=True)
     prefilled = in_vmem(
         functools.partial(attend_kernel, pre_dev),
         bf16(rows, HEAD),
         [offsets],
         [queries, own_kv, last_kv, *prior],
+        loaded=range(3, 3 + XS),
     )
     head_bias = jnp.pad(qkv_bias.reshape(3, heads, HEAD), ((0, 0), (0, GROUP - heads), (0, 0)))
     prefilled, sums = lax.optimization_barrier((prefilled, sums))
     decoded = decode(dec_len, sums, head_bias, dec_cache)
     payload = in_vmem(pack_kernel, bf16(rows + dec_dev * GROUP, HEAD), [], [prefilled, decoded])
-    payload, w_left, w_right, w_far = lax.optimization_barrier((payload, w_left, w_right, w_far))
     gathered = [payload] + [lax.ppermute(payload, "y", shift(YS, s)) for s in (1, -1, 2)]
     gathered += [lax.ppermute(part, "c", [(0, 1), (1, 0)]) for part in gathered]
     piece = w_own.shape[0]
@@ -480,9 +478,6 @@
             pltpu.VMEM((XS, piece, head_width), jnp.bfloat16),
         ],
     )
-    shares, mine = lax.optimization_barrier((shares, mine))
-    new_kv = mine[:heads].reshape(heads, tok_rows, 2, HEAD)
-    new_kv = new_kv.transpose(1, 2, 0, 3).reshape(tok_rows, 2, head_width)
     slab = tok_rows // ZS
     shares = shares.reshape(GROUP * ZS, slab, XS * piece)
     shares = lax.all_to_all(shares, ("y", "c", "z"), 0, 0, tiled=True)
@@ -494,6 +489,10 @@
         [shares, residual, out_bias[None]],
         [pltpu.VMEM((slab, width), jnp.float32)],
     )
+    tied_kv, result = lax.optimization_barrier((own_kv, result))
+    mine = lax.all_to_all(tied_kv.reshape(GROUP, tok_rows, 2 * HEAD), ("y", "c"), 0, 0, tiled=True)
+    new_kv = mine[:heads].reshape(heads, tok_rows, 2, HEAD)
+    new_kv = new_kv.transpose(1, 2, 0, 3).reshape(tok_rows, 2, head_width)
     everyone = [result]
     up = down = result
     for step in range(ZS // 2):

time: 209 us -> 203 us (0.971)
  waiting for transfers between devices: 95 us -> 89.9 us
    ppermute x1, waiting for transfers between devices: 17.6 us -> 8.92 us  [on_device(): lax.ppermute(prior[1], 'x', shift(XS, 1))]
    ppermute x1, waiting for transfers between devices: 2.12 us -> 9.11 us  [on_device(): lax.ppermute(prior[3], 'x', shift(XS, 2))]
    ppermute x1, starting transfers between devices: 4.67 us -> 0.1 us  [on_device(): lax.ppermute(prior[3], 'x', shift(XS, 2))]
    ppermute x1, waiting for transfers between devices: 4.26 us -> 0.01 us  [on_device(): lax.ppermute(prior[2], 'x', shift(XS, -1))]
    ppermute x3, waiting for transfers between devices: 0.13 us -> 4.24 us  [on_device(): lax.ppermute(payload, 'y', shift(YS, s))]
    ppermute x1, starting transfers between devices: 1.27 us -> 4.91 us  [on_device(): lax.ppermute(prior[1], 'x', shift(XS, 1))]
    ppermute x4, waiting for transfers between devices: 13.4 us -> 11.3 us  [on_device(): up = lax.ppermute(up, 'z', shift(ZS, 1))]
    unnamed x51 -> x59, local copies, waits for them, and re-layouts: 5.94 us -> 6.58 us
  transfers between devices with their start and end apart: 40 -> 40, of which waited for: 21 -> 16; matrix products, arithmetic and copies ran while one was open for 1% -> 1% of each run, Pallas kernels for 10% -> 8%
where the time goes in v5:
time: 203 us; the launch traced here: 201 us
  waiting for transfers between devices  89.9 us (44%)
  starting transfers between devices  73.5 us (36%)
  Pallas kernels  28.6 us (14%)
  local copies, waits for them, and re-layouts  8.46 us (4%)
    all_to_all x1, waiting for transfers between devices, on_device(): shares = lax.all_to_all(shares, ('y', 'c', 'z'), 0, 0, tiled=True)  24.9 us
    pallas_call x13, Pallas kernels, in_vmem(): pl.pallas_call(kernel, out_shape=out_shape, in_specs=[pl.BlockSpec(memory...  22.7 us
    ppermute x4, waiting for transfers between devices, on_device(): up = lax.ppermute(up, 'z', shift(ZS, 1))  11.3 us
    all_to_all x1, starting transfers between devices, on_device(): shares = lax.all_to_all(shares, ('y', 'c', 'z'), 0, 0, tiled=True)  10.8 us
    ppermute x4, waiting for transfers between devices, near(): left = lax.ppermute(value, 'x', shift(XS, 1))  9.43 us
    ppermute x1, waiting for transfers between devices, on_device(): lax.ppermute(prior[3], 'x', shift(XS, 2))  9.11 us
    all_to_all x2, starting transfers between devices, reduce_partial(): return lax.all_to_all(partial, 'y', 0, 0, tiled=True)  8.92 us
    ppermute x1, waiting for transfers between devices, on_device(): lax.ppermute(prior[1], 'x', shift(XS, 1))  8.92 us
  transfers between devices with their start and end apart: 40, of which 16 were waited for; matrix products, arithmetic and copies ran while one was open for 1% of the time, Pallas kernels for 8%

profile of v5, /device:TPU:2, one launch (start us, length us, event | category | flops | bytes accessed | tf_op | source)
XLA Modules:
  0.0 201.4 jit_solution(16639005380881375584)
XLA Ops:
  0.6 1.2 copy-done
  1.8 0.9 copy-done.3
  2.7 0.7 copy-done.5
  3.5 0.7 copy-done.6
  4.2 2.4 %shard_map.122 = bf16[8,4,80,224]{3,2,1,0:T(8,128)(2,1)} custom-call(bf16[64,7168]{1,0:T(8,128)(2,1)S(1)} %copy-done, f32[1,7168]{1,0:T(1,128)S(1)} %bitcast.26, f32[1,7168]{1,0:T(1,128)S(1)} %bitcast.27, bf16[16,2,2,896]{3,2,1,0:T(2,128)(2,1)S(1)} %copy-done.3), custom_call_target="tpu_custom_call" | custom-call | tf_op jit(solution)/shard_map/pallas_call | solution.py:31
  6.6 4.6 %all-to-all-start = ((bf16[8,4,80,224]{3,2,1,0:T(8,128)(2,1)}), bf16[8,4,80,224]{3,2,1,0:T(8,128)(2,1)S(1)}, u32[]{:S(2)}, u32[]{:S(2)}) async-start(bf16[8,4,80,224]{3,2,1,0:T(8,128)(2,1)} %shard_map.122), calls=%async_computation | async-start | bytes 2621440 | tf_op jit(solution)/shard_map/all_to_all | solution.py:420
  11.3 1.4 collective-permute-start.2
  12.8 0.7 collective-permute-start
  13.4 1.5 collective-permute-start.1
  14.9 0.5 collective-permute-start.3
  15.5 8.1 %collective-permute-done.2.refs_6_ = bf16[224,896]{1,0:T(8,128)(2,1)S(1)} collective-permute-done((bf16[224,896]{1,0:T(8,128)(2,1)S(1)}, bf16[224,896]{1,0:T(8,128)(2,1)S(1)}, u32[]{:S(2)}, u32[]{:S(2)}) %collective-permute-start.2) | collective-permute-done | bytes 401440 | tf_op jit(solution)/shard_map/ppermute | solution.py:396
  23.6 1.4 collective-permute-start.5
  24.9 0.7 collective-permute-start.4
  25.6 0.8 slice_bitcast_fusion.2
  26.4 7.1 %collective-permute-done.1.refs_4_ = bf16[224,896]{1,0:T(8,128)(2,1)S(1)} collective-permute-done((bf16[224,896]{1,0:T(8,128)(2,1)S(1)}, bf16[224,896]{1,0:T(8,128)(2,1)S(1)}, u32[]{:S(2)}, u32[]{:S(2)}) %collective-permute-start.1) | collective-permute-done | bytes 401440 | tf_op jit(solution)/shard_map/ppermute | solution.py:395
  33.5 6.8 %collective-permute-done.5.refs_8_ = bf16[224,896]{1,0:T(8,128)(2,1)S(1)} collective-permute-done((bf16[224,896]{1,0:T(8,128)(2,1)S(1)}, bf16[224,896]{1,0:T(8,128)(2,1)S(1)}, u32[]{:S(2)}, u32[]{:S(2)}) %collective-permute-start.5) | collective-permute-done | bytes 401440 | tf_op jit(solution)/shard_map/ppermute | solution.py:404
  40.3 0.8 copy-done.19
  41.1 0.6 collective-permute-done.4.refs_7_
  41.7 4.8 %shard_map.123 = (bf16[4,512,256]{2,1,0:T(8,128)(2,1)S(1)}, bf16[4,512,256]{2,1,0:T(8,128)(2,1)S(1)}, f32[8,32,128]{2,1,0:T(8,128)S(1)}) custom-call(bf16[8,4,80,224]{3,2,1,0:T(8,128)(2,1)S(1)} %all-to-all-done.refs_0_.in_ref, bf16[224,896]{1,0:T(8,128)(2,1)} %copy-done.10, bf16[224,896]{1,0:T(8,128)(2,1)} %copy-done.11, bf16[224,896]{1,0:T(8,128)(2,1)} %copy-done.16, ...), custom_call_target="tpu_custom_call" | custom-call | tf_op jit(solution)/shard_map/pallas_call | solution.py:31
  46.6 1.0 collective-permute-start.7
  47.6 2.1 %collective-permute-start.10 = (bf16[112,896]{1,0:T(8,128)(2,1)S(1)}, bf16[112,896]{1,0:T(8,128)(2,1)S(1)}, u32[]{:S(2)}, u32[]{:S(2)}) collective-permute-start(bf16[112,896]{1,0:T(8,128)(2,1)S(1)} %copy-done.13), channel_id=1, source_target_pairs={{0,192},{64,0},{128,64},{192,128},{1,193},{65,1},{129,65},{193,129... | collective-permute-start | bytes 602120 | tf_op jit(solution)/shard_map/ppermute | solution.py:396
  49.7 1.2 shard_map.124
  51.0 4.4 %all-to-all-start.1 = ((bf16[4,512,256]{2,1,0:T(8,128)(2,1)}), bf16[4,512,256]{2,1,0:T(8,128)(2,1)S(1)}, u32[]{:S(2)}, u32[]{:S(2)}) async-start(bf16[4,512,256]{2,1,0:T(8,128)(2,1)} %shard_map.124), calls=%async_computation.1 | async-start | bytes 2097152 | tf_op jit(solution)/shard_map/all_to_all | solution.py:181
  55.8 2.7 %collective-permute-start.9 = (bf16[112,896]{1,0:T(8,128)(2,1)S(1)}, bf16[112,896]{1,0:T(8,128)(2,1)S(1)}, u32[]{:S(2)}, u32[]{:S(2)}) collective-permute-start(bf16[112,896]{1,0:T(8,128)(2,1)S(1)} %copy-done.14), channel_id=1, source_target_pairs={{0,192},{64,0},{128,64},{192,128},{1,193},{65,1},{129,65},{193,129... | collective-permute-start | bytes 602120 | tf_op jit(solution)/shard_map/ppermute | solution.py:396
  58.6 3.5 %collective-permute-start.12 = (bf16[112,896]{1,0:T(8,128)(2,1)S(1)}, bf16[112,896]{1,0:T(8,128)(2,1)S(1)}, u32[]{:S(2)}, u32[]{:S(2)}) collective-permute-start(bf16[112,896]{1,0:T(8,128)(2,1)S(1)} %collective-permute-done.10.refs_6_), channel_id=1, source_target_pairs={{0,192},{64,0},{128,64},{192,128},{1,193},{65,1},{129,65},{193,129... | collective-permute-start | bytes 602120 | tf_op jit(solution)/shard_map/ppermute | solution.py:410
  62.0 2.3 %collective-permute-done.8.refs_4_ = bf16[112,896]{1,0:T(8,128)(2,1)S(1)} collective-permute-done((bf16[112,896]{1,0:T(8,128)(2,1)S(1)}, bf16[112,896]{1,0:T(8,128)(2,1)S(1)}, u32[]{:S(2)}, u32[]{:S(2)}) %collective-permute-start.8) | collective-permute-done | bytes 200736 | tf_op jit(solution)/shard_map/ppermute | solution.py:395
  64.4 3.2 %collective-permute-done.11.refs_7_ = bf16[112,896]{1,0:T(8,128)(2,1)S(1)} collective-permute-done((bf16[112,896]{1,0:T(8,128)(2,1)S(1)}, bf16[112,896]{1,0:T(8,128)(2,1)S(1)}, u32[]{:S(2)}, u32[]{:S(2)}) %collective-permute-start.11) | collective-permute-done | bytes 200736 | tf_op jit(solution)/shard_map/ppermute | solution.py:409
  67.6 0.6 copy-done.24
  68.3 3.6 %shard_map.126 = (bf16[4,560,128]{2,1,0:T(8,128)(2,1)S(1)}, bf16[4,560,128]{2,1,0:T(8,128)(2,1)S(1)}, f32[8,16,128]{2,1,0:T(8,128)}) custom-call(bf16[8,4,80,224]{3,2,1,0:T(8,128)(2,1)S(1)} %all-to-all-done.refs_0_.in_ref, bf16[112,896]{1,0:T(8,128)(2,1)} %get-tuple-element.30.refs_1_, bf16[112,896]{1,0:T(8,128)(2,1)} %get-tuple-element.31.refs_2_, ...), custom_call_target="tpu_custom_call" | custom-call | tf_op jit(solution)/shard_map/pallas_call | solution.py:31
  71.9 2.0 collective-permute-done.13.right_ref
  73.9 0.9 shard_map.127
  74.9 4.5 %all-to-all-start.2 = ((bf16[4,560,128]{2,1,0:T(8,128)(2,1)}), bf16[4,560,128]{2,1,0:T(8,128)(2,1)S(1)}, u32[]{:S(2)}, u32[]{:S(2)}) async-start(bf16[4,560,128]{2,1,0:T(8,128)(2,1)} %shard_map.127), calls=%async_computation.2 | async-start | bytes 1146880 | tf_op jit(solution)/shard_map/all_to_all | solution.py:181
  79.4 2.3 %collective-permute-start.25 = (bf16[224,896]{1,0:T(8,128)(2,1)S(1)}, bf16[224,896]{1,0:T(8,128)(2,1)}, u32[]{:S(2)}, u32[]{:S(2)}) collective-permute-start(bf16[224,896]{1,0:T(8,128)(2,1)S(1)} %bitcast.22), channel_id=1, source_target_pairs={{0,64},{64,128},{128,192},{192,0},{1,65},{65,129},{129,193},{193,1... | collective-permute-start | bytes 1204232 | tf_op jit(solution)/shard_map/ppermute | solution.py:443
  81.6 0.8 collective-permute-start.26
  82.4 0.9 shard_map.125.own_ref
  83.3 1.4 collective-permute-start.14
  84.8 4.9 %collective-permute-start.15 = (bf16[8,2,16,128]{3,2,1,0:T(8,128)(2,1)S(1)}, bf16[8,2,16,128]{3,2,1,0:T(8,128)(2,1)S(1)}, u32[]{:S(2)}, u32[]{:S(2)}) collective-permute-start(bf16[8,2,16,128]{3,2,1,0:T(8,128)(2,1)S(1)} %get-tuple-element.37), channel_id=1, source_target_pairs={{0,64},{64,128},{128,192},{192,0},{1,65},{65,129},{129,193},{193,1... | collective-permute-start | bytes 196616 | tf_op jit(solution)/shard_map/ppermute | solution.py:424
  89.7 8.9 %collective-permute-done.15.refs_1_ = bf16[8,2,16,128]{3,2,1,0:T(8,128)(2,1)S(1)} collective-permute-done((bf16[8,2,16,128]{3,2,1,0:T(8,128)(2,1)S(1)}, bf16[8,2,16,128]{3,2,1,0:T(8,128)(2,1)S(1)}, u32[]{:S(2)}, u32[]{:S(2)}) %collective-permute-start.15) | collective-permute-done | bytes 65568 | tf_op jit(solution)/shard_map/ppermute | solution.py:424
  98.7 4.0 %collective-permute-start.27 = (bf16[224,896]{1,0:T(8,128)(2,1)S(1)}, bf16[224,896]{1,0:T(8,128)(2,1)S(1)}, u32[]{:S(2)}, u32[]{:S(2)}) collective-permute-start(bf16[224,896]{1,0:T(8,128)(2,1)S(1)} %bitcast.24), channel_id=1, source_target_pairs={{0,128},{64,192},{128,0},{192,64},{1,129},{65,193},{129,1},{193,65... | collective-permute-start | bytes 1204232 | tf_op jit(solution)/shard_map/ppermute | solution.py:445
  102.9 9.1 %collective-permute-done.17.refs_3_ = bf16[8,2,16,128]{3,2,1,0:T(8,128)(2,1)S(1)} collective-permute-done((bf16[8,2,16,128]{3,2,1,0:T(8,128)(2,1)S(1)}, bf16[8,2,16,128]{3,2,1,0:T(8,128)(2,1)S(1)}, u32[]{:S(2)}, u32[]{:S(2)}) %collective-permute-start.17) | collective-permute-done | bytes 65568 | tf_op jit(solution)/shard_map/ppermute | solution.py:426
  112.1 0.6 copy-done.28
  112.7 3.9 %shard_map.130.prefill_ref = bf16[512,128]{1,0:T(8,128)(2,1)S(1)} custom-call(s32[2]{0:T(128)S(1)} %copy-done.8, bf16[512,128]{1,0:T(8,128)(2,1)S(1)} %get-tuple-element.35.query_ref, bf16[512,256]{1,0:T(8,128)(2,1)} %shard_map.125.own_ref, bf16[512,256]{1,0:T(8,128)(2,1)S(1)} %collective-permute-done.14.last_ref, bf16[8,2,16,128]{3,2,1,0:T(8,128)(2,1)} %copy-done.4, ...), custom_call_target="tpu_custom_call" | custom-call | tf_op jit(solution)/shard_map/pallas_call | solution.py:31
  116.6 5.9 %decode.1.decode_ref = f32[2,8,128]{2,1,0:T(8,128)S(1)} custom-call(s32[2]{0:T(128)S(1)} %copy-done.9, f32[48,128]{1,0:T(8,128)S(1)} %get-tuple-element.42.sums_ref, f32[3,8,128]{2,1,0:T(8,128)S(1)} %pad.4.bias_ref, bf16[2,1024,2,896]{3,2,1,0:T(2,128)(2,1)} %cache_ref.1), custom_call_target="tpu_custom_call" | custom-call | tf_op jit(solution)/shard_map/decode/pallas_call | solution.py:301
  122.5 1.5 collective-permute-start.18
  124.0 1.8 collective-permute-start.19
  125.8 1.8 collective-permute-start.20
  127.6 2.6 %collective-permute-done.18.refs_1_ = bf16[528,128]{1,0:T(8,128)(2,1)S(1)} collective-permute-done((bf16[528,128]{1,0:T(8,128)(2,1)S(1)}, bf16[528,128]{1,0:T(8,128)(2,1)S(1)}, u32[]{:S(2)}, u32[]{:S(2)}) %collective-permute-start.18) | collective-permute-done | bytes 135200 | tf_op jit(solution)/shard_map/ppermute | solution.py:467
  130.7 1.7 collective-permute-done.20.refs_3_
  132.4 1.3 collective-permute-done.24.refs_7_
  133.7 3.6 %shard_map.132 = bf16[512,896]{1,0:T(8,128)(2,1)} custom-call(bf16[528,128]{1,0:T(8,128)(2,1)S(1)} %shard_map.131.refs_0_, bf16[528,128]{1,0:T(8,128)(2,1)S(1)} %collective-permute-done.18.refs_1_, bf16[528,128]{1,0:T(8,128)(2,1)S(1)} %collective-permute-done.19.refs_2_, bf16[528,128]{1,0:T(8,128)(2,1)S(1)} %collective-permute-done.20.refs_3_, ...), custom_call_target="tpu_custom_call" | custom-call | tf_op jit(solution)/shard_map/pallas_call | solution.py:31
  137.3 10.8 %all-to-all-start.3 = ((bf16[64,8,896]{2,1,0:T(8,128)(2,1)}), bf16[64,8,896]{2,1,0:T(8,128)(2,1)S(1)}, u32[]{:S(2)}, u32[]{:S(2)}) async-start(bf16[64,8,896]{2,1,0:T(8,128)(2,1)} %bitcast.8), calls=%async_computation.3 | async-start | bytes 1835008 | tf_op jit(solution)/shard_map/all_to_all | solution.py:483
  148.1 0.9 constant_dynamic-slice_fusion.hid_ref
  149.0 24.9 %all-to-all-done.3.in_ref = bf16[64,8,896]{2,1,0:T(8,128)(2,1)S(1)} async-done(((bf16[64,8,896]{2,1,0:T(8,128)(2,1)}), bf16[64,8,896]{2,1,0:T(8,128)(2,1)S(1)}, u32[]{:S(2)}, u32[]{:S(2)}) %all-to-all-start.3) | async-done | bytes 917536 | tf_op jit(solution)/shard_map/all_to_all | solution.py:483
  174.1 1.7 collective-permute-start.28
  175.8 1.6 collective-permute-start.29
  177.4 4.2 %all-to-all-start.4 = ((bf16[8,64,256]{2,1,0:T(8,128)(2,1)}), bf16[8,64,256]{2,1,0:T(8,128)(2,1)S(1)}, u32[]{:S(2)}, u32[]{:S(2)}) async-start(bf16[8,64,256]{2,1,0:T(8,128)(2,1)} %bitcast.11), calls=%async_computation.4 | async-start | bytes 524288 | tf_op jit(solution)/shard_map/all_to_all | solution.py:493
  181.6 0.5 collective-permute-start.30
  182.1 2.8 %collective-permute-start.31 = (bf16[8,7168]{1,0:T(8,128)(2,1)S(1)}, bf16[8,7168]{1,0:T(8,128)(2,1)S(1)}, u32[]{:S(2)}, u32[]{:S(2)}) collective-permute-start(bf16[8,7168]{1,0:T(8,128)(2,1)S(1)} %collective-permute-done.29.refs_2_), channel_id=1, source_target_pairs={{0,7},{1,0},{2,1},{3,2},{4,3},{5,4},{6,5},{7,6},{8,15},{9,8},{10,9... | collective-permute-start | bytes 344072 | tf_op jit(solution)/shard_map/ppermute | solution.py:502
  184.9 3.4 %collective-permute-done.30.refs_3_ = bf16[8,7168]{1,0:T(8,128)(2,1)S(1)} collective-permute-done((bf16[8,7168]{1,0:T(8,128)(2,1)S(1)}, bf16[8,7168]{1,0:T(8,128)(2,1)S(1)}, u32[]{:S(2)}, u32[]{:S(2)}) %collective-permute-start.30) | collective-permute-done | bytes 114720 | tf_op jit(solution)/shard_map/ppermute | solution.py:499
  188.4 3.2 %collective-permute-start.33 = (bf16[8,7168]{1,0:T(8,128)(2,1)S(1)}, bf16[8,7168]{1,0:T(8,128)(2,1)S(1)}, u32[]{:S(2)}, u32[]{:S(2)}) collective-permute-start(bf16[8,7168]{1,0:T(8,128)(2,1)S(1)} %collective-permute-done.31.refs_4_), channel_id=1, source_target_pairs={{0,7},{1,0},{2,1},{3,2},{4,3},{5,4},{6,5},{7,6},{8,15},{9,8},{10,9... | collective-permute-start | bytes 344072 | tf_op jit(solution)/shard_map/ppermute | solution.py:502
  191.7 2.7 %collective-permute-done.32.refs_5_ = bf16[8,7168]{1,0:T(8,128)(2,1)S(1)} collective-permute-done((bf16[8,7168]{1,0:T(8,128)(2,1)S(1)}, bf16[8,7168]{1,0:T(8,128)(2,1)S(1)}, u32[]{:S(2)}, u32[]{:S(2)}) %collective-permute-start.32) | collective-permute-done | bytes 114720 | tf_op jit(solution)/shard_map/ppermute | solution.py:499
  194.4 0.8 copy_bitcast_fusion
  195.2 5.1 %collective-permute-done.34.refs_7_ = bf16[8,7168]{1,0:T(8,128)(2,1)S(1)} collective-permute-done((bf16[8,7168]{1,0:T(8,128)(2,1)S(1)}, bf16[8,7168]{1,0:T(8,128)(2,1)S(1)}, u32[]{:S(2)}, u32[]{:S(2)}) %collective-permute-start.34) | collective-permute-done | bytes 114720 | tf_op jit(solution)/shard_map/ppermute | solution.py:499
  200.4 1.0 shard_map.134
  (97 shorter events, 1.9 us)
Async XLA Ops:
  0.6 1.2 copy-start
  1.8 0.9 copy-start.3
  6.6 4.6 %copy-start.12 = (bf16[224,3,896]{2,0,1:T(8,128)(2,1)S(1)}, bf16[224,3,896]{2,0,1:T(8,128)(2,1)}, u32[]{:S(2)}) copy-start(bf16[224,3,896]{2,0,1:T(8,128)(2,1)} %param.14) | copy-start | bytes 3612676
  6.6 35.1 %all-to-all-start = ((bf16[8,4,80,224]{3,2,1,0:T(8,128)(2,1)}), bf16[8,4,80,224]{3,2,1,0:T(8,128)(2,1)S(1)}, u32[]{:S(2)}, u32[]{:S(2)}) async-start(bf16[8,4,80,224]{3,2,1,0:T(8,128)(2,1)} %shard_map.122), calls=%async_computation | async-start | bytes 2621440 | tf_op jit(solution)/shard_map/all_to_all | solution.py:420
  11.3 30.4 %copy-start.10 = (bf16[224,896]{1,0:T(8,128)(2,1)}, bf16[224,896]{1,0:T(8,128)(2,1)S(1)}, u32[]{:S(2)}) copy-start(bf16[224,896]{1,0:T(8,128)(2,1)S(1)} %slice_bitcast_fusion.refs_1_) | copy-start | bytes 1204228
  11.3 30.4 %copy-start.11 = (bf16[224,896]{1,0:T(8,128)(2,1)}, bf16[224,896]{1,0:T(8,128)(2,1)S(1)}, u32[]{:S(2)}) copy-start(bf16[224,896]{1,0:T(8,128)(2,1)S(1)} %slice_bitcast_fusion.1.refs_2_) | copy-start | bytes 1204228
  11.3 12.2 %collective-permute-start.2 = (bf16[224,896]{1,0:T(8,128)(2,1)S(1)}, bf16[224,896]{1,0:T(8,128)(2,1)S(1)}, u32[]{:S(2)}, u32[]{:S(2)}) collective-permute-start(bf16[224,896]{1,0:T(8,128)(2,1)S(1)} %slice_bitcast_fusion.1.refs_2_), channel_id=1, source_target_pairs={{0,192},{64,0},{128,64},{192,128},{1,193},{65,1},{129,65},{193,129... | collective-permute-start | bytes 1204232 | tf_op jit(solution)/shard_map/ppermute | solution.py:396
  12.8 12.2 %collective-permute-start = (bf16[224,896]{1,0:T(8,128)(2,1)S(1)}, bf16[224,896]{1,0:T(8,128)(2,1)S(1)}, u32[]{:S(2)}, u32[]{:S(2)}) collective-permute-start(bf16[224,896]{1,0:T(8,128)(2,1)S(1)} %slice_bitcast_fusion.refs_1_), channel_id=1, source_target_pairs={{0,64},{64,128},{128,192},{192,0},{1,65},{65,129},{129,193},{193,1... | collective-permute-start | bytes 1204232 | tf_op jit(solution)/shard_map/ppermute | solution.py:395
  13.4 20.1 %collective-permute-start.1 = (bf16[224,896]{1,0:T(8,128)(2,1)S(1)}, bf16[224,896]{1,0:T(8,128)(2,1)S(1)}, u32[]{:S(2)}, u32[]{:S(2)}) collective-permute-start(bf16[224,896]{1,0:T(8,128)(2,1)S(1)} %slice_bitcast_fusion.1.refs_2_), channel_id=1, source_target_pairs={{0,64},{64,128},{128,192},{192,0},{1,65},{65,129},{129,193},{193,1... | collective-permute-start | bytes 1204232 | tf_op jit(solution)/shard_map/ppermute | solution.py:395
  14.9 18.6 %collective-permute-start.3 = (bf16[224,896]{1,0:T(8,128)(2,1)S(1)}, bf16[224,896]{1,0:T(8,128)(2,1)S(1)}, u32[]{:S(2)}, u32[]{:S(2)}) collective-permute-start(bf16[224,896]{1,0:T(8,128)(2,1)S(1)} %slice_bitcast_fusion.refs_1_), channel_id=1, source_target_pairs={{0,192},{64,0},{128,64},{192,128},{1,193},{65,1},{129,65},{193,129... | collective-permute-start | bytes 1204232 | tf_op jit(solution)/shard_map/ppermute | solution.py:396
  23.6 16.7 %copy-start.15 = (bf16[224,896]{1,0:T(8,128)(2,1)}, bf16[224,896]{1,0:T(8,128)(2,1)S(1)}, u32[]{:S(2)}) copy-start(bf16[224,896]{1,0:T(8,128)(2,1)S(1)} %collective-permute-done.2.refs_6_) | copy-start | bytes 1204228
  23.6 16.7 %collective-permute-start.5 = (bf16[224,896]{1,0:T(8,128)(2,1)S(1)}, bf16[224,896]{1,0:T(8,128)(2,1)S(1)}, u32[]{:S(2)}, u32[]{:S(2)}) collective-permute-start(bf16[224,896]{1,0:T(8,128)(2,1)S(1)} %collective-permute-done.2.refs_6_), channel_id=1, source_target_pairs={{0,192},{64,0},{128,64},{192,128},{1,193},{65,1},{129,65},{193,129... | collective-permute-start | bytes 1204232 | tf_op jit(solution)/shard_map/ppermute | solution.py:404
  24.9 15.4 %copy-start.16 = (bf16[224,896]{1,0:T(8,128)(2,1)}, bf16[224,896]{1,0:T(8,128)(2,1)S(1)}, u32[]{:S(2)}) copy-start(bf16[224,896]{1,0:T(8,128)(2,1)S(1)} %collective-permute-done.refs_3_) | copy-start | bytes 1204228
  24.9 16.7 %collective-permute-start.4 = (bf16[224,896]{1,0:T(8,128)(2,1)S(1)}, bf16[224,896]{1,0:T(8,128)(2,1)}, u32[]{:S(2)}, u32[]{:S(2)}) collective-permute-start(bf16[224,896]{1,0:T(8,128)(2,1)S(1)} %collective-permute-done.refs_3_), channel_id=1, source_target_pairs={{0,64},{64,128},{128,192},{192,0},{1,65},{65,129},{129,193},{193,1... | collective-permute-start | bytes 1204232 | tf_op jit(solution)/shard_map/ppermute | solution.py:403
  33.5 6.8 %copy-start.17 = (bf16[224,896]{1,0:T(8,128)(2,1)}, bf16[224,896]{1,0:T(8,128)(2,1)S(1)}, u32[]{:S(2)}) copy-start(bf16[224,896]{1,0:T(8,128)(2,1)S(1)} %collective-permute-done.1.refs_4_) | copy-start | bytes 1204228
  33.5 13.1 %copy-start.14 = (bf16[112,896]{1,0:T(8,128)(2,1)S(1)}, bf16[112,896]{1,0:T(8,128)(2,1)}, u32[]{:S(2)}) copy-start(bf16[112,896]{1,0:T(8,128)(2,1)} %get-tuple-element.30.refs_1_) | copy-start | bytes 602116
  33.5 14.1 %copy-start.13 = (bf16[112,896]{1,0:T(8,128)(2,1)S(1)}, bf16[112,896]{1,0:T(8,128)(2,1)}, u32[]{:S(2)}) copy-start(bf16[112,896]{1,0:T(8,128)(2,1)} %get-tuple-element.31.refs_2_) | copy-start | bytes 602116
  33.5 6.8 %copy-start.18 = (bf16[224,896]{1,0:T(8,128)(2,1)}, bf16[224,896]{1,0:T(8,128)(2,1)S(1)}, u32[]{:S(2)}) copy-start(bf16[224,896]{1,0:T(8,128)(2,1)S(1)} %collective-permute-done.3.refs_5_) | copy-start | bytes 1204228
  40.3 0.8 copy-start.19
  46.5 3.2 %collective-permute-start.6 = (bf16[4,512,256]{2,1,0:T(8,128)(2,1)S(1)}, bf16[4,512,256]{2,1,0:T(8,128)(2,1)S(1)}, u32[]{:S(2)}, u32[]{:S(2)}) collective-permute-start(bf16[4,512,256]{2,1,0:T(8,128)(2,1)S(1)} %get-tuple-element.29), channel_id=1, source_target_pairs={{0,8},{8,0},{1,9},{9,1},{2,10},{10,2},{3,11},{11,3},{4,12},{12,4},... | collective-permute-start | bytes 3145736 | tf_op jit(solution)/shard_map/ppermute | solution.py:179
  46.6 11.9 %collective-permute-start.7 = (bf16[112,896]{1,0:T(8,128)(2,1)S(1)}, bf16[112,896]{1,0:T(8,128)(2,1)S(1)}, u32[]{:S(2)}, u32[]{:S(2)}) collective-permute-start(bf16[112,896]{1,0:T(8,128)(2,1)S(1)} %copy-done.14), channel_id=1, source_target_pairs={{0,64},{64,128},{128,192},{192,0},{1,65},{65,129},{129,193},{193,1... | collective-permute-start | bytes 602120 | tf_op jit(solution)/shard_map/ppermute | solution.py:395
  47.6 10.9 %collective-permute-start.10 = (bf16[112,896]{1,0:T(8,128)(2,1)S(1)}, bf16[112,896]{1,0:T(8,128)(2,1)S(1)}, u32[]{:S(2)}, u32[]{:S(2)}) collective-permute-start(bf16[112,896]{1,0:T(8,128)(2,1)S(1)} %copy-done.13), channel_id=1, source_target_pairs={{0,192},{64,0},{128,64},{192,128},{1,193},{65,1},{129,65},{193,129... | collective-permute-start | bytes 602120 | tf_op jit(solution)/shard_map/ppermute | solution.py:396
  51.0 23.9 %all-to-all-start.1 = ((bf16[4,512,256]{2,1,0:T(8,128)(2,1)}), bf16[4,512,256]{2,1,0:T(8,128)(2,1)S(1)}, u32[]{:S(2)}, u32[]{:S(2)}) async-start(bf16[4,512,256]{2,1,0:T(8,128)(2,1)} %shard_map.124), calls=%async_computation.1 | async-start | bytes 2097152 | tf_op jit(solution)/shard_map/all_to_all | solution.py:181
  55.4 9.0 %collective-permute-start.8 = (bf16[112,896]{1,0:T(8,128)(2,1)S(1)}, bf16[112,896]{1,0:T(8,128)(2,1)S(1)}, u32[]{:S(2)}, u32[]{:S(2)}) collective-permute-start(bf16[112,896]{1,0:T(8,128)(2,1)S(1)} %copy-done.13), channel_id=1, source_target_pairs={{0,64},{64,128},{128,192},{192,0},{1,65},{65,129},{129,193},{193,1... | collective-permute-start | bytes 602120 | tf_op jit(solution)/shard_map/ppermute | solution.py:395
  55.8 8.6 %collective-permute-start.9 = (bf16[112,896]{1,0:T(8,128)(2,1)S(1)}, bf16[112,896]{1,0:T(8,128)(2,1)S(1)}, u32[]{:S(2)}, u32[]{:S(2)}) collective-permute-start(bf16[112,896]{1,0:T(8,128)(2,1)S(1)} %copy-done.14), channel_id=1, source_target_pairs={{0,192},{64,0},{128,64},{192,128},{1,193},{65,1},{129,65},{193,129... | collective-permute-start | bytes 602120 | tf_op jit(solution)/shard_map/ppermute | solution.py:396
  58.5 9.0 %copy-start.20 = (bf16[112,896]{1,0:T(8,128)(2,1)}, bf16[112,896]{1,0:T(8,128)(2,1)S(1)}, u32[]{:S(2)}) copy-start(bf16[112,896]{1,0:T(8,128)(2,1)S(1)} %collective-permute-done.7.refs_3_) | copy-start | bytes 602116
  58.5 9.0 %collective-permute-start.11 = (bf16[112,896]{1,0:T(8,128)(2,1)S(1)}, bf16[112,896]{1,0:T(8,128)(2,1)S(1)}, u32[]{:S(2)}, u32[]{:S(2)}) collective-permute-start(bf16[112,896]{1,0:T(8,128)(2,1)S(1)} %collective-permute-done.7.refs_3_), channel_id=1, source_target_pairs={{0,64},{64,128},{128,192},{192,0},{1,65},{65,129},{129,193},{193,1... | collective-permute-start | bytes 602120 | tf_op jit(solution)/shard_map/ppermute | solution.py:409
  58.5 9.0 %copy-start.21 = (bf16[112,896]{1,0:T(8,128)(2,1)}, bf16[112,896]{1,0:T(8,128)(2,1)S(1)}, u32[]{:S(2)}) copy-start(bf16[112,896]{1,0:T(8,128)(2,1)S(1)} %collective-permute-done.10.refs_6_) | copy-start | bytes 602116
  58.6 9.0 %collective-permute-start.12 = (bf16[112,896]{1,0:T(8,128)(2,1)S(1)}, bf16[112,896]{1,0:T(8,128)(2,1)S(1)}, u32[]{:S(2)}, u32[]{:S(2)}) collective-permute-start(bf16[112,896]{1,0:T(8,128)(2,1)S(1)} %collective-permute-done.10.refs_6_), channel_id=1, source_target_pairs={{0,192},{64,0},{128,64},{192,128},{1,193},{65,1},{129,65},{193,129... | collective-permute-start | bytes 602120 | tf_op jit(solution)/shard_map/ppermute | solution.py:410
  64.4 3.2 %copy-start.22 = (bf16[112,896]{1,0:T(8,128)(2,1)}, bf16[112,896]{1,0:T(8,128)(2,1)S(1)}, u32[]{:S(2)}) copy-start(bf16[112,896]{1,0:T(8,128)(2,1)S(1)} %collective-permute-done.8.refs_4_) | copy-start | bytes 602116
  64.4 3.2 %copy-start.23 = (bf16[112,896]{1,0:T(8,128)(2,1)}, bf16[112,896]{1,0:T(8,128)(2,1)S(1)}, u32[]{:S(2)}) copy-start(bf16[112,896]{1,0:T(8,128)(2,1)S(1)} %collective-permute-done.9.refs_5_) | copy-start | bytes 602116
  71.9 2.0 collective-permute-start.13
  73.9 5.5 %copy-start.1 = (bf16[896,224]{0,1:T(8,128)(2,1)S(1)}, bf16[896,224]{0,1:T(8,128)(2,1)}, u32[]{:S(2)}) copy-start(bf16[896,224]{0,1:T(8,128)(2,1)} %param.16) | copy-start | bytes 1204228
  73.9 8.5 %copy-start.2 = (f32[3,896]{1,0:T(4,128)S(1)}, f32[3,896]{1,0:T(4,128)}, u32[]{:S(2)}) copy-start(f32[3,896]{1,0:T(4,128)} %bias_ref.3) | copy-start | bytes 32260
  74.9 28.0 %all-to-all-start.2 = ((bf16[4,560,128]{2,1,0:T(8,128)(2,1)}), bf16[4,560,128]{2,1,0:T(8,128)(2,1)S(1)}, u32[]{:S(2)}, u32[]{:S(2)}) async-start(bf16[4,560,128]{2,1,0:T(8,128)(2,1)} %shard_map.127), calls=%async_computation.2 | async-start | bytes 1146880 | tf_op jit(solution)/shard_map/all_to_all | solution.py:181
  79.4 46.4 %collective-permute-start.25 = (bf16[224,896]{1,0:T(8,128)(2,1)S(1)}, bf16[224,896]{1,0:T(8,128)(2,1)}, u32[]{:S(2)}, u32[]{:S(2)}) collective-permute-start(bf16[224,896]{1,0:T(8,128)(2,1)S(1)} %bitcast.22), channel_id=1, source_target_pairs={{0,64},{64,128},{128,192},{192,0},{1,65},{65,129},{129,193},{193,1... | collective-permute-start | bytes 1204232 | tf_op jit(solution)/shard_map/ppermute | solution.py:443
  81.6 45.9 %collective-permute-start.26 = (bf16[224,896]{1,0:T(8,128)(2,1)S(1)}, bf16[224,896]{1,0:T(8,128)(2,1)}, u32[]{:S(2)}, u32[]{:S(2)}) collective-permute-start(bf16[224,896]{1,0:T(8,128)(2,1)S(1)} %bitcast.23), channel_id=1, source_target_pairs={{0,192},{64,0},{128,64},{192,128},{1,193},{65,1},{129,65},{193,129... | collective-permute-start | bytes 1204232 | tf_op jit(solution)/shard_map/ppermute | solution.py:444
  83.3 29.4 %copy-start.8 = (s32[2]{0:T(128)S(1)}, s32[2]{0:T(128)}, u32[]{:S(2)}) copy-start(s32[2]{0:T(128)} %offset_ref.1) | copy-start | bytes 28
  83.3 33.3 %copy-start.9 = (s32[2]{0:T(128)S(1)}, s32[2]{0:T(128)}, u32[]{:S(2)}) copy-start(s32[2]{0:T(128)} %len_ref.1) | copy-start | bytes 28
  83.3 28.7 %collective-permute-start.14 = (bf16[512,256]{1,0:T(8,128)(2,1)}, bf16[512,256]{1,0:T(8,128)(2,1)S(1)}, u32[]{:S(2)}, u32[]{:S(2)}) collective-permute-start(bf16[512,256]{1,0:T(8,128)(2,1)} %shard_map.125.own_ref), channel_id=1, source_target_pairs={{0,64},{128,192},{1,65},{129,193},{2,66},{130,194},{3,67},{131,195... | collective-permute-start | bytes 786440 | tf_op jit(solution)/shard_map/ppermute | solution.py:434
  84.8 27.2 %copy-start.4 = (bf16[8,2,16,128]{3,2,1,0:T(8,128)(2,1)}, bf16[8,2,16,128]{3,2,1,0:T(8,128)(2,1)S(1)}, u32[]{:S(2)}) copy-start(bf16[8,2,16,128]{3,2,1,0:T(8,128)(2,1)S(1)} %get-tuple-element.36.refs_0_) | copy-start | bytes 196612
  84.8 13.8 %collective-permute-start.15 = (bf16[8,2,16,128]{3,2,1,0:T(8,128)(2,1)S(1)}, bf16[8,2,16,128]{3,2,1,0:T(8,128)(2,1)S(1)}, u32[]{:S(2)}, u32[]{:S(2)}) collective-permute-start(bf16[8,2,16,128]{3,2,1,0:T(8,128)(2,1)S(1)} %get-tuple-element.37), channel_id=1, source_target_pairs={{0,64},{64,128},{128,192},{192,0},{1,65},{65,129},{129,193},{193,1... | collective-permute-start | bytes 196616 | tf_op jit(solution)/shard_map/ppermute | solution.py:424
  89.7 13.0 %collective-permute-start.16 = (bf16[8,2,16,128]{3,2,1,0:T(8,128)(2,1)S(1)}, bf16[8,2,16,128]{3,2,1,0:T(8,128)(2,1)S(1)}, u32[]{:S(2)}, u32[]{:S(2)}) collective-permute-start(bf16[8,2,16,128]{3,2,1,0:T(8,128)(2,1)S(1)} %get-tuple-element.38), channel_id=1, source_target_pairs={{0,192},{64,0},{128,64},{192,128},{1,193},{65,1},{129,65},{193,129... | collective-permute-start | bytes 196616 | tf_op jit(solution)/shard_map/ppermute | solution.py:425
  98.7 13.4 %copy-start.26 = (bf16[8,2,16,128]{3,2,1,0:T(8,128)(2,1)}, bf16[8,2,16,128]{3,2,1,0:T(8,128)(2,1)S(1)}, u32[]{:S(2)}) copy-start(bf16[8,2,16,128]{3,2,1,0:T(8,128)(2,1)S(1)} %collective-permute-done.15.refs_1_) | copy-start | bytes 196612
  98.7 33.7 %collective-permute-start.27 = (bf16[224,896]{1,0:T(8,128)(2,1)S(1)}, bf16[224,896]{1,0:T(8,128)(2,1)S(1)}, u32[]{:S(2)}, u32[]{:S(2)}) collective-permute-start(bf16[224,896]{1,0:T(8,128)(2,1)S(1)} %bitcast.24), channel_id=1, source_target_pairs={{0,128},{64,192},{128,0},{192,64},{1,129},{65,193},{129,1},{193,65... | collective-permute-start | bytes 1204232 | tf_op jit(solution)/shard_map/ppermute | solution.py:445
  102.7 9.4 %copy-start.27 = (bf16[8,2,16,128]{3,2,1,0:T(8,128)(2,1)}, bf16[8,2,16,128]{3,2,1,0:T(8,128)(2,1)S(1)}, u32[]{:S(2)}) copy-start(bf16[8,2,16,128]{3,2,1,0:T(8,128)(2,1)S(1)} %collective-permute-done.16.refs_2_) | copy-start | bytes 196612
  102.7 9.3 %collective-permute-start.17 = (bf16[8,2,16,128]{3,2,1,0:T(8,128)(2,1)S(1)}, bf16[8,2,16,128]{3,2,1,0:T(8,128)(2,1)S(1)}, u32[]{:S(2)}, u32[]{:S(2)}) collective-permute-start(bf16[8,2,16,128]{3,2,1,0:T(8,128)(2,1)S(1)} %get-tuple-element.39), channel_id=1, source_target_pairs={{0,128},{64,192},{128,0},{192,64},{1,129},{65,193},{129,1},{193,65... | collective-permute-start | bytes 196616 | tf_op jit(solution)/shard_map/ppermute | solution.py:426
  122.5 7.7 %collective-permute-start.18 = (bf16[528,128]{1,0:T(8,128)(2,1)S(1)}, bf16[528,128]{1,0:T(8,128)(2,1)S(1)}, u32[]{:S(2)}, u32[]{:S(2)}) collective-permute-start(bf16[528,128]{1,0:T(8,128)(2,1)S(1)} %shard_map.131.refs_0_), channel_id=1, source_target_pairs={{0,16},{16,32},{32,48},{48,0},{1,17},{17,33},{33,49},{49,1},{2,18}... | collective-permute-start | bytes 405512 | tf_op jit(solution)/shard_map/ppermute | solution.py:467
  124.0 6.1 %collective-permute-start.19 = (bf16[528,128]{1,0:T(8,128)(2,1)S(1)}, bf16[528,128]{1,0:T(8,128)(2,1)S(1)}, u32[]{:S(2)}, u32[]{:S(2)}) collective-permute-start(bf16[528,128]{1,0:T(8,128)(2,1)S(1)} %shard_map.131.refs_0_), channel_id=1, source_target_pairs={{0,48},{16,0},{32,16},{48,32},{1,49},{17,1},{33,17},{49,33},{2,50}... | collective-permute-start | bytes 405512 | tf_op jit(solution)/shard_map/ppermute | solution.py:467
  125.8 6.5 %collective-permute-start.20 = (bf16[528,128]{1,0:T(8,128)(2,1)S(1)}, bf16[528,128]{1,0:T(8,128)(2,1)S(1)}, u32[]{:S(2)}, u32[]{:S(2)}) collective-permute-start(bf16[528,128]{1,0:T(8,128)(2,1)S(1)} %shard_map.131.refs_0_), channel_id=1, source_target_pairs={{0,32},{16,48},{32,0},{48,16},{1,33},{17,49},{33,1},{49,17},{2,34}... | collective-permute-start | bytes 405512 | tf_op jit(solution)/shard_map/ppermute | solution.py:467
  127.6 4.8 %collective-permute-start.21 = (bf16[528,128]{1,0:T(8,128)(2,1)S(1)}, bf16[528,128]{1,0:T(8,128)(2,1)S(1)}, u32[]{:S(2)}, u32[]{:S(2)}) collective-permute-start(bf16[528,128]{1,0:T(8,128)(2,1)S(1)} %shard_map.131.refs_0_), channel_id=1, source_target_pairs={{0,8},{8,0},{1,9},{9,1},{2,10},{10,2},{3,11},{11,3},{4,12},{12,4},... | collective-permute-start | bytes 405512 | tf_op jit(solution)/shard_map/ppermute | solution.py:468
  130.2 2.2 %collective-permute-start.22 = (bf16[528,128]{1,0:T(8,128)(2,1)S(1)}, bf16[528,128]{1,0:T(8,128)(2,1)S(1)}, u32[]{:S(2)}, u32[]{:S(2)}) collective-permute-start(bf16[528,128]{1,0:T(8,128)(2,1)S(1)} %collective-permute-done.18.refs_1_), channel_id=1, source_target_pairs={{0,8},{8,0},{1,9},{9,1},{2,10},{10,2},{3,11},{11,3},{4,12},{12,4},... | collective-permute-start | bytes 405512 | tf_op jit(solution)/shard_map/ppermute | solution.py:468
  130.2 2.2 %collective-permute-start.23 = (bf16[528,128]{1,0:T(8,128)(2,1)S(1)}, bf16[528,128]{1,0:T(8,128)(2,1)S(1)}, u32[]{:S(2)}, u32[]{:S(2)}) collective-permute-start(bf16[528,128]{1,0:T(8,128)(2,1)S(1)} %collective-permute-done.19.refs_2_), channel_id=1, source_target_pairs={{0,8},{8,0},{1,9},{9,1},{2,10},{10,2},{3,11},{11,3},{4,12},{12,4},... | collective-permute-start | bytes 405512 | tf_op jit(solution)/shard_map/ppermute | solution.py:468
  132.3 1.4 collective-permute-start.24
  137.3 36.6 %copy-start.7 = (f32[7168]{0:T(1024)S(1)}, f32[7168]{0:T(1024)}, u32[]{:S(2)}) copy-start(f32[7168]{0:T(1024)} %param.17) | copy-start | bytes 86020
  137.3 36.6 %all-to-all-start.3 = ((bf16[64,8,896]{2,1,0:T(8,128)(2,1)}), bf16[64,8,896]{2,1,0:T(8,128)(2,1)S(1)}, u32[]{:S(2)}, u32[]{:S(2)}) async-start(bf16[64,8,896]{2,1,0:T(8,128)(2,1)} %bitcast.8), calls=%async_computation.3 | async-start | bytes 1835008 | tf_op jit(solution)/shard_map/all_to_all | solution.py:483
  174.1 7.5 %collective-permute-start.28 = (bf16[8,7168]{1,0:T(8,128)(2,1)S(1)}, bf16[8,7168]{1,0:T(8,128)(2,1)S(1)}, u32[]{:S(2)}, u32[]{:S(2)}) collective-permute-start(bf16[8,7168]{1,0:T(8,128)(2,1)S(1)} %shard_map.133.refs_0_), channel_id=1, source_target_pairs={{0,1},{1,2},{2,3},{3,4},{4,5},{5,6},{6,7},{7,0},{8,9},{9,10},{10,1... | collective-permute-start | bytes 344072 | tf_op jit(solution)/shard_map/ppermute | solution.py:499
  175.8 6.3 %collective-permute-start.29 = (bf16[8,7168]{1,0:T(8,128)(2,1)S(1)}, bf16[8,7168]{1,0:T(8,128)(2,1)S(1)}, u32[]{:S(2)}, u32[]{:S(2)}) collective-permute-start(bf16[8,7168]{1,0:T(8,128)(2,1)S(1)} %shard_map.133.refs_0_), channel_id=1, source_target_pairs={{0,7},{1,0},{2,1},{3,2},{4,3},{5,4},{6,5},{7,6},{8,15},{9,8},{10,9... | collective-permute-start | bytes 344072 | tf_op jit(solution)/shard_map/ppermute | solution.py:502
  177.4 14.2 %all-to-all-start.4 = ((bf16[8,64,256]{2,1,0:T(8,128)(2,1)}), bf16[8,64,256]{2,1,0:T(8,128)(2,1)S(1)}, u32[]{:S(2)}, u32[]{:S(2)}) async-start(bf16[8,64,256]{2,1,0:T(8,128)(2,1)} %bitcast.11), calls=%async_computation.4 | async-start | bytes 524288 | tf_op jit(solution)/shard_map/all_to_all | solution.py:493
  181.6 6.8 %collective-permute-start.30 = (bf16[8,7168]{1,0:T(8,128)(2,1)S(1)}, bf16[8,7168]{1,0:T(8,128)(2,1)S(1)}, u32[]{:S(2)}, u32[]{:S(2)}) collective-permute-start(bf16[8,7168]{1,0:T(8,128)(2,1)S(1)} %collective-permute-done.28.refs_1_), channel_id=1, source_target_pairs={{0,1},{1,2},{2,3},{3,4},{4,5},{5,6},{6,7},{7,0},{8,9},{9,10},{10,1... | collective-permute-start | bytes 344072 | tf_op jit(solution)/shard_map/ppermute | solution.py:499
  182.1 6.3 %collective-permute-start.31 = (bf16[8,7168]{1,0:T(8,128)(2,1)S(1)}, bf16[8,7168]{1,0:T(8,128)(2,1)S(1)}, u32[]{:S(2)}, u32[]{:S(2)}) collective-permute-start(bf16[8,7168]{1,0:T(8,128)(2,1)S(1)} %collective-permute-done.29.refs_2_), channel_id=1, source_target_pairs={{0,7},{1,0},{2,1},{3,2},{4,3},{5,4},{6,5},{7,6},{8,15},{9,8},{10,9... | collective-permute-start | bytes 344072 | tf_op jit(solution)/shard_map/ppermute | solution.py:502
  188.4 6.0 %collective-permute-start.32 = (bf16[8,7168]{1,0:T(8,128)(2,1)S(1)}, bf16[8,7168]{1,0:T(8,128)(2,1)S(1)}, u32[]{:S(2)}, u32[]{:S(2)}) collective-permute-start(bf16[8,7168]{1,0:T(8,128)(2,1)S(1)} %collective-permute-done.30.refs_3_), channel_id=1, source_target_pairs={{0,1},{1,2},{2,3},{3,4},{4,5},{5,6},{6,7},{7,0},{8,9},{9,10},{10,1... | collective-permute-start | bytes 344072 | tf_op jit(solution)/shard_map/ppermute | solution.py:499
  188.4 6.8 %collective-permute-start.33 = (bf16[8,7168]{1,0:T(8,128)(2,1)S(1)}, bf16[8,7168]{1,0:T(8,128)(2,1)S(1)}, u32[]{:S(2)}, u32[]{:S(2)}) collective-permute-start(bf16[8,7168]{1,0:T(8,128)(2,1)S(1)} %collective-permute-done.31.refs_4_), channel_id=1, source_target_pairs={{0,7},{1,0},{2,1},{3,2},{4,3},{5,4},{6,5},{7,6},{8,15},{9,8},{10,9... | collective-permute-start | bytes 344072 | tf_op jit(solution)/shard_map/ppermute | solution.py:502
  194.4 6.0 %collective-permute-start.34 = (bf16[8,7168]{1,0:T(8,128)(2,1)S(1)}, bf16[8,7168]{1,0:T(8,128)(2,1)S(1)}, u32[]{:S(2)}, u32[]{:S(2)}) collective-permute-start(bf16[8,7168]{1,0:T(8,128)(2,1)S(1)} %collective-permute-done.32.refs_5_), channel_id=1, source_target_pairs={{0,1},{1,2},{2,3},{3,4},{4,5},{5,6},{6,7},{7,0},{8,9},{9,10},{10,1... | collective-permute-start | bytes 344072 | tf_op jit(solution)/shard_map/ppermute | solution.py:499
  (5 other events, 3.6 us)
